TPU v7x, 256 devices: a whole 4x4x8 slice. The times are simulated.
256 devices in a mesh: row: 8 (over x, core), rhs: 32 (over y, z).
Axes of the slice: x: 4, y: 4, z: 8, core: 2. Of those that a mesh axis runs over, the one named last changes fastest.
Arguments:
- local_rhs: bfloat16 [336, 128, 4096], P('row', None, 'rhs'), may hold values from -6 to 6
- top_rhs: bfloat16 [8, 128, 4096], P('row', None, 'rhs'), may hold values from -6 to 6
- diag_inv: bfloat16 [336, 128, 128], P('row', 'rhs'), as said below
- top_inv: bfloat16 [8, 128, 128], P('row', 'rhs'), as said below
- off_blocks: bfloat16 [336, 4, 128, 128], P('row', None, 'rhs'), may hold values from -0.125 to 0.125
- top_factor: bfloat16 [8, 8, 128, 128], P('row', None, 'rhs'), may hold values from -0.1875 to 0.1875
- targets: int32 [336, 4], P('row'), may hold values from 24 to 49, as said below
Outputs:
- local_solution: bfloat16 [336, 128, 4096], P('row', None, 'rhs')
- top_solution: bfloat16 [8, 128, 4096], P('row', None, 'rhs')
Inputs may be any that keep to these rules, and one draw needn't show every extreme that they name: `diag_inv`: each block is lower triangular. `top_inv`: each block is lower triangular. `targets`: row r * 42 + k holds 4 distinct codes; a code c < 42 names local supernode r * 42 + c, of a higher level than k; a code c >= 42 names top block c - 42.
All inputs are finite; a program needn't handle non-finite values.
Results may differ from a plain program's by a relative error of at most 0.023.
Values may be sent and summed in bfloat16 or wider, within the bound.
No kernel may reach another device: no remote copies, remote signals or barrier semaphores. Data moves between devices by JAX's collectives and lax.ppermute only.
A program may use at most 64 MiB of HBM per device.

v0:
```python
import jax
import jax.numpy as jnp
from jax import lax
from jax.sharding import PartitionSpec as P

LEAF = 24


def spread(shard, axis, root):
    mine = lax.axis_index(axis) == root
    return lax.psum(jnp.where(mine, shard, jnp.zeros_like(shard)), axis)


def local(local_rhs, top_rhs, diag_inv, top_inv, off_blocks, top_factor, targets):
    sub_count = local_rhs.shape[0]
    panel_width = local_rhs.shape[1]
    columns = local_rhs.shape[2]
    top_count = lax.axis_size("row")
    cand_count = sub_count + top_count
    acc_local = jnp.zeros((sub_count, panel_width, columns), jnp.float32)
    acc_top = jnp.zeros((top_count, panel_width, columns), jnp.float32)
    level_ranges = ((0, LEAF), (LEAF, LEAF + LEAF // 2), (LEAF + LEAF // 2, sub_count))
    solved = []
    for first_row, end_row in level_ranges:
        residual_rows = (
            local_rhs[first_row:end_row].astype(jnp.float32) - acc_local[first_row:end_row]
        ).astype(jnp.bfloat16)

        def apply_inverse(slice_part, offset, residual_rows=residual_rows):
            return jnp.einsum(
                "jxm,jme->jxe", slice_part, residual_rows, preferred_element_type=jnp.float32
            )

        level_partial = apply_inverse(
            lax.all_gather(diag_inv[first_row:end_row], "rhs", axis=1, tiled=True), jnp.int32(0)
        ).astype(jnp.bfloat16)
        solved.append(level_partial)
        target_codes = targets[first_row:end_row].reshape(-1)
        later_count = cand_count - end_row
        selector = (
            jnp.arange(later_count, dtype=jnp.int32)[:, None] == target_codes[None, :] - end_row
        ).astype(jnp.float32)

        def spread_updates(slice_part, offset, level_partial=level_partial, selector=selector):
            products = jnp.einsum(
                "yiko,yoq->yikq", slice_part, level_partial, preferred_element_type=jnp.float32
            )
            flattened = products.reshape(selector.shape[1], slice_part.shape[2], columns)
            return jnp.einsum("cn,nar->car", selector, flattened, precision=lax.Precision.HIGHEST)

        contrib = spread_updates(
            lax.all_gather(off_blocks[first_row:end_row], "rhs", axis=2, tiled=True), jnp.int32(0)
        )
        acc_local = acc_local.at[end_row:].add(contrib[: sub_count - end_row])
        acc_top = acc_top + contrib[sub_count - end_row :]
    inverse_rows = top_inv.reshape(1, 1, top_inv.shape[1], panel_width)
    top_full, inv_full = (
        lax.all_gather(top_factor, "rhs", axis=2, tiled=True),
        lax.all_gather(inverse_rows, "rhs", axis=2, tiled=True),
    )
    position = lax.axis_index("row")
    own_sum = lax.psum_scatter(
        acc_top.astype(jnp.bfloat16), "row", scatter_dimension=0, tiled=True
    ).astype(jnp.float32)
    base_value = top_rhs[0].astype(jnp.float32) - own_sum[0]

    def top_step(step_index, carry):
        carried, own_solution = carry
        residual_rows = (base_value - carried).astype(jnp.bfloat16)
        candidate = jnp.dot(
            inv_full[0, 0], residual_rows, preferred_element_type=jnp.float32
        ).astype(jnp.bfloat16)
        solution = spread(candidate, "row", step_index)
        own_solution = jnp.where(position == step_index, solution, own_solution)
        coupling_matrix = lax.dynamic_index_in_dim(top_full[0], step_index, 0, keepdims=False)
        update = jnp.dot(coupling_matrix, solution, preferred_element_type=jnp.float32)
        carried = carried + jnp.where(step_index < position, update, 0.0)
        return (carried, own_solution)

    initial_state = (
        jnp.zeros((panel_width, columns), jnp.float32),
        jnp.zeros((panel_width, columns), jnp.bfloat16),
    )
    own_separator = lax.fori_loop(0, top_count, top_step, initial_state)[1][None]
    return (jnp.concatenate(solved, axis=0), own_separator)


def solution(mesh):
    in_specs = (
        P("row", None, "rhs"),
        P("row", None, "rhs"),
        P("row", "rhs", None),
        P("row", "rhs", None),
        P("row", None, "rhs", None),
        P("row", None, "rhs", None),
        P("row", None),
    )
    out_specs = (P("row", None, "rhs"), P("row", None, "rhs"))
    return jax.shard_map(local, mesh=mesh, in_specs=in_specs, out_specs=out_specs, check_vma=False)
```

profile of v0, /device:TPU:1, one launch (start us, length us, event | category | flops | bytes accessed | tf_op | source)
XLA Modules:
  0.0 550.9 jit_solution(5138594552302585885)
XLA Ops:
  7.3 0.9 slice.103
  8.2 0.7 copy.121
  8.9 0.0 all-gather.6.cloned.1.call-start
  8.9 0.9 slice.109
  9.9 0.6 copy.124
  10.6 0.8 slice.99
  11.4 0.1 copy.78
  11.4 0.1 sub.37
  11.6 0.1 slice_add_fusion.3
  11.6 0.1 copy.88
  11.7 0.1 sub.40
  11.9 0.1 slice_add_fusion.2
  12.0 0.1 copy.98
  12.0 0.1 sub.43
  12.1 46.1 %all_gather.28 = bf16[6,128,128]{2,0,1:T(8,128)(2,1)} all-gather(bf16[6,4,128]{2,0,1:T(8,128)(2,1)S(1)} %copy.125), channel_id=1, replica_groups=mesh['row'=8,'rhs'=32] {'rhs'}, dimensions={1}, use_global_device_ids=true | all-gather | bytes 202752 | tf_op jit(solution)/shard_map/all_gather | solution.py:35
  58.2 39.4 %all_gather.26 = bf16[12,128,128]{2,0,1:T(8,128)(2,1)S(1)} all-gather(bf16[12,4,128]{2,0,1:T(8,128)(2,1)S(1)} %copy.122), channel_id=1, replica_groups=mesh['row'=8,'rhs'=32] {'rhs'}, dimensions={1}, use_global_device_ids=true | all-gather | bytes 405504 | tf_op jit(solution)/shard_map/all_gather | solution.py:35
  97.6 36.8 %all_gather.24 = bf16[24,128,128]{2,0,1:T(8,128)(2,1)S(1)} all-gather(bf16[24,4,128]{2,0,1:T(8,128)(2,1)S(1)} %copy.119), channel_id=1, replica_groups=mesh['row'=8,'rhs'=32] {'rhs'}, dimensions={1}, use_global_device_ids=true | all-gather | bytes 811008 | tf_op jit(solution)/shard_map/all_gather | solution.py:35
  134.3 43.1 %all_gather.30 = bf16[6,4,128,128]{3,1,0,2:T(4,128)(2,1)} all-gather(bf16[6,4,4,128]{3,1,0,2:T(4,128)(2,1)S(1)} %copy.126), channel_id=1, replica_groups=mesh['row'=8,'rhs'=32] {'rhs'}, dimensions={2}, use_global_device_ids=true | all-gather | bytes 811008 | tf_op jit(solution)/shard_map/all_gather | solution.py:52
  177.4 0.4 convolution_convert_fusion.1
  177.8 7.2 %fusion.10 = f32[24,128,4,128]{3,1,2,0:T(8,128)} fusion(bf16[24,4,128,128]{3,0,1,2:T(8,128)(2,1)} %all-gather.4.cloned.1.call-done, bf16[24,128,128]{2,1,0:T(8,128)(2,1)S(1)} %convolution_convert_fusion.1), kind=kOutput, calls=%fused_computation.14 | convolution fusion | flops 402653184 | bytes 10223616 | tf_op jit(solution)/shard_map/yiko,yoq->yikq/dot_general | solution.py:45
  185.1 6.7 %copy.82 = f32[96,128,128]{2,0,1:T(8,128)} copy(f32[96,128,128]{1,2,0:T(8,128)} %bitcast.61) | data formatting | bytes 12582912 | tf_op jit(solution)/shard_map/reshape | solution.py:48
  191.8 4.5 fusion.30
  196.3 1.4 copy-done
  197.7 0.3 fusion.15
  198.0 0.3 convolution_convert_fusion.2
  198.3 3.8 fusion.12
  202.1 2.6 copy.92
  204.7 1.2 fusion.34
  206.0 1.9 fusion.22
  207.8 0.2 convolution_convert_fusion.3
  208.1 1.6 fusion.17
  209.7 2.0 copy.102
  211.8 2.0 fusion.14
  213.8 0.8 copy.103
  214.6 34.8 %all_gather.29 = bf16[1,8,128,128]{3,1,0,2:T(8,128)(2,1)S(1)} all-gather(bf16[1,8,4,128]{3,1,0,2:T(8,128)(2,1)S(1)} %copy.97), channel_id=1, replica_groups=mesh['row'=8,'rhs'=32] {'rhs'}, dimensions={2}, use_global_device_ids=true | all-gather | bytes 270336 | tf_op jit(solution)/shard_map/all_gather | solution.py:58
  249.4 35.9 %all-gather = bf16[1,128,128]{2,0,1:T(2,128)(2,1)S(1)} all-gather(bf16[1,4,128]{2,0,1:T(2,128)(2,1)S(1)} %copy.104), channel_id=2, replica_groups=mesh['row'=8,'rhs'=32] {'rhs'}, dimensions={1}, use_global_device_ids=true | all-gather | bytes 33792 | tf_op jit(solution)/shard_map/all_gather | solution.py:59
  285.3 2.3 pad_maximum_fusion
  287.7 0.8 subtract_bitcast_fusion
  288.5 255.2 %while.18 = (s32[]{:T(128)}, f32[128,128]{1,0:T(8,128)S(1)}, bf16[128,128]{0,1:T(8,128)(2,1)S(1)}, s32[]{:T(128)}, bf16[1,8,128,128]{3,2,1,0:T(8,128)(2,1)S(1)},...) while((s32[]{:T(128)}, f32[128,128]{1,0:T(8,128)S(1)}, ...), condition=%wide.region_3.4_spmd.clone, body=%wide.region_1.3_spmd.clone.sunk | while | flops 8568841 | bytes 557243 | solution.py:84
  288.5 0.2 fusion.52
  288.7 86.7 %psum.13 = bf16[128,128]{0,1:T(8,128)(2,1)S(1)} all-reduce(bf16[128,128]{0,1:T(8,128)(2,1)S(1)} %fusion.52), channel_id=1, replica_groups=mesh['row'=8,'rhs'=32] {'row'}, use_global_device_ids=true, to_apply=%region_2.2 | all-reduce | flops 16384 | bytes 65536 | tf_op jit(solution)/shard_map/while/body/eval_jaxpr/psum | solution.py:11
  375.3 0.2 fusion.53
  375.6 0.2 fusion.52
  375.7 23.6 %psum.13 = bf16[128,128]{0,1:T(8,128)(2,1)S(1)} all-reduce(bf16[128,128]{0,1:T(8,128)(2,1)S(1)} %fusion.52), channel_id=1, replica_groups=mesh['row'=8,'rhs'=32] {'row'}, use_global_device_ids=true, to_apply=%region_2.2 | all-reduce | flops 16384 | bytes 65536 | tf_op jit(solution)/shard_map/while/body/eval_jaxpr/psum | solution.py:11
  399.4 0.2 fusion.53
  399.6 0.2 fusion.52
  399.8 23.6 %psum.13 = bf16[128,128]{0,1:T(8,128)(2,1)S(1)} all-reduce(bf16[128,128]{0,1:T(8,128)(2,1)S(1)} %fusion.52), channel_id=1, replica_groups=mesh['row'=8,'rhs'=32] {'row'}, use_global_device_ids=true, to_apply=%region_2.2 | all-reduce | flops 16384 | bytes 65536 | tf_op jit(solution)/shard_map/while/body/eval_jaxpr/psum | solution.py:11
  423.4 0.2 fusion.53
  423.6 0.2 fusion.52
  423.8 23.6 %psum.13 = bf16[128,128]{0,1:T(8,128)(2,1)S(1)} all-reduce(bf16[128,128]{0,1:T(8,128)(2,1)S(1)} %fusion.52), channel_id=1, replica_groups=mesh['row'=8,'rhs'=32] {'row'}, use_global_device_ids=true, to_apply=%region_2.2 | all-reduce | flops 16384 | bytes 65536 | tf_op jit(solution)/shard_map/while/body/eval_jaxpr/psum | solution.py:11
  447.4 0.2 fusion.53
  447.6 0.2 fusion.52
  447.8 23.6 %psum.13 = bf16[128,128]{0,1:T(8,128)(2,1)S(1)} all-reduce(bf16[128,128]{0,1:T(8,128)(2,1)S(1)} %fusion.52), channel_id=1, replica_groups=mesh['row'=8,'rhs'=32] {'row'}, use_global_device_ids=true, to_apply=%region_2.2 | all-reduce | flops 16384 | bytes 65536 | tf_op jit(solution)/shard_map/while/body/eval_jaxpr/psum | solution.py:11
  471.4 0.2 fusion.53
  471.6 0.2 fusion.52
  471.8 23.6 %psum.13 = bf16[128,128]{0,1:T(8,128)(2,1)S(1)} all-reduce(bf16[128,128]{0,1:T(8,128)(2,1)S(1)} %fusion.52), channel_id=1, replica_groups=mesh['row'=8,'rhs'=32] {'row'}, use_global_device_ids=true, to_apply=%region_2.2 | all-reduce | flops 16384 | bytes 65536 | tf_op jit(solution)/shard_map/while/body/eval_jaxpr/psum | solution.py:11
  495.4 0.2 fusion.53
  495.7 0.2 fusion.52
  495.9 23.6 %psum.13 = bf16[128,128]{0,1:T(8,128)(2,1)S(1)} all-reduce(bf16[128,128]{0,1:T(8,128)(2,1)S(1)} %fusion.52), channel_id=1, replica_groups=mesh['row'=8,'rhs'=32] {'row'}, use_global_device_ids=true, to_apply=%region_2.2 | all-reduce | flops 16384 | bytes 65536 | tf_op jit(solution)/shard_map/while/body/eval_jaxpr/psum | solution.py:11
  519.5 0.2 fusion.53
  519.7 0.2 fusion.52
  519.9 23.6 %psum.13 = bf16[128,128]{0,1:T(8,128)(2,1)S(1)} all-reduce(bf16[128,128]{0,1:T(8,128)(2,1)S(1)} %fusion.52), channel_id=1, replica_groups=mesh['row'=8,'rhs'=32] {'row'}, use_global_device_ids=true, to_apply=%region_2.2 | all-reduce | flops 16384 | bytes 65536 | tf_op jit(solution)/shard_map/while/body/eval_jaxpr/psum | solution.py:11
  543.5 0.2 fusion.53
  543.7 0.7 copy.106
  (64 shorter events, 0.5 us)
Async XLA Ops:
  7.2 4.7 slice-start.2
  7.2 4.4 slice-start.3
  7.2 4.6 slice-start.4
  7.2 4.1 copy-start.11
  7.2 170.6 %all-gather.4.cloned.1.call-start = ((), (), s32[]{:S(2)}) async-start(), calls=%async_computation.1 | async-start | bytes 3244032 | tf_op jit(solution)/shard_map/all_gather | solution.py:52
  8.9 168.5 %copy-start.8 = (bf16[42,128,128]{2,1,0:T(8,128)(2,1)S(1)}, bf16[42,128,128]{2,1,0:T(8,128)(2,1)}, u32[]{:S(2)}) copy-start(bf16[42,128,128]{2,1,0:T(8,128)(2,1)} %param.13) | copy-start | bytes 4128772
  8.9 189.4 %all-gather.6.cloned.1.call-start = ((), (), s32[]{:S(2)}) async-start(), calls=%async_computation.2 | async-start | bytes 1622016 | tf_op jit(solution)/shard_map/all_gather | solution.py:52
  10.5 277.2 %reduce-scatter.2.cloned.1.call-start = ((), (), s32[]{:S(2)}) async-start(), calls=%async_computation.3 | async-start | bytes 294912 | tf_op jit(solution)/shard_map/reduce_scatter | solution.py:62
  177.8 7.3 %copy-start.1 = (bf16[24,128,128]{2,1,0:T(8,128)(2,1)}, bf16[24,128,128]{2,1,0:T(8,128)(2,1)S(1)}, u32[]{:S(2)}) copy-start(bf16[24,128,128]{2,1,0:T(8,128)(2,1)S(1)} %convolution_convert_fusion.1) | copy-start | bytes 2359300
  191.8 5.9 %slice-start = ((bf16[42,128,128]{2,1,0:T(8,128)(2,1)}), bf16[12,128,128]{2,1,0:T(8,128)(2,1)S(1)}, s32[]{:S(2)}) async-start(bf16[42,128,128]{2,1,0:T(8,128)(2,1)} %param.13), calls=%async_computation.4 | async-start | bytes 786432 | tf_op jit(solution)/shard_map/slice | solution.py:26
  196.3 1.4 copy-start
  198.3 3.8 copy-start.5
  204.7 1.2 slice-start.1
  204.7 3.1 copy-start.9
  205.9 3.7 copy-start.3
  206.0 2.1 copy-start.6
  208.1 1.6 copy-start.7
  209.7 2.1 copy-start.4
  211.7 2.9 copy-start.12
  211.7 37.7 %copy-start.13 = (bf16[1,4,128]{2,1,0:T(4,128)(2,1)S(1)}, bf16[1,4,128]{2,1,0:T(4,128)(2,1)}, u32[]{:S(2)}) copy-start(bf16[1,4,128]{2,1,0:T(4,128)(2,1)} %param.16) | copy-start | bytes 3076
  211.8 73.6 %copy-start.2 = (bf16[24,128,128]{2,1,0:T(8,128)(2,1)S(1)}, bf16[24,128,128]{2,1,0:T(8,128)(2,1)}, u32[]{:S(2)}) copy-start(bf16[24,128,128]{2,1,0:T(8,128)(2,1)} %copy-done.1) | copy-start | bytes 2359300
  214.5 73.1 %copy-start.10 = (bf16[1,128,128]{2,1,0:T(8,128)(2,1)S(1)}, bf16[1,128,128]{2,1,0:T(8,128)(2,1)}, u32[]{:S(2)}) copy-start(bf16[1,128,128]{2,1,0:T(8,128)(2,1)} %param.14) | copy-start | bytes 98308
Sparse Core Ops, SparseCore 0:
  11.2 80.6 all-gather.3
  94.5 73.3 all-gather.5
  214.7 69.0 reduce-scatter.1
where the time goes:
time: 552 us; the launch traced here: 551 us
  blocking collectives  488 us (88%)
  matrix products  23.9 us (4%)
  local copies, waits for them, and re-layouts  18.8 us (3%)
  between operations  14.2 us (3%)
  other arithmetic  5.59 us (1%)
    psum x8, blocking collectives, spread(): return lax.psum(jnp.where(mine, shard, jnp.zeros_like(shard)), axis)  252 us
    all_gather x3, blocking collectives, local(): lax.all_gather(diag_inv[first_row:end_row], 'rhs', axis=1, tiled=True)  122 us
    all_gather x1, blocking collectives, local(): lax.all_gather(off_blocks[first_row:end_row], 'rhs', axis=2, tiled=True)  43.1 us
    all_gather x1, blocking collectives, local(): lax.all_gather(inverse_rows, 'rhs', axis=2, tiled=True)  35.9 us
    all_gather x1, blocking collectives, local(): lax.all_gather(top_factor, 'rhs', axis=2, tiled=True)  34.8 us
    dot_general x3, matrix products, spread_updates(): jnp.einsum('yiko,yoq->yikq', slice_part, level_partial, preferred_element...  12.6 us
    reshape x3, local copies, waits for them, and re-layouts, spread_updates(): products.reshape(selector.shape[1], slice_part.shape[2], columns)  11.4 us
  transfers between devices with their start and end apart: 3, of which 0 were waited for; matrix products, arithmetic and copies ran while one was open for 5% of the time, Pallas kernels for 0%

commit v1 on v0

v1 whole, which is shorter than its diff:
```python
import jax
import jax.numpy as jnp
from jax import lax
from jax.experimental import pallas as pl
from jax.experimental.pallas import tpu as pltpu
from jax.sharding import PartitionSpec as P

SUB = 42
LEVELS = ((0, 24), (24, 36), (36, 42))
B = 128
NB = 4
TOP = 8
PARTS = 32
ROWS = B // PARTS
GROUP = 16
FIRST = LEVELS[0][1]
LATER = SUB - FIRST
LATER_PAD = -(-LATER // 4) * 4
LOW = tuple(k - k % 2 for k in range(TOP))
START = tuple(sum(TOP - LOW[q] for q in range(k)) for k in range(TOP))
TOP_BLOCKS = sum(TOP - low for low in LOW)
LEAD_ROWS = FIRST * (1 + NB) * ROWS
REST_ROWS = (LATER_PAD + LATER * NB + TOP_BLOCKS) * ROWS
DIAG_LATER = FIRST
DIAG_TOP = FIRST + LATER_PAD
W_BLOCKS = DIAG_TOP + TOP_BLOCKS
F32 = jnp.float32
BF16 = jnp.bfloat16


def substitute(
    codes, row, rhs, top_rhs, lead_hbm, rest_hbm, sol, part,
    lead, rest, stage, natural, weights, product, acc, base, sems,
):
    copies = (
        pltpu.make_async_copy(lead_hbm, lead, sems.at[0]),
        pltpu.make_async_copy(rest_hbm, rest, sems.at[1]),
    )
    for copy in copies:
        copy.start()
    acc[...] = jnp.zeros_like(acc)

    def collect(source, first_row, first_block, groups):
        def step(g, _):
            at = pl.multiple_of(first_row + g * GROUP, GROUP)
            rows = source[:, pl.ds(at, GROUP), :].astype(F32)
            stage[...] = rows.reshape(PARTS * GROUP, B)
            for q in range(GROUP // ROWS):
                for i in range(ROWS):
                    natural[q, pl.ds(i, PARTS, stride=ROWS), :] = stage[
                        pl.ds(q * ROWS + i, PARTS, stride=GROUP), :
                    ]
                weights[first_block + g * 4 + q] = natural[q].astype(BF16)
            return 0

        lax.fori_loop(0, groups, step, 0)

    def summed(target):
        for i in range(ROWS):
            natural[0, pl.ds(i, PARTS, stride=ROWS), :] = acc[target, pl.ds(i * PARTS, PARTS), :]
        return natural[0]

    def level(source, first, end, first_block, off_row, is_leaf):
        def step(n, _):
            s = first + n
            values = rhs[s]
            if not is_leaf:
                values = (values.astype(F32) - summed(s - FIRST)).astype(BF16)
            solved = jnp.dot(weights[first_block + n], values, preferred_element_type=F32)
            solved = solved.astype(BF16)
            sol[s] = solved
            at = pl.multiple_of(off_row + n * GROUP, GROUP)
            stacked = source[:, pl.ds(at, GROUP), :].reshape(PARTS * GROUP, B)
            slot = n % 2
            product[slot] = jnp.dot(stacked, solved, preferred_element_type=F32)
            for j in range(NB):
                target = codes[s * NB + j] - FIRST
                for i in range(ROWS):
                    into = pl.ds(i * PARTS, PARTS)
                    acc[target, into, :] += product[
                        slot, pl.ds(j * ROWS + i, PARTS, stride=GROUP), :
                    ]
            return 0

        lax.fori_loop(0, end - first, step, 0, unroll=2)

    copies[0].wait()
    collect(lead, 0, 0, FIRST // 4)
    level(lead, 0, FIRST, 0, FIRST * ROWS, True)
    copies[1].wait()
    collect(rest, 0, DIAG_LATER, LATER_PAD // 4)
    top_row = (LATER_PAD + LATER * NB) * ROWS
    collect(rest, top_row, DIAG_TOP, TOP_BLOCKS // 4)
    for first, end in LEVELS[1:]:
        off_row = LATER_PAD * ROWS + (first - FIRST) * GROUP
        level(rest, first, end, DIAG_LATER + first - FIRST, off_row, False)

    for t in range(TOP):
        own = jnp.where(row[0] == t, top_rhs[...].astype(F32), 0.0)
        base[t] = own - summed(SUB - FIRST + t)
    for k in range(TOP):
        at = DIAG_TOP + START[k] - LOW[k]
        solved = jnp.dot(weights[at + k], base[k].astype(BF16), preferred_element_type=F32)
        solved = solved.astype(BF16)
        part[k] = solved
        if k + 1 < TOP:
            below = weights[at + k + 1 : at + TOP].reshape((TOP - 1 - k) * B, B)
            update = jnp.dot(below, solved, preferred_element_type=F32)
            base[k + 1 :] = base[k + 1 :] - update.reshape(TOP - 1 - k, B, B)


def run_levels(codes, row, rhs, top_rhs, lead, rest):
    vmem = pl.BlockSpec(memory_space=pltpu.VMEM)
    smem = pl.BlockSpec(memory_space=pltpu.SMEM)
    hbm = pl.BlockSpec(memory_space=pl.ANY)
    flops = 2 * B**3 * (SUB * (1 + NB) + TOP * (TOP + 1) // 2)
    return pl.pallas_call(
        substitute,
        out_shape=(
            jax.ShapeDtypeStruct((SUB, B, B), BF16),
            jax.ShapeDtypeStruct((TOP, B, B), BF16),
        ),
        in_specs=[smem, smem, vmem, vmem, hbm, hbm],
        out_specs=(vmem, vmem),
        scratch_shapes=[
            pltpu.VMEM((PARTS, LEAD_ROWS, B), BF16),
            pltpu.VMEM((PARTS, REST_ROWS, B), BF16),
            pltpu.VMEM((PARTS * GROUP, B), F32),
            pltpu.VMEM((4, B, B), F32),
            pltpu.VMEM((W_BLOCKS, B, B), BF16),
            pltpu.VMEM((2, PARTS * GROUP, B), F32),
            pltpu.VMEM((SUB - FIRST + TOP, B, B), F32),
            pltpu.VMEM((TOP, B, B), F32),
            pltpu.SemaphoreType.DMA((2,)),
        ],
        compiler_params=pltpu.CompilerParams(vmem_limit_bytes=40 << 20),
        cost_estimate=pl.CostEstimate(flops=flops, bytes_accessed=12 << 20, transcendentals=0),
    )(codes, row, rhs, top_rhs, lead, rest)


def local(local_rhs, top_rhs, diag_inv, top_inv, off_blocks, top_factor, targets):
    position = lax.axis_index("row")
    own = (jnp.arange(TOP) == position)[:, None, None]
    top_rows = jnp.where(own, top_inv, top_factor[0])
    top_all = lax.all_gather(top_rows, "row", axis=0)
    top_rows = jnp.concatenate([top_all[LOW[k] :, k] for k in range(TOP)], axis=0)
    pad = jnp.zeros(((LATER_PAD - LATER) * ROWS, B), BF16)
    packed = jnp.concatenate(
        [
            diag_inv[:FIRST].reshape(-1, B),
            off_blocks[:FIRST].reshape(-1, B),
            diag_inv[FIRST:].reshape(-1, B),
            pad,
            off_blocks[FIRST:].reshape(-1, B),
            top_rows.reshape(-1, B),
        ],
        axis=0,
    )
    gathered = lax.all_gather(packed, "rhs", axis=0)
    solved, part = run_levels(
        targets.reshape(-1), position[None], local_rhs, top_rhs[0],
        gathered[:, :LEAD_ROWS], gathered[:, LEAD_ROWS:],
    )
    parts = lax.all_to_all(part, "row", 0, 0, tiled=True)
    own_top = jnp.sum(parts.astype(F32), axis=0, keepdims=True).astype(BF16)
    return solved, own_top


def solution(mesh):
    in_specs = (
        P("row", None, "rhs"),
        P("row", None, "rhs"),
        P("row", "rhs", None),
        P("row", "rhs", None),
        P("row", None, "rhs", None),
        P("row", None, "rhs", None),
        P("row", None),
    )
    out_specs = (P("row", None, "rhs"), P("row", None, "rhs"))
    return jax.shard_map(local, mesh=mesh, in_specs=in_specs, out_specs=out_specs, check_vma=False)
```

time: 552 us -> 172 us (0.31)
  blocking collectives: 488 us -> 27.4 us
  waiting for transfers between devices: 0.09 us -> 97.5 us
  matrix products: 23.9 us -> 0 us
  Pallas kernels: 0 us -> 20.6 us
  local copies, waits for them, and re-layouts: 18.8 us -> 10.3 us
    psum x8 -> x0, blocking collectives: 252 us -> none  [spread(): return lax.psum(jnp.where(mine, shard, jnp.zeros_like(shard)), axis)]
    all_gather x6 -> x1, blocking collectives: 236 us -> 15.8 us  [local(): top_all = lax.all_gather(top_rows, 'row', axis=0)]
    all_gather x2 -> x1, waiting for transfers between devices: 0.04 us -> 97.5 us  [local(): gathered = lax.all_gather(packed, 'rhs', axis=0)]
    dot_general x25 -> x0, matrix products: 23.9 us -> none  [the longest x3 12.6 us: spread_updates(): jnp.einsum('yiko,yoq->yikq', slice_part, level_partial, preferred_element...]
    pallas_call x0 -> x1, Pallas kernels: none -> 20.6 us  [run_levels(): pl.pallas_call(substitute, out_shape=(jax.ShapeDtypeStruct((SUB, B, B), B...]
    all_to_all x0 -> x1, blocking collectives: none -> 11.6 us  [local(): parts = lax.all_to_all(part, 'row', 0, 0, tiled=True)]
    reshape x3 -> x1, local copies, waits for them, and re-layouts: 11.4 us -> 0.1 us  [local(): targets.reshape(-1)]
    slice x13 -> x10, local copies, waits for them, and re-layouts: 2.63 us -> 8.4 us  [the longest x1 2.51 us: local(): gathered[:, LEAD_ROWS:]]
  transfers between devices with their start and end apart: 3 -> 1, of which waited for: 0 -> 1; matrix products, arithmetic and copies ran while one was open for 5% -> 1% of each run, Pallas kernels for 0% -> 0%
where the time goes in v1:
time: 172 us; the launch traced here: 171 us
  waiting for transfers between devices  97.5 us (57%)
  blocking collectives  27.4 us (16%)
  Pallas kernels  20.6 us (12%)
  between operations  14.2 us (8%)
  local copies, waits for them, and re-layouts  10.3 us (6%)
    all_gather x1, waiting for transfers between devices, local(): gathered = lax.all_gather(packed, 'rhs', axis=0)  97.5 us
    pallas_call x1, Pallas kernels, run_levels(): pl.pallas_call(substitute, out_shape=(jax.ShapeDtypeStruct((SUB, B, B), B...  20.6 us
    all_gather x1, blocking collectives, local(): top_all = lax.all_gather(top_rows, 'row', axis=0)  15.8 us
    all_to_all x1, blocking collectives, local(): parts = lax.all_to_all(part, 'row', 0, 0, tiled=True)  11.6 us
  transfers between devices with their start and end apart: 1, of which 1 were waited for; matrix products, arithmetic and copies ran while one was open for 1% of the time, Pallas kernels for 0%

profile of v1, /device:TPU:1, one launch (start us, length us, event | category | flops | bytes accessed | tf_op | source)
XLA Modules:
  0.0 171.5 jit_solution(2211171588921640610)
XLA Ops:
  7.2 0.0 all-gather.3.cloned.1.call-start
  7.2 0.8 copy_select_fusion
  8.0 15.8 %all_gather.10 = bf16[8,8,4,128]{3,1,2,0:T(8,128)(2,1)S(1)} all-gather(bf16[1,8,4,128]{3,1,2,0:T(8,128)(2,1)S(1)} %copy_select_fusion), channel_id=1, replica_groups=mesh['row'=8,'rhs'=32] {'row'}, dimensions={0}, use_global_device_ids=true | all-gather | bytes 73728 | tf_op jit(solution)/shard_map/all_gather | solution.py:145
  23.9 0.8 slice.42
  24.7 0.7 slice.44
  25.4 0.9 slice.43
  26.3 0.9 slice.45
  27.3 0.2 concatenate.6
  27.6 0.0 copy-start.2
  27.6 0.7 copy-done.2
  28.3 0.0 all-gather.3.cloned.1.call-update
  28.3 0.8 copy.25
  29.1 0.1 reshape.35.codes
  29.2 97.5 %all-gather.3.cloned.1.call-done = bf16[32256,128]{1,0:T(8,128)(2,1)} async-done(((bf16[1008,128]{1,0:T(8,128)(2,1)}), bf16[32256,128]{1,0:T(8,128)(2,1)}) %all-gather.3.cloned.1.call-update) | async-done | bytes 8257552 | tf_op jit(solution)/shard_map/all_gather | solution.py:159
  126.7 2.5 %slice.65.rest_hbm = bf16[32,528,128]{2,1,0:T(8,128)(2,1)S(1)} slice(bf16[32,1008,128]{2,1,0:T(8,128)(2,1)} %bitcast.27), slice={[0:32], [480:1008], [0:128]} | slice | bytes 8650752 | tf_op jit(solution)/shard_map/slice | solution.py:162
  129.2 0.0 copy-start
  129.2 0.0 copy-start.1
  129.2 2.5 %slice.64.lead_hbm = bf16[32,480,128]{2,1,0:T(8,128)(2,1)S(1)} slice(bf16[32,1008,128]{2,1,0:T(8,128)(2,1)} %bitcast.28), slice={[0:32], [0:480], [0:128]} | slice | bytes 7864320 | tf_op jit(solution)/shard_map/slice | solution.py:162
  131.7 0.0 copy-done
  131.7 0.0 copy-done.1
  131.7 20.6 %shard_map.86 = (bf16[42,128,128]{2,1,0:T(8,128)(2,1)}, bf16[8,128,128]{2,1,0:T(8,128)(2,1)S(1)}) custom-call(s32[168]{0:T(256)S(1)} %reshape.35.codes, s32[1]{0:T(128)} %bitcast.row, bf16[42,128,128]{2,1,0:T(8,128)(2,1)S(1)} %copy-done, bf16[128,128]{1,0:T(8,128)(2,1)S(1)} %bitcast.26, bf16[32,480,128]{2,1,0:T(8,128)(2,1)S(1)} %slice.64.lead_hbm, ...), custom_call_target="tpu_custom_call" | custom-call | flops 1031798784 | bytes 12582912 | tf_op jit(solution)/shard_map/pallas_call | solution.py:117
  152.4 11.6 %all_to_all.5 = bf16[8,128,128]{2,1,0:T(8,128)(2,1)S(1)} all-to-all(bf16[8,128,128]{2,1,0:T(8,128)(2,1)S(1)} %get-tuple-element.5), channel_id=1, replica_groups=mesh['row'=8,'rhs'=32] {'row'}, dimensions={0} | all-to-all | bytes 524288 | tf_op jit(solution)/shard_map/all_to_all | solution.py:164
  164.0 0.7 reduce_sum.12
  (16 shorter events, 0.2 us)
Async XLA Ops:
  7.2 119.5 %all-gather.3.cloned.1.call-start = ((), (), s32[]{:S(2)}) async-start(), calls=%async_computation.1 | async-start | bytes 8515584 | tf_op jit(solution)/shard_map/all_gather | solution.py:159
  27.6 0.7 copy-start.2
  129.2 2.5 %copy-start = (bf16[42,128,128]{2,1,0:T(8,128)(2,1)S(1)}, bf16[42,128,128]{2,1,0:T(8,128)(2,1)}, u32[]{:S(2)}) copy-start(bf16[42,128,128]{2,1,0:T(8,128)(2,1)} %rhs.1) | copy-start | bytes 4128772
  129.2 2.5 %copy-start.1 = (bf16[1,128,128]{2,1,0:T(8,128)(2,1)S(1)}, bf16[1,128,128]{2,1,0:T(8,128)(2,1)}, u32[]{:S(2)}) copy-start(bf16[1,128,128]{2,1,0:T(8,128)(2,1)} %param.8) | copy-start | bytes 98308
Sparse Core Ops, SparseCore 0:
  28.4 98.1 all-gather.2

commit v2 on v1

v2 whole, which is shorter than its diff:
```python
import jax
import jax.numpy as jnp
from jax import lax
from jax.experimental import pallas as pl
from jax.experimental.pallas import tpu as pltpu
from jax.sharding import PartitionSpec as P

SUB = 42
LEVELS = ((0, 24), (24, 36), (36, 42))
B = 128
NB = 4
TOP = 8
PARTS = 32
ROWS = B // PARTS
GROUP = 16
FIRST = LEVELS[0][1]
LATER = SUB - FIRST
LATER_PAD = -(-LATER // 4) * 4
LOW = tuple(k - k % 2 for k in range(TOP))
START = tuple(sum(TOP - LOW[q] for q in range(k)) for k in range(TOP))
TOP_BLOCKS = sum(TOP - low for low in LOW)
LEAD_ROWS = FIRST * (1 + NB) * ROWS
REST_ROWS = (LATER_PAD + LATER * NB + TOP_BLOCKS) * ROWS
TOP_ROW = (LATER_PAD + LATER * NB) * ROWS
NY, NZ = 4, 8
Z_ORDER = (0, 1, -1, 2, -2, 3, -3, 4)
F32 = jnp.float32
BF16 = jnp.bfloat16


def collect(source, stage, natural, weights, first_row, first_block, groups):
    def step(g, _):
        at = pl.multiple_of(first_row + g * GROUP, GROUP)
        rows = source[:, pl.ds(at, GROUP), :].astype(F32)
        stage[...] = rows.reshape(PARTS * GROUP, B)
        for q in range(GROUP // ROWS):
            for i in range(ROWS):
                natural[q, pl.ds(i, PARTS, stride=ROWS), :] = stage[
                    pl.ds(q * ROWS + i, PARTS, stride=GROUP), :
                ]
            weights[first_block + g * 4 + q] = natural[q].astype(BF16)
        return 0

    lax.fori_loop(0, groups, step, 0)


def summed(acc, natural, target):
    for i in range(ROWS):
        natural[0, pl.ds(i, PARTS, stride=ROWS), :] = acc[target, pl.ds(i * PARTS, PARTS), :]
    return natural[0]


def solve_level(
    codes, rhs, source, weights, product, acc, natural, sol,
    first, end, shift, first_block, off_row, is_leaf,
):
    def step(n, _):
        s = first + n
        values = rhs[s - shift]
        if not is_leaf:
            values = (values.astype(F32) - summed(acc, natural, s - FIRST)).astype(BF16)
        solved = jnp.dot(weights[first_block + n], values, preferred_element_type=F32)
        solved = solved.astype(BF16)
        sol[s - shift] = solved
        at = pl.multiple_of(off_row + n * GROUP, GROUP)
        stacked = source[:, pl.ds(at, GROUP), :].reshape(PARTS * GROUP, B)
        slot = n % 2
        product[slot] = jnp.dot(stacked, solved, preferred_element_type=F32)
        for j in range(NB):
            target = codes[s * NB + j] - FIRST
            for i in range(ROWS):
                into = pl.ds(i * PARTS, PARTS)
                acc[target, into, :] += product[
                    slot, pl.ds(j * ROWS + i, PARTS, stride=GROUP), :
                ]
        return 0

    lax.fori_loop(0, end - first, step, 0, unroll=2)


def place(pieces, gathered, place_row, sems):
    copies = []
    for n, (ref, slot, dy, dz) in enumerate(pieces):
        part = lax.rem(place_row[1] - dy + NY, NY) * NZ + lax.rem(place_row[2] - dz + NZ, NZ)
        copies.append(pltpu.make_async_copy(ref.at[slot], gathered.at[part], sems.at[n]))
    for copy in copies:
        copy.start()
    return copies


def lead_pieces(own, right, left, far_low, far_high):
    half = NZ // 2
    pieces = []
    for q, dz in enumerate(Z_ORDER):
        pieces += [(own, q, 0, dz), (right, q, 1, dz), (left, q, -1, dz)]
        pieces.append((far_low, q, 2, dz) if q < half else (far_high, q - half, 2, dz))
    return pieces


def rest_pieces(near, far_low, far_high):
    pieces = []
    for q, dy in enumerate((0, 1, -1, 2)):
        pieces += [(ref, q, dy, Z_ORDER[m]) for m, ref in enumerate(near)]
        pieces.append((far_low, q, dy, 4) if q < 2 else (far_high, q - 2, dy, 4))
    return pieces


def leaf_level(
    codes, where, rhs, own, right, left, far_low, far_high, sol, acc_out,
    lead, stage, natural, weights, product, sems,
):
    copies = place(lead_pieces(own, right, left, far_low, far_high), lead, where, sems)
    acc_out[...] = jnp.zeros_like(acc_out)
    for copy in copies:
        copy.wait()
    collect(lead, stage, natural, weights, 0, 0, FIRST // 4)
    solve_level(
        codes, rhs, lead, weights, product, acc_out, natural, sol,
        0, FIRST, 0, 0, FIRST * ROWS, True,
    )


def later_levels(
    codes, where, rhs_hbm, top_rhs, acc_in, sol_in, n0, n1, n2, n3, n4, n5, n6, far_low, far_high,
    sol_hbm, part, rest, rhs, acc, sol, stage, natural, weights, product, base, sems, more_sems,
):
    del sol_in
    loads = (
        pltpu.make_async_copy(rhs_hbm.at[pl.ds(FIRST, LATER)], rhs, more_sems.at[0]),
        pltpu.make_async_copy(acc_in, acc, more_sems.at[1]),
    )
    for copy in loads:
        copy.start()
    pieces = rest_pieces((n0, n1, n2, n3, n4, n5, n6), far_low, far_high)
    for copy in place(pieces, rest, where, sems):
        copy.wait()
    collect(rest, stage, natural, weights, 0, 0, LATER_PAD // 4)
    collect(rest, stage, natural, weights, TOP_ROW, LATER_PAD, TOP_BLOCKS // 4)
    for copy in loads:
        copy.wait()
    for first, end in LEVELS[1:]:
        off_row = LATER_PAD * ROWS + (first - FIRST) * GROUP
        solve_level(
            codes, rhs, rest, weights, product, acc, natural, sol,
            first, end, FIRST, first - FIRST, off_row, False,
        )
    store = pltpu.make_async_copy(sol, sol_hbm.at[pl.ds(FIRST, LATER)], more_sems.at[2])
    store.start()

    for t in range(TOP):
        own = jnp.where(where[0] == t, top_rhs[...].astype(F32), 0.0)
        base[t] = own - summed(acc, natural, SUB - FIRST + t)
    for k in range(TOP):
        at = LATER_PAD + START[k] - LOW[k]
        solved = jnp.dot(weights[at + k], base[k].astype(BF16), preferred_element_type=F32)
        solved = solved.astype(BF16)
        part[k] = solved
        if k + 1 < TOP:
            below = weights[at + k + 1 : at + TOP].reshape((TOP - 1 - k) * B, B)
            update = jnp.dot(below, solved, preferred_element_type=F32)
            base[k + 1 :] = base[k + 1 :] - update.reshape(TOP - 1 - k, B, B)
    store.wait()


VMEM = pl.BlockSpec(memory_space=pltpu.VMEM)
SMEM = pl.BlockSpec(memory_space=pltpu.SMEM)
HBM = pl.BlockSpec(memory_space=pl.ANY)
WORK = (
    pltpu.VMEM((PARTS * GROUP, B), F32),
    pltpu.VMEM((4, B, B), F32),
)
ACC_SHAPE = (SUB - FIRST + TOP, B, B)


def cost(blocks, nbytes):
    return pl.CostEstimate(flops=2 * B**3 * blocks, bytes_accessed=nbytes, transcendentals=0)


def run_leaves(codes, where, rhs, pieces):
    block = pl.BlockSpec((FIRST, B, B), lambda n: (0, 0, 0))
    return pl.pallas_call(
        leaf_level,
        grid=(1,),
        out_shape=(
            jax.ShapeDtypeStruct((SUB, B, B), BF16),
            jax.ShapeDtypeStruct(ACC_SHAPE, F32),
        ),
        in_specs=[SMEM, SMEM, block] + [HBM] * 5,
        out_specs=(block, pl.BlockSpec(ACC_SHAPE, lambda n: (0, 0, 0))),
        scratch_shapes=[
            pltpu.VMEM((PARTS, LEAD_ROWS, B), BF16),
            *WORK,
            pltpu.VMEM((FIRST, B, B), BF16),
            pltpu.VMEM((2, PARTS * GROUP, B), F32),
            pltpu.SemaphoreType.DMA((PARTS,)),
        ],
        compiler_params=pltpu.CompilerParams(vmem_limit_bytes=32 << 20),
        cost_estimate=cost(FIRST * (1 + NB), 8 << 20),
    )(codes, where, rhs, *pieces)


def run_later(codes, where, rhs, top_rhs, acc, sol, pieces):
    return pl.pallas_call(
        later_levels,
        out_shape=(
            jax.ShapeDtypeStruct((SUB, B, B), BF16),
            jax.ShapeDtypeStruct((TOP, B, B), BF16),
        ),
        in_specs=[SMEM, SMEM, HBM, VMEM, HBM, HBM] + [HBM] * 9,
        out_specs=(HBM, VMEM),
        input_output_aliases={5: 0},
        scratch_shapes=[
            pltpu.VMEM((PARTS, REST_ROWS, B), BF16),
            pltpu.VMEM((LATER, B, B), BF16),
            pltpu.VMEM(ACC_SHAPE, F32),
            pltpu.VMEM((LATER, B, B), BF16),
            *WORK,
            pltpu.VMEM((LATER_PAD + TOP_BLOCKS, B, B), BF16),
            pltpu.VMEM((2, PARTS * GROUP, B), F32),
            pltpu.VMEM((TOP, B, B), F32),
            pltpu.SemaphoreType.DMA((PARTS,)),
            pltpu.SemaphoreType.DMA((3,)),
        ],
        compiler_params=pltpu.CompilerParams(vmem_limit_bytes=32 << 20),
        cost_estimate=cost(LATER * (1 + NB) + TOP * (TOP + 1) // 2, 8 << 20),
    )(codes, where, rhs, top_rhs, acc, sol, *pieces)


def shift_z(x, k):
    pairs = [(y * NZ + z, y * NZ + (z + k) % NZ) for y in range(NY) for z in range(NZ)]
    return lax.ppermute(x, "rhs", pairs)


def shift_y(x, k):
    pairs = [(y * NZ + z, (y + k) % NY * NZ + z) for y in range(NY) for z in range(NZ)]
    return lax.ppermute(x, "rhs", pairs)


def gather_z_then_y(x):
    held, right, left = [x], x, x
    for _ in range(3):
        right, left = shift_z(right, 1), shift_z(left, -1)
        held += [right, left]
    held.append(shift_z(right, 1))
    own = jnp.stack(held)
    right, left = shift_y(own, 1), shift_y(own, -1)
    half = NZ // 2
    return own, right, left, shift_y(right[:half], 1), shift_y(left[half:], -1)


def gather_y_then_z(x):
    own = jnp.stack([x, shift_y(x, 1), shift_y(x, -1), shift_y(x, 2)])
    held, right, left = [own], own, own
    for _ in range(3):
        right, left = shift_z(right, 1), shift_z(left, -1)
        held += [right, left]
    return (*held, shift_z(right[:2], 1), shift_z(left[2:], -1))


def local(local_rhs, top_rhs, diag_inv, top_inv, off_blocks, top_factor, targets):
    position, part = lax.axis_index("row"), lax.axis_index("rhs")
    own = (jnp.arange(TOP) == position)[:, None, None]
    top_rows = jnp.where(own, top_inv, top_factor[0])
    lead = jnp.concatenate(
        [diag_inv[:FIRST].reshape(-1, B), off_blocks[:FIRST].reshape(-1, B)], axis=0
    )
    lead_all = gather_z_then_y(lead)
    top_all = lax.all_gather(top_rows, "row", axis=0)
    top_rows = jnp.concatenate([top_all[LOW[k] :, k] for k in range(TOP)], axis=0)
    rest = jnp.concatenate(
        [
            diag_inv[FIRST:].reshape(-1, B),
            jnp.zeros(((LATER_PAD - LATER) * ROWS, B), BF16),
            off_blocks[FIRST:].reshape(-1, B),
            top_rows.reshape(-1, B),
        ],
        axis=0,
    )
    rest_all = gather_y_then_z(rest)
    codes = targets.reshape(-1)
    where = jnp.stack([position, part // NZ, part % NZ])
    sol, acc = run_leaves(codes, where, local_rhs, lead_all)
    sol, addends = run_later(codes, where, local_rhs, top_rhs[0], acc, sol, rest_all)
    parts = lax.all_to_all(addends, "row", 0, 0, tiled=True)
    own_top = jnp.sum(parts.astype(F32), axis=0, keepdims=True).astype(BF16)
    return sol, own_top


def solution(mesh):
    in_specs = (
        P("row", None, "rhs"),
        P("row", None, "rhs"),
        P("row", "rhs", None),
        P("row", "rhs", None),
        P("row", None, "rhs", None),
        P("row", None, "rhs", None),
        P("row", None),
    )
    out_specs = (P("row", None, "rhs"), P("row", None, "rhs"))
    return jax.shard_map(local, mesh=mesh, in_specs=in_specs, out_specs=out_specs, check_vma=False)
```

time: 172 us -> 142 us (0.83)
  waiting for transfers between devices: 97.5 us -> 32.9 us
  starting transfers between devices: 0.04 us -> 30.9 us
  between operations: 14.2 us -> 1.05 us
  Pallas kernels: 20.6 us -> 33.3 us
  blocking collectives: 27.4 us -> 29.8 us
    all_gather x1 -> x0, waiting for transfers between devices: 97.5 us -> none  [local(): gathered = lax.all_gather(packed, 'rhs', axis=0)]
    ppermute x0 -> x22, waiting for transfers between devices: none -> 32.9 us  [the longest x15 23.3 us: shift_z(): return lax.ppermute(x, 'rhs', pairs)]
    ppermute x0 -> x22, starting transfers between devices: none -> 30.9 us  [the longest x15 23.4 us: shift_z(): return lax.ppermute(x, 'rhs', pairs)]
    pallas_call x1 -> x2, Pallas kernels: 20.6 us -> 33.3 us  [the longest x1 19.1 us: run_later(): pl.pallas_call(later_levels, out_shape=(jax.ShapeDtypeStruct((SUB, B, B),...]
    all_to_all x1, blocking collectives: 11.6 us -> 16 us  [local(): parts = lax.all_to_all(addends, 'row', 0, 0, tiled=True)]
    unnamed x12 -> x45, local copies, waits for them, and re-layouts: 1.56 us -> 4.71 us
    all_gather x1, blocking collectives: 15.8 us -> 13.8 us  [local(): top_all = lax.all_gather(top_rows, 'row', axis=0)]
    slice x2 -> x4, local copies, waits for them, and re-layouts: 4.99 us -> 3.14 us  [the longest x2 1.46 us: gather_y_then_z(): return (*held, shift_z(right[:2], 1), shift_z(left[2:], -1))]
  transfers between devices with their start and end apart: 1 -> 22, of which waited for: 1 -> 8; matrix products, arithmetic and copies ran while one was open for 1% -> 5% of each run, Pallas kernels for 0% -> 10%
where the time goes in v2:
time: 142 us
  Pallas kernels  33.3 us (23%)
  waiting for transfers between devices  32.9 us (23%)
  starting transfers between devices  30.9 us (22%)
  blocking collectives  29.8 us (21%)
  local copies, waits for them, and re-layouts  11.7 us (8%)
  other arithmetic  1.87 us (1%)
    ppermute x15, starting transfers between devices, shift_z(): return lax.ppermute(x, 'rhs', pairs)  23.4 us
    ppermute x15, waiting for transfers between devices, shift_z(): return lax.ppermute(x, 'rhs', pairs)  23.3 us
    pallas_call x1, Pallas kernels, run_later(): pl.pallas_call(later_levels, out_shape=(jax.ShapeDtypeStruct((SUB, B, B),...  19.1 us
    all_to_all x1, blocking collectives, local(): parts = lax.all_to_all(addends, 'row', 0, 0, tiled=True)  16 us
    pallas_call x1, Pallas kernels, run_leaves(): pl.pallas_call(leaf_level, grid=(1,), out_shape=(jax.ShapeDtypeStruct((SU...  14.2 us
    all_gather x1, blocking collectives, local(): top_all = lax.all_gather(top_rows, 'row', axis=0)  13.8 us
    ppermute x7, waiting for transfers between devices, shift_y(): return lax.ppermute(x, 'rhs', pairs)  9.57 us
    ppermute x7, starting transfers between devices, shift_y(): return lax.ppermute(x, 'rhs', pairs)  7.47 us
  transfers between devices with their start and end apart: 22, of which 8 were waited for; matrix products, arithmetic and copies ran while one was open for 5% of the time, Pallas kernels for 10%

profile of v2, /device:TPU:1, one launch (start us, length us, event | category | flops | bytes accessed | tf_op | source)
XLA Modules:
  0.0 141.5 jit_solution(8420645870865005800)
XLA Ops:
  0.6 0.9 slice.49
  1.6 0.8 slice.48
  2.3 2.5 %collective-permute-start = (bf16[480,128]{1,0:T(8,128)(2,1)S(1)}, bf16[480,128]{1,0:T(8,128)(2,1)S(1)}, u32[]{:S(2)}, u32[]{:S(2)}) collective-permute-start(bf16[480,128]{1,0:T(8,128)(2,1)S(1)} %pad_maximum_fusion.2), channel_id=1, source_target_pairs={{0,1},{1,2},{2,3},{3,4},{4,5},{5,6},{6,7},{7,0},{8,9},{9,10},{10,1... | collective-permute-start | bytes 368648 | tf_op jit(solution)/shard_map/ppermute | solution.py:231
  4.9 4.0 %collective-permute-start.1 = (bf16[480,128]{1,0:T(8,128)(2,1)S(1)}, bf16[480,128]{1,0:T(8,128)(2,1)S(1)}, u32[]{:S(2)}, u32[]{:S(2)}) collective-permute-start(bf16[480,128]{1,0:T(8,128)(2,1)S(1)} %pad_maximum_fusion.2), channel_id=1, source_target_pairs={{0,7},{1,0},{2,1},{3,2},{4,3},{5,4},{6,5},{7,6},{8,15},{9,8},{10,9... | collective-permute-start | bytes 368648 | tf_op jit(solution)/shard_map/ppermute | solution.py:231
  8.9 0.8 copy_select_fusion
  9.7 13.8 %all_gather.4 = bf16[8,8,4,128]{3,1,2,0:T(8,128)(2,1)S(1)} all-gather(bf16[1,8,4,128]{3,1,2,0:T(8,128)(2,1)S(1)} %copy_select_fusion), channel_id=1, replica_groups=mesh['row'=8,'rhs'=32] {'row'}, dimensions={0}, use_global_device_ids=true | all-gather | bytes 73728 | tf_op jit(solution)/shard_map/all_gather | solution.py:268
  23.6 0.9 slice.53
  24.6 0.7 slice.52
  25.3 0.2 concatenate.10
  25.6 0.1 pad.5.clone
  25.6 0.1 pad_maximum_fusion.1
  25.8 1.4 collective-permute-start.11
  27.2 1.5 %collective-permute-start.12 = (bf16[528,128]{1,0:T(8,128)(2,1)S(1)}, bf16[528,128]{1,0:T(8,128)(2,1)S(1)}, u32[]{:S(2)}, u32[]{:S(2)}) collective-permute-start(bf16[528,128]{1,0:T(8,128)(2,1)S(1)} %pad_maximum_fusion.1), channel_id=1, source_target_pairs={{0,24},{1,25},{2,26},{3,27},{4,28},{5,29},{6,30},{7,31},{8,0},{9,1... | collective-permute-start | bytes 405512 | tf_op jit(solution)/shard_map/ppermute | solution.py:236
  28.7 1.6 %collective-permute-start.13 = (bf16[528,128]{1,0:T(8,128)(2,1)S(1)}, bf16[528,128]{1,0:T(8,128)(2,1)S(1)}, u32[]{:S(2)}, u32[]{:S(2)}) collective-permute-start(bf16[528,128]{1,0:T(8,128)(2,1)S(1)} %pad_maximum_fusion.1), channel_id=1, source_target_pairs={{0,16},{1,17},{2,18},{3,19},{4,20},{5,21},{6,22},{7,23},{8,24},{9,... | collective-permute-start | bytes 405512 | tf_op jit(solution)/shard_map/ppermute | solution.py:236
  30.2 0.1 fusion.4
  30.4 0.1 collective-permute-start.2
  30.5 2.7 %collective-permute-start.3 = (bf16[480,128]{1,0:T(8,128)(2,1)S(1)}, bf16[480,128]{1,0:T(8,128)(2,1)S(1)}, u32[]{:S(2)}, u32[]{:S(2)}) collective-permute-start(bf16[480,128]{1,0:T(8,128)(2,1)S(1)} %collective-permute-done.1), channel_id=1, source_target_pairs={{0,7},{1,0},{2,1},{3,2},{4,3},{5,4},{6,5},{7,6},{8,15},{9,8},{10,9... | collective-permute-start | bytes 368648 | tf_op jit(solution)/shard_map/ppermute | solution.py:231
  33.3 0.0 collective-permute-done.11
  33.3 2.9 %collective-permute-done.13 = bf16[528,128]{1,0:T(8,128)(2,1)S(1)} collective-permute-done((bf16[528,128]{1,0:T(8,128)(2,1)S(1)}, bf16[528,128]{1,0:T(8,128)(2,1)S(1)}, u32[]{:S(2)}, u32[]{:S(2)}) %collective-permute-start.13) | collective-permute-done | bytes 135200 | tf_op jit(solution)/shard_map/ppermute | solution.py:236
  36.2 0.1 pad_maximum_fusion.n0
  36.3 0.1 collective-permute-start.14
  36.4 2.7 %collective-permute-start.15 = (bf16[4,528,128]{2,1,0:T(8,128)(2,1)S(1)}, bf16[4,528,128]{2,1,0:T(8,128)(2,1)S(1)}, u32[]{:S(2)}, u32[]{:S(2)}) collective-permute-start(bf16[4,528,128]{2,1,0:T(8,128)(2,1)S(1)} %pad_maximum_fusion.n0), channel_id=1, source_target_pairs={{0,7},{1,0},{2,1},{3,2},{4,3},{5,4},{6,5},{7,6},{8,15},{9,8},{10,9... | collective-permute-start | bytes 1622024 | tf_op jit(solution)/shard_map/ppermute | solution.py:231
  39.1 0.0 collective-permute-start.4
  39.1 0.0 collective-permute-done.3
  39.1 2.7 %collective-permute-start.5 = (bf16[480,128]{1,0:T(8,128)(2,1)S(1)}, bf16[480,128]{1,0:T(8,128)(2,1)S(1)}, u32[]{:S(2)}, u32[]{:S(2)}) collective-permute-start(bf16[480,128]{1,0:T(8,128)(2,1)S(1)} %collective-permute-done.3), channel_id=1, source_target_pairs={{0,7},{1,0},{2,1},{3,2},{4,3},{5,4},{6,5},{7,6},{8,15},{9,8},{10,9... | collective-permute-start | bytes 368648 | tf_op jit(solution)/shard_map/ppermute | solution.py:231
  41.9 11.1 %collective-permute-done.4 = bf16[480,128]{1,0:T(8,128)(2,1)S(1)} collective-permute-done((bf16[480,128]{1,0:T(8,128)(2,1)S(1)}, bf16[480,128]{1,0:T(8,128)(2,1)S(1)}, u32[]{:S(2)}, u32[]{:S(2)}) %collective-permute-start.4) | collective-permute-done | bytes 122912 | tf_op jit(solution)/shard_map/ppermute | solution.py:231
  53.0 0.0 collective-permute-start.6
  53.1 4.9 %collective-permute-done.6 = bf16[480,128]{1,0:T(8,128)(2,1)S(1)} collective-permute-done((bf16[480,128]{1,0:T(8,128)(2,1)S(1)}, bf16[480,128]{1,0:T(8,128)(2,1)S(1)}, u32[]{:S(2)}, u32[]{:S(2)}) %collective-permute-start.6) | collective-permute-done | bytes 122912 | tf_op jit(solution)/shard_map/ppermute | solution.py:231
  58.0 0.0 copy-start.3
  58.0 0.0 copy-start.18
  58.0 0.0 copy-start
  58.0 0.5 collective-permute-start.8
  58.5 1.0 collective-permute-start.7
  59.5 0.0 collective-permute-start.16
  59.6 0.8 copy-done.9
  60.4 0.0 collective-permute-done.15.n2
  60.4 2.7 %collective-permute-start.17 = (bf16[4,528,128]{2,1,0:T(8,128)(2,1)S(1)}, bf16[4,528,128]{2,1,0:T(8,128)(2,1)S(1)}, u32[]{:S(2)}, u32[]{:S(2)}) collective-permute-start(bf16[4,528,128]{2,1,0:T(8,128)(2,1)S(1)} %collective-permute-done.15.n2), channel_id=1, source_target_pairs={{0,7},{1,0},{2,1},{3,2},{4,3},{5,4},{6,5},{7,6},{8,15},{9,8},{10,9... | collective-permute-start | bytes 1622024 | tf_op jit(solution)/shard_map/ppermute | solution.py:231
  63.0 0.8 copy-done.11
  63.9 7.0 %collective-permute-done.16.n3 = bf16[4,528,128]{2,1,0:T(8,128)(2,1)S(1)} collective-permute-done((bf16[4,528,128]{2,1,0:T(8,128)(2,1)S(1)}, bf16[4,528,128]{2,1,0:T(8,128)(2,1)S(1)}, u32[]{:S(2)}, u32[]{:S(2)}) %collective-permute-start.16) | collective-permute-done | bytes 540704 | tf_op jit(solution)/shard_map/ppermute | solution.py:231
  70.9 0.0 collective-permute-start.18
  70.9 0.0 collective-permute-done.17.n4
  70.9 3.2 %collective-permute-start.19 = (bf16[4,528,128]{2,1,0:T(8,128)(2,1)S(1)}, bf16[4,528,128]{2,1,0:T(8,128)(2,1)S(1)}, u32[]{:S(2)}, u32[]{:S(2)}) collective-permute-start(bf16[4,528,128]{2,1,0:T(8,128)(2,1)S(1)} %collective-permute-done.17.n4), channel_id=1, source_target_pairs={{0,7},{1,0},{2,1},{3,2},{4,3},{5,4},{6,5},{7,6},{8,15},{9,8},{10,9... | collective-permute-start | bytes 1622024 | tf_op jit(solution)/shard_map/ppermute | solution.py:231
  74.1 4.1 %collective-permute-done.8.left = bf16[8,480,128]{2,1,0:T(8,128)(2,1)S(1)} collective-permute-done((bf16[8,480,128]{2,1,0:T(8,128)(2,1)S(1)}, bf16[8,480,128]{2,1,0:T(8,128)(2,1)S(1)}, u32[]{:S(2)}, u32[]{:S(2)}) %collective-permute-start.8) | collective-permute-done | bytes 983072 | tf_op jit(solution)/shard_map/ppermute | solution.py:236
  78.3 0.8 slice.65
  79.1 1.1 collective-permute-start.10
  80.2 0.8 slice.64
  81.0 0.4 collective-permute-start.9
  81.4 0.2 collective-permute-done.18.n5
  81.6 0.7 slice.74
  82.4 0.8 copy-done.5
  83.2 0.7 slice.75
  83.9 0.8 copy-done.7
  84.7 2.7 %collective-permute-start.21 = (bf16[2,528,128]{2,1,0:T(8,128)(2,1)}, bf16[2,528,128]{2,1,0:T(8,128)(2,1)}, u32[]{:S(2)}, u32[]{:S(2)}) collective-permute-start(bf16[2,528,128]{2,1,0:T(8,128)(2,1)} %slice.75), channel_id=1, source_target_pairs={{0,7},{1,0},{2,1},{3,2},{4,3},{5,4},{6,5},{7,6},{8,15},{9,8},{10,9... | collective-permute-start | bytes 811016 | tf_op jit(solution)/shard_map/ppermute | solution.py:231
  87.4 0.1 copy.16
  87.5 0.1 reshape.35.codes
  87.6 0.1 pad_add_fusion.where
  87.7 0.5 collective-permute-done.10.far_high
  88.1 2.1 %collective-permute-done.9.far_low = bf16[4,480,128]{2,1,0:T(8,128)(2,1)} collective-permute-done((bf16[4,480,128]{2,1,0:T(8,128)(2,1)}, bf16[4,480,128]{2,1,0:T(8,128)(2,1)}, u32[]{:S(2)}, u32[]{:S(2)}) %collective-permute-start.9) | collective-permute-done | bytes 491552 | tf_op jit(solution)/shard_map/ppermute | solution.py:236
  90.2 1.2 copy-done.4
  91.4 0.0 copy-start.17
  91.5 14.2 %shard_map.86 = (bf16[42,128,128]{2,1,0:T(8,128)(2,1)}, f32[26,128,128]{2,1,0:T(8,128)S(1)}) custom-call(s32[168]{0:T(256)S(1)} %reshape.35.codes, s32[3]{0:T(128)S(1)} %pad_add_fusion.where, bf16[42,128,128]{2,1,0:T(8,128)(2,1)S(1)} %copy-done, bf16[8,480,128]{2,1,0:T(8,128)(2,1)S(1)} %copy-done.4, bf16[8,480,128]{2,1,0:T(8,128)(2,1)S(1)} %collective-permute-done.7.right, ...), custom_call_target="tpu_custom_call" | custom-call | flops 503316480 | bytes 8388608 | tf_op jit(solution)/shard_map/pallas_call | solution.py:181
  105.7 19.1 %shard_map.87 = (bf16[42,128,128]{2,1,0:T(8,128)(2,1)}, bf16[8,128,128]{2,1,0:T(8,128)(2,1)S(1)}) custom-call(s32[168]{0:T(256)S(1)} %reshape.35.codes, s32[3]{0:T(128)S(1)} %pad_add_fusion.where, bf16[42,128,128]{2,1,0:T(8,128)(2,1)S(1)} %copy-done, bf16[128,128]{1,0:T(8,128)(2,1)S(1)} %bitcast.48, ...), custom_call_target="tpu_custom_call", output_to_operand_aliasing={{0}: (5, {})} | custom-call | flops 528482304 | bytes 8388608 | tf_op jit(solution)/shard_map/pallas_call | solution.py:203
  124.9 16.0 %all_to_all.5 = bf16[8,128,128]{2,1,0:T(8,128)(2,1)S(1)} all-to-all(bf16[8,128,128]{2,1,0:T(8,128)(2,1)S(1)} %get-tuple-element.9), channel_id=1, replica_groups=mesh['row'=8,'rhs'=32] {'row'}, dimensions={0} | all-to-all | bytes 524288 | tf_op jit(solution)/shard_map/all_to_all | solution.py:284
  140.9 0.7 reduce_sum.12
  (60 shorter events, 0.4 us)
Async XLA Ops:
  2.3 28.1 %collective-permute-start = (bf16[480,128]{1,0:T(8,128)(2,1)S(1)}, bf16[480,128]{1,0:T(8,128)(2,1)S(1)}, u32[]{:S(2)}, u32[]{:S(2)}) collective-permute-start(bf16[480,128]{1,0:T(8,128)(2,1)S(1)} %pad_maximum_fusion.2), channel_id=1, source_target_pairs={{0,1},{1,2},{2,3},{3,4},{4,5},{5,6},{6,7},{7,0},{8,9},{9,10},{10,1... | collective-permute-start | bytes 368648 | tf_op jit(solution)/shard_map/ppermute | solution.py:231
  4.9 25.7 %collective-permute-start.1 = (bf16[480,128]{1,0:T(8,128)(2,1)S(1)}, bf16[480,128]{1,0:T(8,128)(2,1)S(1)}, u32[]{:S(2)}, u32[]{:S(2)}) collective-permute-start(bf16[480,128]{1,0:T(8,128)(2,1)S(1)} %pad_maximum_fusion.2), channel_id=1, source_target_pairs={{0,7},{1,0},{2,1},{3,2},{4,3},{5,4},{6,5},{7,6},{8,15},{9,8},{10,9... | collective-permute-start | bytes 368648 | tf_op jit(solution)/shard_map/ppermute | solution.py:231
  25.8 7.5 %collective-permute-start.11 = (bf16[528,128]{1,0:T(8,128)(2,1)S(1)}, bf16[528,128]{1,0:T(8,128)(2,1)S(1)}, u32[]{:S(2)}, u32[]{:S(2)}) collective-permute-start(bf16[528,128]{1,0:T(8,128)(2,1)S(1)} %pad_maximum_fusion.1), channel_id=1, source_target_pairs={{0,8},{1,9},{2,10},{3,11},{4,12},{5,13},{6,14},{7,15},{8,16},{9,17... | collective-permute-start | bytes 405512 | tf_op jit(solution)/shard_map/ppermute | solution.py:236
  27.2 6.1 %collective-permute-start.12 = (bf16[528,128]{1,0:T(8,128)(2,1)S(1)}, bf16[528,128]{1,0:T(8,128)(2,1)S(1)}, u32[]{:S(2)}, u32[]{:S(2)}) collective-permute-start(bf16[528,128]{1,0:T(8,128)(2,1)S(1)} %pad_maximum_fusion.1), channel_id=1, source_target_pairs={{0,24},{1,25},{2,26},{3,27},{4,28},{5,29},{6,30},{7,31},{8,0},{9,1... | collective-permute-start | bytes 405512 | tf_op jit(solution)/shard_map/ppermute | solution.py:236
  28.7 7.5 %collective-permute-start.13 = (bf16[528,128]{1,0:T(8,128)(2,1)S(1)}, bf16[528,128]{1,0:T(8,128)(2,1)S(1)}, u32[]{:S(2)}, u32[]{:S(2)}) collective-permute-start(bf16[528,128]{1,0:T(8,128)(2,1)S(1)} %pad_maximum_fusion.1), channel_id=1, source_target_pairs={{0,16},{1,17},{2,18},{3,19},{4,20},{5,21},{6,22},{7,23},{8,24},{9,... | collective-permute-start | bytes 405512 | tf_op jit(solution)/shard_map/ppermute | solution.py:236
  30.4 8.6 %collective-permute-start.2 = (bf16[480,128]{1,0:T(8,128)(2,1)S(1)}, bf16[480,128]{1,0:T(8,128)(2,1)S(1)}, u32[]{:S(2)}, u32[]{:S(2)}) collective-permute-start(bf16[480,128]{1,0:T(8,128)(2,1)S(1)} %collective-permute-done), channel_id=1, source_target_pairs={{0,1},{1,2},{2,3},{3,4},{4,5},{5,6},{6,7},{7,0},{8,9},{9,10},{10,1... | collective-permute-start | bytes 368648 | tf_op jit(solution)/shard_map/ppermute | solution.py:231
  30.5 8.5 %collective-permute-start.3 = (bf16[480,128]{1,0:T(8,128)(2,1)S(1)}, bf16[480,128]{1,0:T(8,128)(2,1)S(1)}, u32[]{:S(2)}, u32[]{:S(2)}) collective-permute-start(bf16[480,128]{1,0:T(8,128)(2,1)S(1)} %collective-permute-done.1), channel_id=1, source_target_pairs={{0,7},{1,0},{2,1},{3,2},{4,3},{5,4},{6,5},{7,6},{8,15},{9,8},{10,9... | collective-permute-start | bytes 368648 | tf_op jit(solution)/shard_map/ppermute | solution.py:231
  36.3 44.7 %copy-start.1 = (bf16[4,528,128]{2,1,0:T(8,128)(2,1)}, bf16[4,528,128]{2,1,0:T(8,128)(2,1)S(1)}, u32[]{:S(2)}) copy-start(bf16[4,528,128]{2,1,0:T(8,128)(2,1)S(1)} %pad_maximum_fusion.n0) | copy-start | bytes 1622020
  36.3 23.2 %collective-permute-start.14 = (bf16[4,528,128]{2,1,0:T(8,128)(2,1)S(1)}, bf16[4,528,128]{2,1,0:T(8,128)(2,1)S(1)}, u32[]{:S(2)}, u32[]{:S(2)}) collective-permute-start(bf16[4,528,128]{2,1,0:T(8,128)(2,1)S(1)} %pad_maximum_fusion.n0), channel_id=1, source_target_pairs={{0,1},{1,2},{2,3},{3,4},{4,5},{5,6},{6,7},{7,0},{8,9},{9,10},{10,1... | collective-permute-start | bytes 1622024 | tf_op jit(solution)/shard_map/ppermute | solution.py:231
  36.4 24.0 %collective-permute-start.15 = (bf16[4,528,128]{2,1,0:T(8,128)(2,1)S(1)}, bf16[4,528,128]{2,1,0:T(8,128)(2,1)S(1)}, u32[]{:S(2)}, u32[]{:S(2)}) collective-permute-start(bf16[4,528,128]{2,1,0:T(8,128)(2,1)S(1)} %pad_maximum_fusion.n0), channel_id=1, source_target_pairs={{0,7},{1,0},{2,1},{3,2},{4,3},{5,4},{6,5},{7,6},{8,15},{9,8},{10,9... | collective-permute-start | bytes 1622024 | tf_op jit(solution)/shard_map/ppermute | solution.py:231
  39.1 13.9 %collective-permute-start.4 = (bf16[480,128]{1,0:T(8,128)(2,1)S(1)}, bf16[480,128]{1,0:T(8,128)(2,1)S(1)}, u32[]{:S(2)}, u32[]{:S(2)}) collective-permute-start(bf16[480,128]{1,0:T(8,128)(2,1)S(1)} %collective-permute-done.2), channel_id=1, source_target_pairs={{0,1},{1,2},{2,3},{3,4},{4,5},{5,6},{6,7},{7,0},{8,9},{9,10},{10,1... | collective-permute-start | bytes 368648 | tf_op jit(solution)/shard_map/ppermute | solution.py:231
  39.1 13.9 %collective-permute-start.5 = (bf16[480,128]{1,0:T(8,128)(2,1)S(1)}, bf16[480,128]{1,0:T(8,128)(2,1)S(1)}, u32[]{:S(2)}, u32[]{:S(2)}) collective-permute-start(bf16[480,128]{1,0:T(8,128)(2,1)S(1)} %collective-permute-done.3), channel_id=1, source_target_pairs={{0,7},{1,0},{2,1},{3,2},{4,3},{5,4},{6,5},{7,6},{8,15},{9,8},{10,9... | collective-permute-start | bytes 368648 | tf_op jit(solution)/shard_map/ppermute | solution.py:231
  53.0 4.9 %collective-permute-start.6 = (bf16[480,128]{1,0:T(8,128)(2,1)S(1)}, bf16[480,128]{1,0:T(8,128)(2,1)S(1)}, u32[]{:S(2)}, u32[]{:S(2)}) collective-permute-start(bf16[480,128]{1,0:T(8,128)(2,1)S(1)} %collective-permute-done.4), channel_id=1, source_target_pairs={{0,1},{1,2},{2,3},{3,4},{4,5},{5,6},{6,7},{7,0},{8,9},{9,10},{10,1... | collective-permute-start | bytes 368648 | tf_op jit(solution)/shard_map/ppermute | solution.py:231
  58.0 25.9 %copy-start.3 = (bf16[8,480,128]{2,1,0:T(8,128)(2,1)}, bf16[8,480,128]{2,1,0:T(8,128)(2,1)S(1)}, u32[]{:S(2)}) copy-start(bf16[8,480,128]{2,1,0:T(8,128)(2,1)S(1)} %bitcast_dynamic-update-slice_fusion.own) | copy-start | bytes 2949124
  58.0 29.4 %copy-start.18 = (s32[42,4]{0,1:T(4,128)S(1)}, s32[42,4]{0,1:T(4,128)}, u32[]{:S(2)}) copy-start(s32[42,4]{0,1:T(4,128)} %param.13) | copy-start | bytes 2020
  58.0 32.2 %copy-start = (bf16[42,128,128]{2,1,0:T(8,128)(2,1)S(1)}, bf16[42,128,128]{2,1,0:T(8,128)(2,1)}, u32[]{:S(2)}) copy-start(bf16[42,128,128]{2,1,0:T(8,128)(2,1)} %rhs_hbm.1) | copy-start | bytes 4128772
  58.0 20.3 %collective-permute-start.8 = (bf16[8,480,128]{2,1,0:T(8,128)(2,1)S(1)}, bf16[8,480,128]{2,1,0:T(8,128)(2,1)S(1)}, u32[]{:S(2)}, u32[]{:S(2)}) collective-permute-start(bf16[8,480,128]{2,1,0:T(8,128)(2,1)S(1)} %bitcast_dynamic-update-slice_fusion.own), channel_id=1, source_target_pairs={{0,24},{1,25},{2,26},{3,27},{4,28},{5,29},{6,30},{7,31},{8,0},{9,1... | collective-permute-start | bytes 2949128 | tf_op jit(solution)/shard_map/ppermute | solution.py:236
  58.5 21.7 %collective-permute-start.7 = (bf16[8,480,128]{2,1,0:T(8,128)(2,1)S(1)}, bf16[8,480,128]{2,1,0:T(8,128)(2,1)S(1)}, u32[]{:S(2)}, u32[]{:S(2)}) collective-permute-start(bf16[8,480,128]{2,1,0:T(8,128)(2,1)S(1)} %bitcast_dynamic-update-slice_fusion.own), channel_id=1, source_target_pairs={{0,8},{1,9},{2,10},{3,11},{4,12},{5,13},{6,14},{7,15},{8,16},{9,17... | collective-permute-start | bytes 2949128 | tf_op jit(solution)/shard_map/ppermute | solution.py:236
  59.5 11.4 %collective-permute-start.16 = (bf16[4,528,128]{2,1,0:T(8,128)(2,1)S(1)}, bf16[4,528,128]{2,1,0:T(8,128)(2,1)S(1)}, u32[]{:S(2)}, u32[]{:S(2)}) collective-permute-start(bf16[4,528,128]{2,1,0:T(8,128)(2,1)S(1)} %collective-permute-done.14.n1), channel_id=1, source_target_pairs={{0,1},{1,2},{2,3},{3,4},{4,5},{5,6},{6,7},{7,0},{8,9},{9,10},{10,1... | collective-permute-start | bytes 1622024 | tf_op jit(solution)/shard_map/ppermute | solution.py:231
  59.5 0.8 copy-start.9
  60.4 10.5 %collective-permute-start.17 = (bf16[4,528,128]{2,1,0:T(8,128)(2,1)S(1)}, bf16[4,528,128]{2,1,0:T(8,128)(2,1)S(1)}, u32[]{:S(2)}, u32[]{:S(2)}) collective-permute-start(bf16[4,528,128]{2,1,0:T(8,128)(2,1)S(1)} %collective-permute-done.15.n2), channel_id=1, source_target_pairs={{0,7},{1,0},{2,1},{3,2},{4,3},{5,4},{6,5},{7,6},{8,15},{9,8},{10,9... | collective-permute-start | bytes 1622024 | tf_op jit(solution)/shard_map/ppermute | solution.py:231
  63.0 0.8 copy-start.11
  70.9 13.0 %copy-start.13 = (bf16[4,528,128]{2,1,0:T(8,128)(2,1)}, bf16[4,528,128]{2,1,0:T(8,128)(2,1)S(1)}, u32[]{:S(2)}) copy-start(bf16[4,528,128]{2,1,0:T(8,128)(2,1)S(1)} %collective-permute-done.16.n3) | copy-start | bytes 1622020
  70.9 10.7 %collective-permute-start.18 = (bf16[4,528,128]{2,1,0:T(8,128)(2,1)S(1)}, bf16[4,528,128]{2,1,0:T(8,128)(2,1)S(1)}, u32[]{:S(2)}, u32[]{:S(2)}) collective-permute-start(bf16[4,528,128]{2,1,0:T(8,128)(2,1)S(1)} %collective-permute-done.16.n3), channel_id=1, source_target_pairs={{0,1},{1,2},{2,3},{3,4},{4,5},{5,6},{6,7},{7,0},{8,9},{9,10},{10,1... | collective-permute-start | bytes 1622024 | tf_op jit(solution)/shard_map/ppermute | solution.py:231
  70.9 13.0 %copy-start.15 = (bf16[4,528,128]{2,1,0:T(8,128)(2,1)}, bf16[4,528,128]{2,1,0:T(8,128)(2,1)S(1)}, u32[]{:S(2)}) copy-start(bf16[4,528,128]{2,1,0:T(8,128)(2,1)S(1)} %collective-permute-done.17.n4) | copy-start | bytes 1622020
  70.9 12.3 %collective-permute-start.19 = (bf16[4,528,128]{2,1,0:T(8,128)(2,1)S(1)}, bf16[4,528,128]{2,1,0:T(8,128)(2,1)S(1)}, u32[]{:S(2)}, u32[]{:S(2)}) collective-permute-start(bf16[4,528,128]{2,1,0:T(8,128)(2,1)S(1)} %collective-permute-done.17.n4), channel_id=1, source_target_pairs={{0,7},{1,0},{2,1},{3,2},{4,3},{5,4},{6,5},{7,6},{8,15},{9,8},{10,9... | collective-permute-start | bytes 1622024 | tf_op jit(solution)/shard_map/ppermute | solution.py:231
  79.1 9.0 %collective-permute-start.10 = (bf16[4,480,128]{2,1,0:T(8,128)(2,1)}, bf16[4,480,128]{2,1,0:T(8,128)(2,1)}, u32[]{:S(2)}, u32[]{:S(2)}) collective-permute-start(bf16[4,480,128]{2,1,0:T(8,128)(2,1)} %slice.65), channel_id=1, source_target_pairs={{0,24},{1,25},{2,26},{3,27},{4,28},{5,29},{6,30},{7,31},{8,0},{9,1... | collective-permute-start | bytes 1474568 | tf_op jit(solution)/shard_map/ppermute | solution.py:236
  81.0 9.2 %collective-permute-start.9 = (bf16[4,480,128]{2,1,0:T(8,128)(2,1)}, bf16[4,480,128]{2,1,0:T(8,128)(2,1)}, u32[]{:S(2)}, u32[]{:S(2)}) collective-permute-start(bf16[4,480,128]{2,1,0:T(8,128)(2,1)} %slice.64), channel_id=1, source_target_pairs={{0,8},{1,9},{2,10},{3,11},{4,12},{5,13},{6,14},{7,15},{8,16},{9,17... | collective-permute-start | bytes 1474568 | tf_op jit(solution)/shard_map/ppermute | solution.py:236
  82.4 0.8 copy-start.5
  83.2 22.5 %collective-permute-start.20 = (bf16[2,528,128]{2,1,0:T(8,128)(2,1)}, bf16[2,528,128]{2,1,0:T(8,128)(2,1)}, u32[]{:S(2)}, u32[]{:S(2)}) collective-permute-start(bf16[2,528,128]{2,1,0:T(8,128)(2,1)} %slice.74), channel_id=1, source_target_pairs={{0,1},{1,2},{2,3},{3,4},{4,5},{5,6},{6,7},{7,0},{8,9},{9,10},{10,1... | collective-permute-start | bytes 811016 | tf_op jit(solution)/shard_map/ppermute | solution.py:231
  83.9 0.8 copy-start.7
  84.7 20.9 %collective-permute-start.21 = (bf16[2,528,128]{2,1,0:T(8,128)(2,1)}, bf16[2,528,128]{2,1,0:T(8,128)(2,1)}, u32[]{:S(2)}, u32[]{:S(2)}) collective-permute-start(bf16[2,528,128]{2,1,0:T(8,128)(2,1)} %slice.75), channel_id=1, source_target_pairs={{0,7},{1,0},{2,1},{3,2},{4,3},{5,4},{6,5},{7,6},{8,15},{9,8},{10,9... | collective-permute-start | bytes 811016 | tf_op jit(solution)/shard_map/ppermute | solution.py:231
  87.7 18.0 %copy-start.2 = (bf16[4,528,128]{2,1,0:T(8,128)(2,1)S(1)}, bf16[4,528,128]{2,1,0:T(8,128)(2,1)}, u32[]{:S(2)}) copy-start(bf16[4,528,128]{2,1,0:T(8,128)(2,1)} %copy-done.1) | copy-start | bytes 1622020
  90.2 1.2 copy-start.4
  91.4 14.3 %copy-start.6 = (bf16[4,528,128]{2,1,0:T(8,128)(2,1)S(1)}, bf16[4,528,128]{2,1,0:T(8,128)(2,1)}, u32[]{:S(2)}) copy-start(bf16[4,528,128]{2,1,0:T(8,128)(2,1)} %copy-done.5) | copy-start | bytes 1622020
  91.4 14.3 %copy-start.8 = (bf16[4,528,128]{2,1,0:T(8,128)(2,1)S(1)}, bf16[4,528,128]{2,1,0:T(8,128)(2,1)}, u32[]{:S(2)}) copy-start(bf16[4,528,128]{2,1,0:T(8,128)(2,1)} %copy-done.7) | copy-start | bytes 1622020
  91.4 14.3 %copy-start.10 = (bf16[4,528,128]{2,1,0:T(8,128)(2,1)S(1)}, bf16[4,528,128]{2,1,0:T(8,128)(2,1)}, u32[]{:S(2)}) copy-start(bf16[4,528,128]{2,1,0:T(8,128)(2,1)} %copy-done.9) | copy-start | bytes 1622020
  91.4 14.3 %copy-start.12 = (bf16[4,528,128]{2,1,0:T(8,128)(2,1)S(1)}, bf16[4,528,128]{2,1,0:T(8,128)(2,1)}, u32[]{:S(2)}) copy-start(bf16[4,528,128]{2,1,0:T(8,128)(2,1)} %copy-done.11) | copy-start | bytes 1622020
  91.4 14.3 %copy-start.14 = (bf16[4,528,128]{2,1,0:T(8,128)(2,1)S(1)}, bf16[4,528,128]{2,1,0:T(8,128)(2,1)}, u32[]{:S(2)}) copy-start(bf16[4,528,128]{2,1,0:T(8,128)(2,1)} %copy-done.13) | copy-start | bytes 1622020
  91.4 14.3 %copy-start.16 = (bf16[4,528,128]{2,1,0:T(8,128)(2,1)S(1)}, bf16[4,528,128]{2,1,0:T(8,128)(2,1)}, u32[]{:S(2)}) copy-start(bf16[4,528,128]{2,1,0:T(8,128)(2,1)} %copy-done.15) | copy-start | bytes 1622020
  91.4 14.3 %copy-start.17 = (bf16[1,128,128]{2,1,0:T(8,128)(2,1)S(1)}, bf16[1,128,128]{2,1,0:T(8,128)(2,1)}, u32[]{:S(2)}) copy-start(bf16[1,128,128]{2,1,0:T(8,128)(2,1)} %param.8) | copy-start | bytes 98308

commit v3 on v2

v3 whole, which is shorter than its diff:
```python
import jax
import jax.numpy as jnp
from jax import lax
from jax.experimental import pallas as pl
from jax.experimental.pallas import tpu as pltpu
from jax.sharding import PartitionSpec as P

SUB = 42
LEVELS = ((0, 24), (24, 36), (36, 42))
B = 128
NB = 4
TOP = 8
PARTS = 32
ROWS = B // PARTS
GROUP = 16
FIRST = LEVELS[0][1]
LATER = SUB - FIRST
LATER_PAD = -(-LATER // 4) * 4
LOW = tuple(k - k % 2 for k in range(TOP))
START = tuple(sum(TOP - LOW[q] for q in range(k)) for k in range(TOP))
TOP_BLOCKS = sum(TOP - low for low in LOW)
LEAD_ROWS = FIRST * (1 + NB) * ROWS
REST_ROWS = (LATER_PAD + LATER * NB + TOP_BLOCKS) * ROWS
TOP_ROW = (LATER_PAD + LATER * NB) * ROWS
NY, NZ = 4, 8
ROW, RHS = ("x", "core"), ("y", "z")
F32 = jnp.float32
BF16 = jnp.bfloat16


def collect(source, stage, natural, weights, first_row, first_block, groups):
    def step(g, _):
        at = pl.multiple_of(first_row + g * GROUP, GROUP)
        rows = source[:, pl.ds(at, GROUP), :].astype(F32)
        stage[...] = rows.reshape(PARTS * GROUP, B)
        for q in range(GROUP // ROWS):
            for i in range(ROWS):
                natural[q, pl.ds(i, PARTS, stride=ROWS), :] = stage[
                    pl.ds(q * ROWS + i, PARTS, stride=GROUP), :
                ]
            weights[first_block + g * 4 + q] = natural[q].astype(BF16)
        return 0

    lax.fori_loop(0, groups, step, 0)


def summed(acc, natural, target):
    for i in range(ROWS):
        natural[0, pl.ds(i, PARTS, stride=ROWS), :] = acc[target, pl.ds(i * PARTS, PARTS), :]
    return natural[0]


def solve_level(
    codes, rhs, source, weights, product, acc, natural, sol,
    first, end, shift, first_block, off_row, is_leaf,
):
    for n in range(end - first):
        values = rhs[first + n]
        if not is_leaf:
            values = (values.astype(F32) - summed(acc, natural, first + n - FIRST)).astype(BF16)
        solved = jnp.dot(weights[first_block + n], values, preferred_element_type=F32)
        sol[first + n - shift] = solved.astype(BF16)
    for n in range(end - first):
        stacked = source[:, pl.ds(off_row + n * GROUP, GROUP), :].reshape(PARTS * GROUP, B)
        slot = n % 2
        product[slot] = jnp.dot(stacked, sol[first + n - shift], preferred_element_type=F32)
        for j in range(NB):
            target = codes[(first + n) * NB + j] - FIRST
            for i in range(ROWS):
                into = pl.ds(i * PARTS, PARTS)
                acc[target, into, :] += product[
                    slot, pl.ds(j * ROWS + i, PARTS, stride=GROUP), :
                ]


def leaf_level(codes, rhs, lead, sol, acc, stage, natural, weights, product):
    acc[...] = jnp.zeros_like(acc)
    collect(lead, stage, natural, weights, 0, 0, FIRST // 4)
    solve_level(
        codes, rhs, lead, weights, product, acc, natural, sol,
        0, FIRST, 0, 0, FIRST * ROWS, True,
    )


def later_levels(
    codes, where, rhs, top_rhs, acc_in, leaf_sol, rest,
    sol_hbm, part, acc, sol, stage, natural, weights, product, base, sems,
):
    stores = (
        pltpu.make_async_copy(leaf_sol, sol_hbm.at[pl.ds(0, FIRST)], sems.at[0]),
        pltpu.make_async_copy(sol, sol_hbm.at[pl.ds(FIRST, LATER)], sems.at[1]),
    )
    stores[0].start()
    acc[...] = acc_in[...]
    collect(rest, stage, natural, weights, 0, 0, LATER_PAD // 4)
    collect(rest, stage, natural, weights, TOP_ROW, LATER_PAD, TOP_BLOCKS // 4)
    for first, end in LEVELS[1:]:
        off_row = LATER_PAD * ROWS + (first - FIRST) * GROUP
        solve_level(
            codes, rhs, rest, weights, product, acc, natural, sol,
            first, end, FIRST, first - FIRST, off_row, False,
        )
    stores[1].start()

    for t in range(TOP):
        own = jnp.where(where[0] == t, top_rhs[...].astype(F32), 0.0)
        base[t] = own - summed(acc, natural, SUB - FIRST + t)
    for k in range(TOP):
        at = LATER_PAD + START[k] - LOW[k]
        solved = jnp.dot(weights[at + k], base[k].astype(BF16), preferred_element_type=F32)
        solved = solved.astype(BF16)
        part[k] = solved
        if k + 1 < TOP:
            below = weights[at + k + 1 : at + TOP].reshape((TOP - 1 - k) * B, B)
            update = jnp.dot(below, solved, preferred_element_type=F32)
            base[k + 1 :] = base[k + 1 :] - update.reshape(TOP - 1 - k, B, B)
    for store in stores:
        store.wait()


VMEM = pl.BlockSpec(memory_space=pltpu.VMEM)
SMEM = pl.BlockSpec(memory_space=pltpu.SMEM)
HBM = pl.BlockSpec(memory_space=pl.ANY)
WORK = (
    pltpu.VMEM((PARTS * GROUP, B), F32),
    pltpu.VMEM((4, B, B), F32),
)
ACC_SHAPE = (SUB - FIRST + TOP, B, B)


def cost(blocks, nbytes):
    return pl.CostEstimate(flops=2 * B**3 * blocks, bytes_accessed=nbytes, transcendentals=0)


def run_leaves(codes, rhs, lead):
    return pl.pallas_call(
        leaf_level,
        out_shape=(
            jax.ShapeDtypeStruct((FIRST, B, B), BF16),
            jax.ShapeDtypeStruct(ACC_SHAPE, F32),
        ),
        in_specs=[SMEM, VMEM, VMEM],
        out_specs=(VMEM, VMEM),
        scratch_shapes=[
            *WORK,
            pltpu.VMEM((FIRST, B, B), BF16),
            pltpu.VMEM((2, PARTS * GROUP, B), F32),
        ],
        compiler_params=pltpu.CompilerParams(vmem_limit_bytes=16 << 20),
        cost_estimate=cost(FIRST * (1 + NB), 8 << 20),
    )(codes, rhs, lead)


def run_later(codes, where, rhs, top_rhs, acc, leaf_sol, rest):
    return pl.pallas_call(
        later_levels,
        out_shape=(
            jax.ShapeDtypeStruct((SUB, B, B), BF16),
            jax.ShapeDtypeStruct((TOP, B, B), BF16),
        ),
        in_specs=[SMEM, SMEM] + [VMEM] * 5,
        out_specs=(HBM, VMEM),
        scratch_shapes=[
            pltpu.VMEM(ACC_SHAPE, F32),
            pltpu.VMEM((LATER, B, B), BF16),
            *WORK,
            pltpu.VMEM((LATER_PAD + TOP_BLOCKS, B, B), BF16),
            pltpu.VMEM((2, PARTS * GROUP, B), F32),
            pltpu.VMEM((TOP, B, B), F32),
            pltpu.SemaphoreType.DMA((2,)),
        ],
        compiler_params=pltpu.CompilerParams(vmem_limit_bytes=16 << 20),
        cost_estimate=cost(LATER * (1 + NB) + TOP * (TOP + 1) // 2, 8 << 20),
    )(codes, where, rhs, top_rhs, acc, leaf_sol, rest)


def shift(x, axis, k):
    size = lax.axis_size(axis)
    return lax.ppermute(x, axis, [(n, (n + k) % size) for n in range(size)])


def put(buffer, x, *start):
    start = start + (0,) * (buffer.ndim - len(start))
    shape = (1,) * (buffer.ndim - x.ndim) + x.shape
    return lax.dynamic_update_slice(buffer, x.reshape(shape), start)


def gather_z_then_y(x):
    y, z = lax.axis_index("y"), lax.axis_index("z")
    own = put(jnp.zeros((NZ, *x.shape), x.dtype), x, z)
    right, left = x, x
    for k in range(1, 4):
        right, left = shift(right, "z", 1), shift(left, "z", -1)
        own = put(put(own, right, (z - k) % NZ), left, (z + k) % NZ)
    own = put(own, shift(right, "z", 1), (z + 4) % NZ)
    half = NZ // 2
    every = put(jnp.zeros((NY, *own.shape), x.dtype), own, y)
    right, left = shift(own, "y", 1), shift(own, "y", -1)
    every = put(put(every, right, (y - 1) % NY), left, (y + 1) % NY)
    every = put(every, shift(right[:half], "y", 1)[None], (y + 2) % NY)
    every = put(every, shift(left[half:], "y", -1)[None], (y + 2) % NY, half)
    return every.reshape(PARTS, *x.shape)


def gather_y_then_z(x):
    y, z = lax.axis_index("y"), lax.axis_index("z")
    own = put(jnp.zeros((NY, *x.shape), x.dtype), x, y)
    for k in (1, -1, 2):
        own = put(own, shift(x, "y", k), (y - k) % NY)
    half = NY // 2
    every = put(jnp.zeros((NY, NZ, *x.shape), x.dtype), own[:, None], 0, z)
    right, left = own, own
    for k in range(1, 4):
        right, left = shift(right, "z", 1), shift(left, "z", -1)
        every = put(put(every, right[:, None], 0, (z - k) % NZ), left[:, None], 0, (z + k) % NZ)
    every = put(every, shift(right[:half], "z", 1)[:, None], 0, (z + 4) % NZ)
    every = put(every, shift(left[half:], "z", -1)[:, None], half, (z + 4) % NZ)
    return every.reshape(PARTS, *x.shape)


def gather_row(x):
    chip = lax.axis_index("x")
    pair = lax.all_gather(x, "core", axis=0)
    every = put(jnp.zeros((lax.axis_size("x"), *pair.shape), x.dtype), pair, chip)
    for k in (1, -1, 2):
        every = put(every, shift(pair, "x", k), (chip - k) % lax.axis_size("x"))
    return every.reshape(TOP, *x.shape)


def local(local_rhs, top_rhs, diag_inv, top_inv, off_blocks, top_factor, targets):
    position = lax.axis_index(ROW)
    diag, off = diag_inv.reshape(-1, B), off_blocks.reshape(-1, B)
    own = (jnp.arange(TOP) == position)[:, None, None]
    top_all = gather_row(jnp.where(own, top_inv, top_factor[0]))
    top_rows = jnp.concatenate([top_all[LOW[k] :, k] for k in range(TOP)], axis=0)
    lead = jnp.concatenate([diag[: FIRST * ROWS], off[: FIRST * GROUP]], axis=0)
    rest = jnp.concatenate(
        [
            diag[FIRST * ROWS :],
            jnp.zeros(((LATER_PAD - LATER) * ROWS, B), BF16),
            off[FIRST * GROUP :],
            top_rows.reshape(-1, B),
        ],
        axis=0,
    )
    lead_all = gather_z_then_y(lead)
    rest_all = gather_y_then_z(rest)
    codes = targets.reshape(-1)
    leaf_sol, acc = run_leaves(codes, local_rhs, lead_all)
    sol, addends = run_later(codes, position[None], local_rhs, top_rhs[0], acc, leaf_sol, rest_all)
    parts = lax.all_to_all(addends, ROW, 0, 0, tiled=True)
    own_top = jnp.sum(parts.astype(F32), axis=0, keepdims=True).astype(BF16)
    return sol, own_top


def solution(mesh):
    mesh = jax.sharding.Mesh(mesh.devices.reshape(4, 2, NY, NZ), (*ROW, *RHS))
    in_specs = (
        P(ROW, None, RHS),
        P(ROW, None, RHS),
        P(ROW, RHS, None),
        P(ROW, RHS, None),
        P(ROW, None, RHS, None),
        P(ROW, None, RHS, None),
        P(ROW, None),
    )
    out_specs = (P(ROW, None, RHS), P(ROW, None, RHS))
    return jax.shard_map(local, mesh=mesh, in_specs=in_specs, out_specs=out_specs, check_vma=False)
```

time: 142 us -> 109 us (0.77)
  Pallas kernels: 33.3 us -> 12.1 us
  blocking collectives: 29.8 us -> 17.9 us
  starting transfers between devices: 30.9 us -> 37.4 us
  local copies, waits for them, and re-layouts: 11.7 us -> 7.44 us
  waiting for transfers between devices: 32.9 us -> 30.9 us
    pallas_call x1, Pallas kernels: 19.1 us -> 7.41 us  [run_later(): pl.pallas_call(later_levels, out_shape=(jax.ShapeDtypeStruct((SUB, B, B),...]
    all_gather x1, blocking collectives: 13.8 us -> 2.43 us  [gather_row(): pair = lax.all_gather(x, 'core', axis=0)]
    pallas_call x1, Pallas kernels: 14.2 us -> 4.74 us  [run_leaves(): pl.pallas_call(leaf_level, out_shape=(jax.ShapeDtypeStruct((FIRST, B, B),...]
    ppermute x22 -> x25, starting transfers between devices: 30.9 us -> 37.4 us  [shift(): return lax.ppermute(x, axis, [(n, (n + k) % size) for n in range(size)])]
    unnamed x45 -> x5, local copies, waits for them, and re-layouts: 4.71 us -> 0.79 us
    slice x8, local copies, waits for them, and re-layouts: 6.47 us -> 3.43 us  [the longest x2 1.68 us: local(): lead = jnp.concatenate([diag[:FIRST * ROWS], off[:FIRST * GROUP]], axis=0)]
    ppermute x22 -> x25, waiting for transfers between devices: 32.9 us -> 30.9 us  [shift(): return lax.ppermute(x, axis, [(n, (n + k) % size) for n in range(size)])]
  transfers between devices with their start and end apart: 22 -> 25, of which waited for: 8 -> 7; matrix products, arithmetic and copies ran while one was open for 5% -> 6% of each run, Pallas kernels for 10% -> 4%
where the time goes in v3:
time: 109 us
  starting transfers between devices  37.4 us (34%)
  waiting for transfers between devices  30.9 us (28%)
  blocking collectives  17.9 us (16%)
  Pallas kernels  12.1 us (11%)
  local copies, waits for them, and re-layouts  7.44 us (7%)
  other arithmetic  1.77 us (2%)
  between operations  1.45 us (1%)
    ppermute x25, starting transfers between devices, shift(): return lax.ppermute(x, axis, [(n, (n + k) % size) for n in range(size)])  37.4 us
    ppermute x25, waiting for transfers between devices, shift(): return lax.ppermute(x, axis, [(n, (n + k) % size) for n in range(size)])  30.9 us
    all_to_all x1, blocking collectives, local(): parts = lax.all_to_all(addends, ROW, 0, 0, tiled=True)  15.5 us
    pallas_call x1, Pallas kernels, run_later(): pl.pallas_call(later_levels, out_shape=(jax.ShapeDtypeStruct((SUB, B, B),...  7.41 us
    pallas_call x1, Pallas kernels, run_leaves(): pl.pallas_call(leaf_level, out_shape=(jax.ShapeDtypeStruct((FIRST, B, B),...  4.74 us
    all_gather x1, blocking collectives, gather_row(): pair = lax.all_gather(x, 'core', axis=0)  2.43 us
  transfers between devices with their start and end apart: 25, of which 7 were waited for; matrix products, arithmetic and copies ran while one was open for 6% of the time, Pallas kernels for 4%

profile of v3, /device:TPU:1, one launch (start us, length us, event | category | flops | bytes accessed | tf_op | source)
XLA Modules:
  0.0 109.0 jit_solution(7343272067721042904)
XLA Ops:
  0.6 0.9 slice.62
  1.6 0.8 slice.60
  2.3 2.5 %collective-permute-start = (bf16[480,128]{1,0:T(8,128)(2,1)S(1)}, bf16[480,128]{1,0:T(8,128)(2,1)S(1)}, u32[]{:S(2)}, u32[]{:S(2)}) collective-permute-start(bf16[480,128]{1,0:T(8,128)(2,1)S(1)} %pad_maximum_fusion.1), channel_id=1, source_target_pairs={{0,1},{1,2},{2,3},{3,4},{4,5},{5,6},{6,7},{7,0},{8,9},{9,10},{10,1... | collective-permute-start | bytes 368648 | tf_op jit(solution)/shard_map/ppermute | solution.py:179
  4.9 4.0 %collective-permute-start.1 = (bf16[480,128]{1,0:T(8,128)(2,1)S(1)}, bf16[480,128]{1,0:T(8,128)(2,1)S(1)}, u32[]{:S(2)}, u32[]{:S(2)}) collective-permute-start(bf16[480,128]{1,0:T(8,128)(2,1)S(1)} %pad_maximum_fusion.1), channel_id=1, source_target_pairs={{0,7},{1,0},{2,1},{3,2},{4,3},{5,4},{6,5},{7,6},{8,15},{9,8},{10,9... | collective-permute-start | bytes 368648 | tf_op jit(solution)/shard_map/ppermute | solution.py:179
  8.9 0.8 copy_select_fusion
  9.7 2.4 %all_gather.4 = bf16[2,8,4,128]{3,1,2,0:T(8,128)(2,1)S(1)} all-gather(bf16[1,8,4,128]{3,1,2,0:T(8,128)(2,1)S(1)} %copy_select_fusion), channel_id=1, replica_groups=mesh['x'=4,'core'=2,'y'=4,'z'=8] {'core'}, dimensions={0}, use_global_device_ids=true | all-gather | bytes 24576 | tf_op jit(solution)/shard_map/all_gather | solution.py:223
  12.1 1.2 %collective-permute-start.11 = (bf16[2,8,4,128]{3,1,2,0:T(8,128)(2,1)S(1)}, bf16[2,8,4,128]{3,1,2,0:T(8,128)(2,1)S(1)}, u32[]{:S(2)}, u32[]{:S(2)}) collective-permute-start(bf16[2,8,4,128]{3,1,2,0:T(8,128)(2,1)S(1)} %all_gather.4), channel_id=1, source_target_pairs={{0,64},{64,128},{128,192},{192,0},{1,65},{65,129},{129,193},{193,1... | collective-permute-start | bytes 49160 | tf_op jit(solution)/shard_map/ppermute | solution.py:179
  13.3 1.5 %collective-permute-start.12 = (bf16[2,8,4,128]{3,1,2,0:T(8,128)(2,1)S(1)}, bf16[2,8,4,128]{3,1,2,0:T(8,128)(2,1)S(1)}, u32[]{:S(2)}, u32[]{:S(2)}) collective-permute-start(bf16[2,8,4,128]{3,1,2,0:T(8,128)(2,1)S(1)} %all_gather.4), channel_id=1, source_target_pairs={{0,192},{64,0},{128,64},{192,128},{1,193},{65,1},{129,65},{193,129... | collective-permute-start | bytes 49160 | tf_op jit(solution)/shard_map/ppermute | solution.py:179
  14.8 1.5 %collective-permute-start.13 = (bf16[2,8,4,128]{3,1,2,0:T(8,128)(2,1)S(1)}, bf16[2,8,4,128]{3,1,2,0:T(8,128)(2,1)S(1)}, u32[]{:S(2)}, u32[]{:S(2)}) collective-permute-start(bf16[2,8,4,128]{3,1,2,0:T(8,128)(2,1)S(1)} %all_gather.4), channel_id=1, source_target_pairs={{0,128},{64,192},{128,0},{192,64},{1,129},{65,193},{129,1},{193,65... | collective-permute-start | bytes 49160 | tf_op jit(solution)/shard_map/ppermute | solution.py:179
  16.4 0.1 broadcast_in_dim.76
  16.7 0.9 slice.68
  17.7 0.7 slice.66
  18.4 0.8 copy.77
  19.2 0.1 reshape.95.codes
  19.4 0.1 pad.1.clone
  19.5 0.0 collective-permute-done.13
  19.7 0.2 concatenate.10
  19.9 0.1 pad_maximum_fusion
  20.0 1.4 %collective-permute-start.14 = (bf16[528,128]{1,0:T(8,128)(2,1)S(1)}, bf16[528,128]{1,0:T(8,128)(2,1)S(1)}, u32[]{:S(2)}, u32[]{:S(2)}) collective-permute-start(bf16[528,128]{1,0:T(8,128)(2,1)S(1)} %pad_maximum_fusion), channel_id=1, source_target_pairs={{0,8},{8,16},{16,24},{24,0},{1,9},{9,17},{17,25},{25,1},{2,10},{10... | collective-permute-start | bytes 405512 | tf_op jit(solution)/shard_map/ppermute | solution.py:179
  21.4 1.5 %collective-permute-start.15 = (bf16[528,128]{1,0:T(8,128)(2,1)S(1)}, bf16[528,128]{1,0:T(8,128)(2,1)S(1)}, u32[]{:S(2)}, u32[]{:S(2)}) collective-permute-start(bf16[528,128]{1,0:T(8,128)(2,1)S(1)} %pad_maximum_fusion), channel_id=1, source_target_pairs={{0,24},{8,0},{16,8},{24,16},{1,25},{9,1},{17,9},{25,17},{2,26},{10... | collective-permute-start | bytes 405512 | tf_op jit(solution)/shard_map/ppermute | solution.py:179
  22.9 1.6 %collective-permute-start.16 = (bf16[528,128]{1,0:T(8,128)(2,1)S(1)}, bf16[528,128]{1,0:T(8,128)(2,1)S(1)}, u32[]{:S(2)}, u32[]{:S(2)}) collective-permute-start(bf16[528,128]{1,0:T(8,128)(2,1)S(1)} %pad_maximum_fusion), channel_id=1, source_target_pairs={{0,16},{8,24},{16,0},{24,8},{1,17},{9,25},{17,1},{25,9},{2,18},{10... | collective-permute-start | bytes 405512 | tf_op jit(solution)/shard_map/ppermute | solution.py:179
  24.5 0.1 broadcast_in_dim.80
  24.5 0.2 bitcast_dynamic-update-slice_fusion.17
  24.7 0.1 collective-permute-start.2
  24.8 2.7 %collective-permute-start.3 = (bf16[480,128]{1,0:T(8,128)(2,1)S(1)}, bf16[480,128]{1,0:T(8,128)(2,1)S(1)}, u32[]{:S(2)}, u32[]{:S(2)}) collective-permute-start(bf16[480,128]{1,0:T(8,128)(2,1)S(1)} %collective-permute-done.1), channel_id=1, source_target_pairs={{0,7},{1,0},{2,1},{3,2},{4,3},{5,4},{6,5},{7,6},{8,15},{9,8},{10,9... | collective-permute-start | bytes 368648 | tf_op jit(solution)/shard_map/ppermute | solution.py:179
  27.6 2.0 %collective-permute-done.16 = bf16[528,128]{1,0:T(8,128)(2,1)S(1)} collective-permute-done((bf16[528,128]{1,0:T(8,128)(2,1)S(1)}, bf16[528,128]{1,0:T(8,128)(2,1)S(1)}, u32[]{:S(2)}, u32[]{:S(2)}) %collective-permute-start.16) | collective-permute-done | bytes 135200 | tf_op jit(solution)/shard_map/ppermute | solution.py:179
  29.7 0.1 collective-permute-start.17
  29.8 2.7 %collective-permute-start.18 = (bf16[4,528,128]{2,1,0:T(8,128)(2,1)S(1)}, bf16[4,528,128]{2,1,0:T(8,128)(2,1)S(1)}, u32[]{:S(2)}, u32[]{:S(2)}) collective-permute-start(bf16[4,528,128]{2,1,0:T(8,128)(2,1)S(1)} %bitcast_dynamic-update-slice_fusion.14), channel_id=1, source_target_pairs={{0,7},{1,0},{2,1},{3,2},{4,3},{5,4},{6,5},{7,6},{8,15},{9,8},{10,9... | collective-permute-start | bytes 1622024 | tf_op jit(solution)/shard_map/ppermute | solution.py:179
  32.4 0.6 broadcast_in_dim.79
  33.0 0.1 bitcast_dynamic-update-slice_fusion.9
  33.1 0.1 collective-permute-start.4
  33.2 2.7 %collective-permute-start.5 = (bf16[480,128]{1,0:T(8,128)(2,1)S(1)}, bf16[480,128]{1,0:T(8,128)(2,1)S(1)}, u32[]{:S(2)}, u32[]{:S(2)}) collective-permute-start(bf16[480,128]{1,0:T(8,128)(2,1)S(1)} %collective-permute-done.3), channel_id=1, source_target_pairs={{0,7},{1,0},{2,1},{3,2},{4,3},{5,4},{6,5},{7,6},{8,15},{9,8},{10,9... | collective-permute-start | bytes 368648 | tf_op jit(solution)/shard_map/ppermute | solution.py:179
  35.9 9.3 %collective-permute-done.4 = bf16[480,128]{1,0:T(8,128)(2,1)S(1)} collective-permute-done((bf16[480,128]{1,0:T(8,128)(2,1)S(1)}, bf16[480,128]{1,0:T(8,128)(2,1)S(1)}, u32[]{:S(2)}, u32[]{:S(2)}) %collective-permute-start.4) | collective-permute-done | bytes 122912 | tf_op jit(solution)/shard_map/ppermute | solution.py:179
  45.2 4.9 %collective-permute-done.6 = bf16[480,128]{1,0:T(8,128)(2,1)S(1)} collective-permute-done((bf16[480,128]{1,0:T(8,128)(2,1)S(1)}, bf16[480,128]{1,0:T(8,128)(2,1)S(1)}, u32[]{:S(2)}, u32[]{:S(2)}) %collective-permute-start.6) | collective-permute-done | bytes 122912 | tf_op jit(solution)/shard_map/ppermute | solution.py:179
  50.1 0.1 collective-permute-start.7
  50.2 2.7 %collective-permute-start.8 = (bf16[8,480,128]{2,1,0:T(8,128)(2,1)S(1)}, bf16[8,480,128]{2,1,0:T(8,128)(2,1)S(1)}, u32[]{:S(2)}, u32[]{:S(2)}) collective-permute-start(bf16[8,480,128]{2,1,0:T(8,128)(2,1)S(1)} %bitcast_dynamic-update-slice_fusion.18), channel_id=1, source_target_pairs={{0,24},{8,0},{16,8},{24,16},{1,25},{9,1},{17,9},{25,17},{2,26},{10... | collective-permute-start | bytes 2949128 | tf_op jit(solution)/shard_map/ppermute | solution.py:179
  52.9 2.7 %collective-permute-start.20 = (bf16[4,528,128]{2,1,0:T(8,128)(2,1)S(1)}, bf16[4,528,128]{2,1,0:T(8,128)(2,1)S(1)}, u32[]{:S(2)}, u32[]{:S(2)}) collective-permute-start(bf16[4,528,128]{2,1,0:T(8,128)(2,1)S(1)} %collective-permute-done.18), channel_id=1, source_target_pairs={{0,7},{1,0},{2,1},{3,2},{4,3},{5,4},{6,5},{7,6},{8,15},{9,8},{10,9... | collective-permute-start | bytes 1622024 | tf_op jit(solution)/shard_map/ppermute | solution.py:179
  55.6 0.6 broadcast_in_dim.75
  56.1 0.1 bitcast_dynamic-update-slice_fusion.2
  56.3 0.1 bitcast_dynamic-update-slice_fusion.8
  56.4 0.1 bitcast_dynamic-update-slice_fusion.7
  56.4 6.6 %collective-permute-done.19 = bf16[4,528,128]{2,1,0:T(8,128)(2,1)S(1)} collective-permute-done((bf16[4,528,128]{2,1,0:T(8,128)(2,1)S(1)}, bf16[4,528,128]{2,1,0:T(8,128)(2,1)S(1)}, u32[]{:S(2)}, u32[]{:S(2)}) %collective-permute-start.19) | collective-permute-done | bytes 540704 | tf_op jit(solution)/shard_map/ppermute | solution.py:179
  63.0 2.7 %collective-permute-start.22 = (bf16[4,528,128]{2,1,0:T(8,128)(2,1)S(1)}, bf16[4,528,128]{2,1,0:T(8,128)(2,1)S(1)}, u32[]{:S(2)}, u32[]{:S(2)}) collective-permute-start(bf16[4,528,128]{2,1,0:T(8,128)(2,1)S(1)} %collective-permute-done.20), channel_id=1, source_target_pairs={{0,7},{1,0},{2,1},{3,2},{4,3},{5,4},{6,5},{7,6},{8,15},{9,8},{10,9... | collective-permute-start | bytes 1622024 | tf_op jit(solution)/shard_map/ppermute | solution.py:179
  65.7 0.1 bitcast_dynamic-update-slice_fusion.6
  65.8 0.1 bitcast_dynamic-update-slice_fusion.5
  65.9 4.5 %collective-permute-done.7 = bf16[8,480,128]{2,1,0:T(8,128)(2,1)S(1)} collective-permute-done((bf16[8,480,128]{2,1,0:T(8,128)(2,1)S(1)}, bf16[8,480,128]{2,1,0:T(8,128)(2,1)S(1)}, u32[]{:S(2)}, u32[]{:S(2)}) %collective-permute-start.7) | collective-permute-done | bytes 983072 | tf_op jit(solution)/shard_map/ppermute | solution.py:179
  70.4 0.1 collective-permute-start.9
  70.6 0.0 copy-start
  70.6 2.7 %collective-permute-start.10 = (bf16[4,480,128]{2,1,0:T(8,128)(2,1)S(1)}, bf16[4,480,128]{2,1,0:T(8,128)(2,1)S(1)}, u32[]{:S(2)}, u32[]{:S(2)}) collective-permute-start(bf16[4,480,128]{2,1,0:T(8,128)(2,1)S(1)} %slice.81), channel_id=1, source_target_pairs={{0,24},{8,0},{16,8},{24,16},{1,25},{9,1},{17,9},{25,17},{2,26},{10... | collective-permute-start | bytes 1474568 | tf_op jit(solution)/shard_map/ppermute | solution.py:179
  73.3 0.1 bitcast_dynamic-update-slice_fusion.1
  73.4 0.1 bitcast_dynamic-update-slice_fusion
  73.6 0.6 collective-permute-done.21
  74.2 0.1 collective-permute-start.23
  74.3 2.9 %collective-permute-start.24 = (bf16[2,528,128]{2,1,0:T(8,128)(2,1)S(1)}, bf16[2,528,128]{2,1,0:T(8,128)(2,1)S(1)}, u32[]{:S(2)}, u32[]{:S(2)}) collective-permute-start(bf16[2,528,128]{2,1,0:T(8,128)(2,1)S(1)} %slice.91), channel_id=1, source_target_pairs={{0,7},{1,0},{2,1},{3,2},{4,3},{5,4},{6,5},{7,6},{8,15},{9,8},{10,9... | collective-permute-start | bytes 811016 | tf_op jit(solution)/shard_map/ppermute | solution.py:179
  77.3 0.1 bitcast_dynamic-update-slice_fusion.4
  77.4 0.1 bitcast_dynamic-update-slice_fusion.3
  77.4 0.0 copy-start.1
  77.5 3.0 %collective-permute-done.9 = bf16[4,480,128]{2,1,0:T(8,128)(2,1)S(1)} collective-permute-done((bf16[4,480,128]{2,1,0:T(8,128)(2,1)S(1)}, bf16[4,480,128]{2,1,0:T(8,128)(2,1)S(1)}, u32[]{:S(2)}, u32[]{:S(2)}) %collective-permute-start.9) | collective-permute-done | bytes 491552 | tf_op jit(solution)/shard_map/ppermute | solution.py:179
  80.5 0.1 bitcast_dynamic-update-slice_fusion.11
  80.5 0.1 bitcast_dynamic-update-slice_fusion.10
  80.6 4.7 %shard_map.86 = (bf16[24,128,128]{2,1,0:T(8,128)(2,1)S(1)}, f32[26,128,128]{2,1,0:T(8,128)S(1)}) custom-call(s32[168]{0:T(256)S(1)} %reshape.95.codes, bf16[42,128,128]{2,1,0:T(8,128)(2,1)S(1)} %copy-done, bf16[32,480,128]{2,1,0:T(8,128)(2,1)S(1)} %bitcast.105), custom_call_target="tpu_custom_call" | custom-call | flops 503316480 | bytes 8388608 | tf_op jit(solution)/shard_map/pallas_call | solution.py:136
  85.5 7.4 %shard_map.87 = (bf16[42,128,128]{2,1,0:T(8,128)(2,1)}, bf16[8,128,128]{2,1,0:T(8,128)(2,1)S(1)}) custom-call(s32[168]{0:T(256)S(1)} %reshape.95.codes, s32[1]{0:T(128)} %bitcast.where, bf16[42,128,128]{2,1,0:T(8,128)(2,1)S(1)} %copy-done, bf16[128,128]{1,0:T(8,128)(2,1)S(1)} %bitcast.106, f32[26,128,128]{2,1,0:T(8,128)S(1)} %get-tuple-element.6.acc_in, ...), custom_call_target="tpu_custom_call" | custom-call | flops 528482304 | bytes 8388608 | tf_op jit(solution)/shard_map/pallas_call | solution.py:155
  92.9 15.5 %all_to_all.5 = bf16[8,128,128]{2,1,0:T(8,128)(2,1)S(1)} all-to-all(bf16[8,128,128]{2,1,0:T(8,128)(2,1)S(1)} %get-tuple-element.9), channel_id=1, replica_groups=mesh['x'=4,'core'=2,'y'=4,'z'=8] {'x','core'}, dimensions={0} | all-to-all | bytes 524288 | tf_op jit(solution)/shard_map/all_to_all | solution.py:251
  108.4 0.7 reduce_sum.12
  (56 shorter events, 0.7 us)
Async XLA Ops:
  2.3 22.4 %collective-permute-start = (bf16[480,128]{1,0:T(8,128)(2,1)S(1)}, bf16[480,128]{1,0:T(8,128)(2,1)S(1)}, u32[]{:S(2)}, u32[]{:S(2)}) collective-permute-start(bf16[480,128]{1,0:T(8,128)(2,1)S(1)} %pad_maximum_fusion.1), channel_id=1, source_target_pairs={{0,1},{1,2},{2,3},{3,4},{4,5},{5,6},{6,7},{7,0},{8,9},{9,10},{10,1... | collective-permute-start | bytes 368648 | tf_op jit(solution)/shard_map/ppermute | solution.py:179
  4.9 19.9 %collective-permute-start.1 = (bf16[480,128]{1,0:T(8,128)(2,1)S(1)}, bf16[480,128]{1,0:T(8,128)(2,1)S(1)}, u32[]{:S(2)}, u32[]{:S(2)}) collective-permute-start(bf16[480,128]{1,0:T(8,128)(2,1)S(1)} %pad_maximum_fusion.1), channel_id=1, source_target_pairs={{0,7},{1,0},{2,1},{3,2},{4,3},{5,4},{6,5},{7,6},{8,15},{9,8},{10,9... | collective-permute-start | bytes 368648 | tf_op jit(solution)/shard_map/ppermute | solution.py:179
  12.1 7.3 %collective-permute-start.11 = (bf16[2,8,4,128]{3,1,2,0:T(8,128)(2,1)S(1)}, bf16[2,8,4,128]{3,1,2,0:T(8,128)(2,1)S(1)}, u32[]{:S(2)}, u32[]{:S(2)}) collective-permute-start(bf16[2,8,4,128]{3,1,2,0:T(8,128)(2,1)S(1)} %all_gather.4), channel_id=1, source_target_pairs={{0,64},{64,128},{128,192},{192,0},{1,65},{65,129},{129,193},{193,1... | collective-permute-start | bytes 49160 | tf_op jit(solution)/shard_map/ppermute | solution.py:179
  13.3 6.1 %collective-permute-start.12 = (bf16[2,8,4,128]{3,1,2,0:T(8,128)(2,1)S(1)}, bf16[2,8,4,128]{3,1,2,0:T(8,128)(2,1)S(1)}, u32[]{:S(2)}, u32[]{:S(2)}) collective-permute-start(bf16[2,8,4,128]{3,1,2,0:T(8,128)(2,1)S(1)} %all_gather.4), channel_id=1, source_target_pairs={{0,192},{64,0},{128,64},{192,128},{1,193},{65,1},{129,65},{193,129... | collective-permute-start | bytes 49160 | tf_op jit(solution)/shard_map/ppermute | solution.py:179
  14.8 4.7 %collective-permute-start.13 = (bf16[2,8,4,128]{3,1,2,0:T(8,128)(2,1)S(1)}, bf16[2,8,4,128]{3,1,2,0:T(8,128)(2,1)S(1)}, u32[]{:S(2)}, u32[]{:S(2)}) collective-permute-start(bf16[2,8,4,128]{3,1,2,0:T(8,128)(2,1)S(1)} %all_gather.4), channel_id=1, source_target_pairs={{0,128},{64,192},{128,0},{192,64},{1,129},{65,193},{129,1},{193,65... | collective-permute-start | bytes 49160 | tf_op jit(solution)/shard_map/ppermute | solution.py:179
  20.0 7.5 %collective-permute-start.14 = (bf16[528,128]{1,0:T(8,128)(2,1)S(1)}, bf16[528,128]{1,0:T(8,128)(2,1)S(1)}, u32[]{:S(2)}, u32[]{:S(2)}) collective-permute-start(bf16[528,128]{1,0:T(8,128)(2,1)S(1)} %pad_maximum_fusion), channel_id=1, source_target_pairs={{0,8},{8,16},{16,24},{24,0},{1,9},{9,17},{17,25},{25,1},{2,10},{10... | collective-permute-start | bytes 405512 | tf_op jit(solution)/shard_map/ppermute | solution.py:179
  21.4 6.2 %collective-permute-start.15 = (bf16[528,128]{1,0:T(8,128)(2,1)S(1)}, bf16[528,128]{1,0:T(8,128)(2,1)S(1)}, u32[]{:S(2)}, u32[]{:S(2)}) collective-permute-start(bf16[528,128]{1,0:T(8,128)(2,1)S(1)} %pad_maximum_fusion), channel_id=1, source_target_pairs={{0,24},{8,0},{16,8},{24,16},{1,25},{9,1},{17,9},{25,17},{2,26},{10... | collective-permute-start | bytes 405512 | tf_op jit(solution)/shard_map/ppermute | solution.py:179
  22.9 6.7 %collective-permute-start.16 = (bf16[528,128]{1,0:T(8,128)(2,1)S(1)}, bf16[528,128]{1,0:T(8,128)(2,1)S(1)}, u32[]{:S(2)}, u32[]{:S(2)}) collective-permute-start(bf16[528,128]{1,0:T(8,128)(2,1)S(1)} %pad_maximum_fusion), channel_id=1, source_target_pairs={{0,16},{8,24},{16,0},{24,8},{1,17},{9,25},{17,1},{25,9},{2,18},{10... | collective-permute-start | bytes 405512 | tf_op jit(solution)/shard_map/ppermute | solution.py:179
  24.7 8.4 %collective-permute-start.2 = (bf16[480,128]{1,0:T(8,128)(2,1)S(1)}, bf16[480,128]{1,0:T(8,128)(2,1)S(1)}, u32[]{:S(2)}, u32[]{:S(2)}) collective-permute-start(bf16[480,128]{1,0:T(8,128)(2,1)S(1)} %collective-permute-done), channel_id=1, source_target_pairs={{0,1},{1,2},{2,3},{3,4},{4,5},{5,6},{6,7},{7,0},{8,9},{9,10},{10,1... | collective-permute-start | bytes 368648 | tf_op jit(solution)/shard_map/ppermute | solution.py:179
  24.8 8.4 %collective-permute-start.3 = (bf16[480,128]{1,0:T(8,128)(2,1)S(1)}, bf16[480,128]{1,0:T(8,128)(2,1)S(1)}, u32[]{:S(2)}, u32[]{:S(2)}) collective-permute-start(bf16[480,128]{1,0:T(8,128)(2,1)S(1)} %collective-permute-done.1), channel_id=1, source_target_pairs={{0,7},{1,0},{2,1},{3,2},{4,3},{5,4},{6,5},{7,6},{8,15},{9,8},{10,9... | collective-permute-start | bytes 368648 | tf_op jit(solution)/shard_map/ppermute | solution.py:179
  29.7 23.2 %collective-permute-start.17 = (bf16[4,528,128]{2,1,0:T(8,128)(2,1)S(1)}, bf16[4,528,128]{2,1,0:T(8,128)(2,1)S(1)}, u32[]{:S(2)}, u32[]{:S(2)}) collective-permute-start(bf16[4,528,128]{2,1,0:T(8,128)(2,1)S(1)} %bitcast_dynamic-update-slice_fusion.14), channel_id=1, source_target_pairs={{0,1},{1,2},{2,3},{3,4},{4,5},{5,6},{6,7},{7,0},{8,9},{9,10},{10,1... | collective-permute-start | bytes 1622024 | tf_op jit(solution)/shard_map/ppermute | solution.py:179
  29.8 23.1 %collective-permute-start.18 = (bf16[4,528,128]{2,1,0:T(8,128)(2,1)S(1)}, bf16[4,528,128]{2,1,0:T(8,128)(2,1)S(1)}, u32[]{:S(2)}, u32[]{:S(2)}) collective-permute-start(bf16[4,528,128]{2,1,0:T(8,128)(2,1)S(1)} %bitcast_dynamic-update-slice_fusion.14), channel_id=1, source_target_pairs={{0,7},{1,0},{2,1},{3,2},{4,3},{5,4},{6,5},{7,6},{8,15},{9,8},{10,9... | collective-permute-start | bytes 1622024 | tf_op jit(solution)/shard_map/ppermute | solution.py:179
  33.1 12.1 %collective-permute-start.4 = (bf16[480,128]{1,0:T(8,128)(2,1)S(1)}, bf16[480,128]{1,0:T(8,128)(2,1)S(1)}, u32[]{:S(2)}, u32[]{:S(2)}) collective-permute-start(bf16[480,128]{1,0:T(8,128)(2,1)S(1)} %collective-permute-done.2), channel_id=1, source_target_pairs={{0,1},{1,2},{2,3},{3,4},{4,5},{5,6},{6,7},{7,0},{8,9},{9,10},{10,1... | collective-permute-start | bytes 368648 | tf_op jit(solution)/shard_map/ppermute | solution.py:179
  33.2 12.0 %collective-permute-start.5 = (bf16[480,128]{1,0:T(8,128)(2,1)S(1)}, bf16[480,128]{1,0:T(8,128)(2,1)S(1)}, u32[]{:S(2)}, u32[]{:S(2)}) collective-permute-start(bf16[480,128]{1,0:T(8,128)(2,1)S(1)} %collective-permute-done.3), channel_id=1, source_target_pairs={{0,7},{1,0},{2,1},{3,2},{4,3},{5,4},{6,5},{7,6},{8,15},{9,8},{10,9... | collective-permute-start | bytes 368648 | tf_op jit(solution)/shard_map/ppermute | solution.py:179
  45.2 4.9 %collective-permute-start.6 = (bf16[480,128]{1,0:T(8,128)(2,1)S(1)}, bf16[480,128]{1,0:T(8,128)(2,1)S(1)}, u32[]{:S(2)}, u32[]{:S(2)}) collective-permute-start(bf16[480,128]{1,0:T(8,128)(2,1)S(1)} %collective-permute-done.4), channel_id=1, source_target_pairs={{0,1},{1,2},{2,3},{3,4},{4,5},{5,6},{6,7},{7,0},{8,9},{9,10},{10,1... | collective-permute-start | bytes 368648 | tf_op jit(solution)/shard_map/ppermute | solution.py:179
  50.1 20.3 %collective-permute-start.7 = (bf16[8,480,128]{2,1,0:T(8,128)(2,1)S(1)}, bf16[8,480,128]{2,1,0:T(8,128)(2,1)S(1)}, u32[]{:S(2)}, u32[]{:S(2)}) collective-permute-start(bf16[8,480,128]{2,1,0:T(8,128)(2,1)S(1)} %bitcast_dynamic-update-slice_fusion.18), channel_id=1, source_target_pairs={{0,8},{8,16},{16,24},{24,0},{1,9},{9,17},{17,25},{25,1},{2,10},{10... | collective-permute-start | bytes 2949128 | tf_op jit(solution)/shard_map/ppermute | solution.py:179
  50.2 20.3 %collective-permute-start.8 = (bf16[8,480,128]{2,1,0:T(8,128)(2,1)S(1)}, bf16[8,480,128]{2,1,0:T(8,128)(2,1)S(1)}, u32[]{:S(2)}, u32[]{:S(2)}) collective-permute-start(bf16[8,480,128]{2,1,0:T(8,128)(2,1)S(1)} %bitcast_dynamic-update-slice_fusion.18), channel_id=1, source_target_pairs={{0,24},{8,0},{16,8},{24,16},{1,25},{9,1},{17,9},{25,17},{2,26},{10... | collective-permute-start | bytes 2949128 | tf_op jit(solution)/shard_map/ppermute | solution.py:179
  52.9 10.1 %collective-permute-start.19 = (bf16[4,528,128]{2,1,0:T(8,128)(2,1)S(1)}, bf16[4,528,128]{2,1,0:T(8,128)(2,1)S(1)}, u32[]{:S(2)}, u32[]{:S(2)}) collective-permute-start(bf16[4,528,128]{2,1,0:T(8,128)(2,1)S(1)} %collective-permute-done.17), channel_id=1, source_target_pairs={{0,1},{1,2},{2,3},{3,4},{4,5},{5,6},{6,7},{7,0},{8,9},{9,10},{10,1... | collective-permute-start | bytes 1622024 | tf_op jit(solution)/shard_map/ppermute | solution.py:179
  52.9 10.1 %collective-permute-start.20 = (bf16[4,528,128]{2,1,0:T(8,128)(2,1)S(1)}, bf16[4,528,128]{2,1,0:T(8,128)(2,1)S(1)}, u32[]{:S(2)}, u32[]{:S(2)}) collective-permute-start(bf16[4,528,128]{2,1,0:T(8,128)(2,1)S(1)} %collective-permute-done.18), channel_id=1, source_target_pairs={{0,7},{1,0},{2,1},{3,2},{4,3},{5,4},{6,5},{7,6},{8,15},{9,8},{10,9... | collective-permute-start | bytes 1622024 | tf_op jit(solution)/shard_map/ppermute | solution.py:179
  63.0 11.2 %collective-permute-start.21 = (bf16[4,528,128]{2,1,0:T(8,128)(2,1)S(1)}, bf16[4,528,128]{2,1,0:T(8,128)(2,1)S(1)}, u32[]{:S(2)}, u32[]{:S(2)}) collective-permute-start(bf16[4,528,128]{2,1,0:T(8,128)(2,1)S(1)} %collective-permute-done.19), channel_id=1, source_target_pairs={{0,1},{1,2},{2,3},{3,4},{4,5},{5,6},{6,7},{7,0},{8,9},{9,10},{10,1... | collective-permute-start | bytes 1622024 | tf_op jit(solution)/shard_map/ppermute | solution.py:179
  63.0 11.3 %collective-permute-start.22 = (bf16[4,528,128]{2,1,0:T(8,128)(2,1)S(1)}, bf16[4,528,128]{2,1,0:T(8,128)(2,1)S(1)}, u32[]{:S(2)}, u32[]{:S(2)}) collective-permute-start(bf16[4,528,128]{2,1,0:T(8,128)(2,1)S(1)} %collective-permute-done.20), channel_id=1, source_target_pairs={{0,7},{1,0},{2,1},{3,2},{4,3},{5,4},{6,5},{7,6},{8,15},{9,8},{10,9... | collective-permute-start | bytes 1622024 | tf_op jit(solution)/shard_map/ppermute | solution.py:179
  70.4 10.0 %collective-permute-start.9 = (bf16[4,480,128]{2,1,0:T(8,128)(2,1)S(1)}, bf16[4,480,128]{2,1,0:T(8,128)(2,1)S(1)}, u32[]{:S(2)}, u32[]{:S(2)}) collective-permute-start(bf16[4,480,128]{2,1,0:T(8,128)(2,1)S(1)} %slice.80), channel_id=1, source_target_pairs={{0,8},{8,16},{16,24},{24,0},{1,9},{9,17},{17,25},{25,1},{2,10},{10... | collective-permute-start | bytes 1474568 | tf_op jit(solution)/shard_map/ppermute | solution.py:179
  70.6 10.1 %copy-start = (bf16[42,128,128]{2,1,0:T(8,128)(2,1)S(1)}, bf16[42,128,128]{2,1,0:T(8,128)(2,1)}, u32[]{:S(2)}) copy-start(bf16[42,128,128]{2,1,0:T(8,128)(2,1)} %rhs.3) | copy-start | bytes 4128772
  70.6 10.0 %collective-permute-start.10 = (bf16[4,480,128]{2,1,0:T(8,128)(2,1)S(1)}, bf16[4,480,128]{2,1,0:T(8,128)(2,1)S(1)}, u32[]{:S(2)}, u32[]{:S(2)}) collective-permute-start(bf16[4,480,128]{2,1,0:T(8,128)(2,1)S(1)} %slice.81), channel_id=1, source_target_pairs={{0,24},{8,0},{16,8},{24,16},{1,25},{9,1},{17,9},{25,17},{2,26},{10... | collective-permute-start | bytes 1474568 | tf_op jit(solution)/shard_map/ppermute | solution.py:179
  74.2 11.2 %collective-permute-start.23 = (bf16[2,528,128]{2,1,0:T(8,128)(2,1)S(1)}, bf16[2,528,128]{2,1,0:T(8,128)(2,1)S(1)}, u32[]{:S(2)}, u32[]{:S(2)}) collective-permute-start(bf16[2,528,128]{2,1,0:T(8,128)(2,1)S(1)} %slice.90), channel_id=1, source_target_pairs={{0,1},{1,2},{2,3},{3,4},{4,5},{5,6},{6,7},{7,0},{8,9},{9,10},{10,1... | collective-permute-start | bytes 811016 | tf_op jit(solution)/shard_map/ppermute | solution.py:179
  74.3 11.1 %collective-permute-start.24 = (bf16[2,528,128]{2,1,0:T(8,128)(2,1)S(1)}, bf16[2,528,128]{2,1,0:T(8,128)(2,1)S(1)}, u32[]{:S(2)}, u32[]{:S(2)}) collective-permute-start(bf16[2,528,128]{2,1,0:T(8,128)(2,1)S(1)} %slice.91), channel_id=1, source_target_pairs={{0,7},{1,0},{2,1},{3,2},{4,3},{5,4},{6,5},{7,6},{8,15},{9,8},{10,9... | collective-permute-start | bytes 811016 | tf_op jit(solution)/shard_map/ppermute | solution.py:179
  77.4 8.1 %copy-start.1 = (bf16[1,128,128]{2,1,0:T(8,128)(2,1)S(1)}, bf16[1,128,128]{2,1,0:T(8,128)(2,1)}, u32[]{:S(2)}) copy-start(bf16[1,128,128]{2,1,0:T(8,128)(2,1)} %param.8) | copy-start | bytes 98308

commit v4 on v3

--- a/solution.py
+++ b/solution.py
@@ -16,14 +16,15 @@
 FIRST = LEVELS[0][1]
 LATER = SUB - FIRST
 LATER_PAD = -(-LATER // 4) * 4
-LOW = tuple(k - k % 2 for k in range(TOP))
-START = tuple(sum(TOP - LOW[q] for q in range(k)) for k in range(TOP))
-TOP_BLOCKS = sum(TOP - low for low in LOW)
+WIDTH = tuple(t - t % 2 + 2 for t in range(TOP))
+START = tuple(sum(WIDTH[:t]) for t in range(TOP))
+TOP_BLOCKS = sum(WIDTH)
 LEAD_ROWS = FIRST * (1 + NB) * ROWS
-REST_ROWS = (LATER_PAD + LATER * NB + TOP_BLOCKS) * ROWS
-TOP_ROW = (LATER_PAD + LATER * NB) * ROWS
-NY, NZ = 4, 8
+REST_ROWS = (LATER_PAD + LATER * NB) * ROWS
+TOP_ROWS = TOP * ROWS
 ROW, RHS = ("x", "core"), ("y", "z")
+NX, NY, NZ = 4, 4, 8
+HI, LO = 2, 4
 F32 = jnp.float32
 BF16 = jnp.bfloat16
 
@@ -83,7 +84,7 @@
 
 
 def later_levels(
-    codes, where, rhs, top_rhs, acc_in, leaf_sol, rest,
+    codes, where, rhs, top_rhs, acc_in, leaf_sol, rest, top,
     sol_hbm, part, acc, sol, stage, natural, weights, product, base, sems,
 ):
     stores = (
@@ -93,7 +94,7 @@
     stores[0].start()
     acc[...] = acc_in[...]
     collect(rest, stage, natural, weights, 0, 0, LATER_PAD // 4)
-    collect(rest, stage, natural, weights, TOP_ROW, LATER_PAD, TOP_BLOCKS // 4)
+    collect(top, stage, natural, weights, 0, LATER_PAD, TOP_BLOCKS // 4)
     for first, end in LEVELS[1:]:
         off_row = LATER_PAD * ROWS + (first - FIRST) * GROUP
         solve_level(
@@ -106,14 +107,12 @@
         own = jnp.where(where[0] == t, top_rhs[...].astype(F32), 0.0)
         base[t] = own - summed(acc, natural, SUB - FIRST + t)
     for k in range(TOP):
-        at = LATER_PAD + START[k] - LOW[k]
-        solved = jnp.dot(weights[at + k], base[k].astype(BF16), preferred_element_type=F32)
+        at = LATER_PAD + k
+        solved = jnp.dot(weights[at + START[k]], base[k].astype(BF16), preferred_element_type=F32)
         solved = solved.astype(BF16)
         part[k] = solved
-        if k + 1 < TOP:
-            below = weights[at + k + 1 : at + TOP].reshape((TOP - 1 - k) * B, B)
-            update = jnp.dot(below, solved, preferred_element_type=F32)
-            base[k + 1 :] = base[k + 1 :] - update.reshape(TOP - 1 - k, B, B)
+        for t in range(k + 1, TOP):
+            base[t] -= jnp.dot(weights[at + START[t]], solved, preferred_element_type=F32)
     for store in stores:
         store.wait()
 
@@ -151,14 +150,14 @@
     )(codes, rhs, lead)
 
 
-def run_later(codes, where, rhs, top_rhs, acc, leaf_sol, rest):
+def run_later(codes, where, rhs, top_rhs, acc, leaf_sol, rest, top):
     return pl.pallas_call(
         later_levels,
         out_shape=(
             jax.ShapeDtypeStruct((SUB, B, B), BF16),
             jax.ShapeDtypeStruct((TOP, B, B), BF16),
         ),
-        in_specs=[SMEM, SMEM] + [VMEM] * 5,
+        in_specs=[SMEM, SMEM] + [VMEM] * 6,
         out_specs=(HBM, VMEM),
         scratch_shapes=[
             pltpu.VMEM(ACC_SHAPE, F32),
@@ -171,7 +170,7 @@
         ],
         compiler_params=pltpu.CompilerParams(vmem_limit_bytes=16 << 20),
         cost_estimate=cost(LATER * (1 + NB) + TOP * (TOP + 1) // 2, 8 << 20),
-    )(codes, where, rhs, top_rhs, acc, leaf_sol, rest)
+    )(codes, where, rhs, top_rhs, acc, leaf_sol, rest, top)
 
 
 def shift(x, axis, k):
@@ -180,81 +179,102 @@
 
 
 def put(buffer, x, *start):
-    start = start + (0,) * (buffer.ndim - len(start))
-    shape = (1,) * (buffer.ndim - x.ndim) + x.shape
-    return lax.dynamic_update_slice(buffer, x.reshape(shape), start)
-
-
-def gather_z_then_y(x):
-    y, z = lax.axis_index("y"), lax.axis_index("z")
-    own = put(jnp.zeros((NZ, *x.shape), x.dtype), x, z)
-    right, left = x, x
-    for k in range(1, 4):
-        right, left = shift(right, "z", 1), shift(left, "z", -1)
-        own = put(put(own, right, (z - k) % NZ), left, (z + k) % NZ)
-    own = put(own, shift(right, "z", 1), (z + 4) % NZ)
-    half = NZ // 2
-    every = put(jnp.zeros((NY, *own.shape), x.dtype), own, y)
+    return lax.dynamic_update_slice(buffer, x, start + (0,) * (buffer.ndim - len(start)))
+
+
+def gather(rows, top):
+    chip, y, z = lax.axis_index("x"), lax.axis_index("y"), lax.axis_index("z")
+    hi, lo = z // LO, z % LO
+    packed = jnp.concatenate([rows, top], axis=0)
+    other = shift(packed, "z", LO)
+    pair = put(put(jnp.zeros((HI, *packed.shape), BF16), packed[None], hi), other[None], 1 - hi)
+    lead, late = pair[:, :LEAD_ROWS], pair[:, LEAD_ROWS:]
+
+    right, left = shift(lead, "z", 1), shift(lead, "z", -1)
+    far_low, far_high = shift(right[:1], "z", 1), shift(left[1:], "z", -1)
+    own = jnp.zeros((HI, LO, LEAD_ROWS, B), BF16)
+    own = put(own, lead[:, None], 0, lo)
+    own = put(own, right[:, None], 0, (lo - 1) % LO)
+    own = put(own, left[:, None], 0, (lo + 1) % LO)
+    own = put(own, far_low[:, None], 0, (lo + 2) % LO)
+    own = put(own, far_high[:, None], 1, (lo + 2) % LO)
+
+    late_all = put(jnp.zeros((NY, *late.shape), BF16), late[None], y)
+    for k in (1, -1, 2):
+        late_all = put(late_all, shift(late, "y", k)[None], (y - k) % NY)
+    rest, top = late_all[:, :, :REST_ROWS], late_all[:, :, REST_ROWS:]
+    rest_right, rest_left = shift(rest, "z", 1), shift(rest, "z", -1)
+
     right, left = shift(own, "y", 1), shift(own, "y", -1)
-    every = put(put(every, right, (y - 1) % NY), left, (y + 1) % NY)
-    every = put(every, shift(right[:half], "y", 1)[None], (y + 2) % NY)
-    every = put(every, shift(left[half:], "y", -1)[None], (y + 2) % NY, half)
-    return every.reshape(PARTS, *x.shape)
-
-
-def gather_y_then_z(x):
-    y, z = lax.axis_index("y"), lax.axis_index("z")
-    own = put(jnp.zeros((NY, *x.shape), x.dtype), x, y)
+
+    cores = lax.all_gather(top, "core", axis=0)
+    chips = put(jnp.zeros((NX, *cores.shape), BF16), cores[None], chip)
     for k in (1, -1, 2):
-        own = put(own, shift(x, "y", k), (y - k) % NY)
-    half = NY // 2
-    every = put(jnp.zeros((NY, NZ, *x.shape), x.dtype), own[:, None], 0, z)
-    right, left = own, own
-    for k in range(1, 4):
-        right, left = shift(right, "z", 1), shift(left, "z", -1)
-        every = put(put(every, right[:, None], 0, (z - k) % NZ), left[:, None], 0, (z + k) % NZ)
-    every = put(every, shift(right[:half], "z", 1)[:, None], 0, (z + 4) % NZ)
-    every = put(every, shift(left[half:], "z", -1)[:, None], half, (z + 4) % NZ)
-    return every.reshape(PARTS, *x.shape)
-
-
-def gather_row(x):
-    chip = lax.axis_index("x")
-    pair = lax.all_gather(x, "core", axis=0)
-    every = put(jnp.zeros((lax.axis_size("x"), *pair.shape), x.dtype), pair, chip)
-    for k in (1, -1, 2):
-        every = put(every, shift(pair, "x", k), (chip - k) % lax.axis_size("x"))
-    return every.reshape(TOP, *x.shape)
+        chips = put(chips, shift(cores, "x", k)[None], (chip - k) % NX)
+    chips = chips.reshape(TOP, NY, HI, TOP_ROWS, B)
+    top = jnp.concatenate([chips[t, :, :, : WIDTH[t] * ROWS] for t in range(TOP)], axis=2)
+
+    split = NY * REST_ROWS
+    flat_top = top.reshape(-1, B)
+    next_right = jnp.concatenate([rest_right[:, 0].reshape(-1, B), flat_top], axis=0)
+    next_left = jnp.concatenate([rest_left[:, 1].reshape(-1, B), flat_top], axis=0)
+    next_right, next_left = shift(next_right, "z", 1), shift(next_left, "z", -1)
+    rest_low = next_right[:split].reshape(NY, 1, REST_ROWS, B)
+    rest_high = next_left[:split].reshape(NY, 1, REST_ROWS, B)
+    top_right, top_left = next_right[split:].reshape(top.shape), next_left[split:].reshape(top.shape)
+
+    far_low, far_high = shift(right[:1], "y", 1), shift(left[1:], "y", -1)
+    lead_all = put(jnp.zeros((NY, *own.shape), BF16), own[None], y)
+    lead_all = put(lead_all, right[None], (y - 1) % NY)
+    lead_all = put(lead_all, left[None], (y + 1) % NY)
+    lead_all = put(lead_all, far_low[None], (y + 2) % NY)
+    lead_all = put(lead_all, far_high[None], (y + 2) % NY, 1)
+
+    top_low, top_high = shift(top_right[:, :1], "z", 1), shift(top_left[:, 1:], "z", -1)
+
+    def join(own, right, left, low, high):
+        every = jnp.zeros((NY, HI, LO, own.shape[2], B), BF16)
+        every = put(every, own[:, :, None], 0, 0, lo)
+        every = put(every, right[:, :, None], 0, 0, (lo - 1) % LO)
+        every = put(every, left[:, :, None], 0, 0, (lo + 1) % LO)
+        every = put(every, low[:, :, None], 0, 0, (lo + 2) % LO)
+        every = put(every, high[:, :, None], 0, 1, (lo + 2) % LO)
+        return every.reshape(PARTS, own.shape[2], B)
+
+    rest_all = join(rest, rest_right, rest_left, rest_low, rest_high)
+    top_all = join(top, top_right, top_left, top_low, top_high)
+    return lead_all.reshape(PARTS, LEAD_ROWS, B), rest_all, top_all
 
 
 def local(local_rhs, top_rhs, diag_inv, top_inv, off_blocks, top_factor, targets):
     position = lax.axis_index(ROW)
     diag, off = diag_inv.reshape(-1, B), off_blocks.reshape(-1, B)
     own = (jnp.arange(TOP) == position)[:, None, None]
-    top_all = gather_row(jnp.where(own, top_inv, top_factor[0]))
-    top_rows = jnp.concatenate([top_all[LOW[k] :, k] for k in range(TOP)], axis=0)
-    lead = jnp.concatenate([diag[: FIRST * ROWS], off[: FIRST * GROUP]], axis=0)
-    rest = jnp.concatenate(
+    top_rows = jnp.where(own, top_inv, top_factor[0]).reshape(-1, B)
+    pad = jnp.zeros(((LATER_PAD - LATER) * ROWS, B), BF16)
+    rows = jnp.concatenate(
         [
+            diag[: FIRST * ROWS],
+            off[: FIRST * GROUP],
             diag[FIRST * ROWS :],
-            jnp.zeros(((LATER_PAD - LATER) * ROWS, B), BF16),
+            pad,
             off[FIRST * GROUP :],
-            top_rows.reshape(-1, B),
         ],
         axis=0,
     )
-    lead_all = gather_z_then_y(lead)
-    rest_all = gather_y_then_z(rest)
+    lead_all, rest_all, top_all = gather(rows, top_rows)
     codes = targets.reshape(-1)
     leaf_sol, acc = run_leaves(codes, local_rhs, lead_all)
-    sol, addends = run_later(codes, position[None], local_rhs, top_rhs[0], acc, leaf_sol, rest_all)
+    sol, addends = run_later(
+        codes, position[None], local_rhs, top_rhs[0], acc, leaf_sol, rest_all, top_all
+    )
     parts = lax.all_to_all(addends, ROW, 0, 0, tiled=True)
     own_top = jnp.sum(parts.astype(F32), axis=0, keepdims=True).astype(BF16)
     return sol, own_top
 
 
 def solution(mesh):
-    mesh = jax.sharding.Mesh(mesh.devices.reshape(4, 2, NY, NZ), (*ROW, *RHS))
+    mesh = jax.sharding.Mesh(mesh.devices.reshape(NX, 2, NY, NZ), (*ROW, *RHS))
     in_specs = (
         P(ROW, None, RHS),
         P(ROW, None, RHS),

time: 109 us -> 121 us (1.11)
  waiting for transfers between devices: 30.9 us -> 35.5 us
  starting transfers between devices: 37.4 us -> 41.6 us
  blocking collectives: 17.9 us -> 19.3 us
  local copies, waits for them, and re-layouts: 7.44 us -> 8.76 us
    ppermute x25 -> x21, waiting for transfers between devices: 30.9 us -> 35.5 us  [shift(): return lax.ppermute(x, axis, [(n, (n + k) % size) for n in range(size)])]
    ppermute x25 -> x21, starting transfers between devices: 37.4 us -> 41.6 us  [shift(): return lax.ppermute(x, axis, [(n, (n + k) % size) for n in range(size)])]
    all_gather x1, blocking collectives: 2.43 us -> 3.99 us  [gather(): cores = lax.all_gather(top, 'core', axis=0)]
    broadcast_in_dim x6 -> x10, local copies, waits for them, and re-layouts: 1.34 us -> 2.48 us  [the longest x3 0.85 us: local(): top_rows = jnp.where(own, top_inv, top_factor[0]).reshape(-1, B)]
  transfers between devices with their start and end apart: 25 -> 21, of which waited for: 7 -> 10; matrix products, arithmetic and copies ran while one was open for 6% -> 4% of each run, Pallas kernels for 4% -> 0%
where the time goes in v4:
time: 121 us; the launch traced here: 120 us
  starting transfers between devices  41.6 us (34%)
  waiting for transfers between devices  35.5 us (29%)
  blocking collectives  19.3 us (16%)
  Pallas kernels  12.3 us (10%)
  local copies, waits for them, and re-layouts  8.76 us (7%)
  other arithmetic  1.53 us (1%)
  between operations  1.33 us (1%)
    ppermute x21, starting transfers between devices, shift(): return lax.ppermute(x, axis, [(n, (n + k) % size) for n in range(size)])  41.6 us
    ppermute x21, waiting for transfers between devices, shift(): return lax.ppermute(x, axis, [(n, (n + k) % size) for n in range(size)])  35.5 us
    all_to_all x1, blocking collectives, local(): parts = lax.all_to_all(addends, ROW, 0, 0, tiled=True)  15.3 us
    pallas_call x1, Pallas kernels, run_later(): pl.pallas_call(later_levels, out_shape=(jax.ShapeDtypeStruct((SUB, B, B),...  7.5 us
    pallas_call x1, Pallas kernels, run_leaves(): pl.pallas_call(leaf_level, out_shape=(jax.ShapeDtypeStruct((FIRST, B, B),...  4.84 us
    all_gather x1, blocking collectives, gather(): cores = lax.all_gather(top, 'core', axis=0)  3.99 us
  transfers between devices with their start and end apart: 21, of which 10 were waited for; matrix products, arithmetic and copies ran while one was open for 4% of the time, Pallas kernels for 0%

profile of v4, /device:TPU:1, one launch (start us, length us, event | category | flops | bytes accessed | tf_op | source)
XLA Modules:
  0.0 120.2 jit_solution(2033118225895605116)
XLA Ops:
  0.6 0.8 slice.96
  1.4 0.7 slice.100
  2.1 0.9 slice.98
  3.0 0.9 slice.102
  4.1 0.1 broadcast_in_dim.136
  4.1 0.1 broadcast_in_dim.137
  4.2 0.7 broadcast_in_dim.140
  4.9 0.8 constant_dynamic-update-slice_fusion
  5.7 7.8 %collective-permute-start = (bf16[880,128]{1,0:T(8,128)(2,1)S(1)}, bf16[880,128]{1,0:T(8,128)(2,1)S(1)}, u32[]{:S(2)}, u32[]{:S(2)}) collective-permute-start(bf16[880,128]{1,0:T(8,128)(2,1)S(1)} %constant_dynamic-update-slice_fusion), channel_id=1, source_target_pairs={{0,4},{1,5},{2,6},{3,7},{4,0},{5,1},{6,2},{7,3},{8,12},{9,13},{10,... | collective-permute-start | bytes 675848 | tf_op jit(solution)/shard_map/ppermute | solution.py:178
  13.5 0.8 copy.26
  14.2 0.1 reshape.51.codes
  14.4 0.1 broadcast_in_dim.134
  14.5 3.6 %collective-permute-done = bf16[880,128]{1,0:T(8,128)(2,1)S(1)} collective-permute-done((bf16[880,128]{1,0:T(8,128)(2,1)S(1)}, bf16[880,128]{1,0:T(8,128)(2,1)S(1)}, u32[]{:S(2)}, u32[]{:S(2)}) %collective-permute-start) | collective-permute-done | bytes 225312 | tf_op jit(solution)/shard_map/ppermute | solution.py:178
  18.2 4.5 %collective-permute-start.1 = (bf16[2,480,128]{2,1,0:T(8,128)(2,1)S(1)}, bf16[2,480,128]{2,1,0:T(8,128)(2,1)S(1)}, u32[]{:S(2)}, u32[]{:S(2)}) collective-permute-start(bf16[2,480,128]{2,1,0:T(8,128)(2,1)S(1)} %slice.128), channel_id=1, source_target_pairs={{0,1},{1,2},{2,3},{3,4},{4,5},{5,6},{6,7},{7,0},{8,9},{9,10},{10,1... | collective-permute-start | bytes 737288 | tf_op jit(solution)/shard_map/ppermute | solution.py:178
  22.7 3.9 %collective-permute-start.2 = (bf16[2,480,128]{2,1,0:T(8,128)(2,1)S(1)}, bf16[2,480,128]{2,1,0:T(8,128)(2,1)S(1)}, u32[]{:S(2)}, u32[]{:S(2)}) collective-permute-start(bf16[2,480,128]{2,1,0:T(8,128)(2,1)S(1)} %slice.128), channel_id=1, source_target_pairs={{0,7},{1,0},{2,1},{3,2},{4,3},{5,4},{6,5},{7,6},{8,15},{9,8},{10,9... | collective-permute-start | bytes 737288 | tf_op jit(solution)/shard_map/ppermute | solution.py:178
  26.6 1.4 %collective-permute-start.9 = (bf16[2,400,128]{2,1,0:T(8,128)(2,1)S(1)}, bf16[2,400,128]{2,1,0:T(8,128)(2,1)S(1)}, u32[]{:S(2)}, u32[]{:S(2)}) collective-permute-start(bf16[2,400,128]{2,1,0:T(8,128)(2,1)S(1)} %slice.133), channel_id=1, source_target_pairs={{0,8},{8,16},{16,24},{24,0},{1,9},{9,17},{17,25},{25,1},{2,10},{10... | collective-permute-start | bytes 614408 | tf_op jit(solution)/shard_map/ppermute | solution.py:178
  27.9 1.5 %collective-permute-start.10 = (bf16[2,400,128]{2,1,0:T(8,128)(2,1)S(1)}, bf16[2,400,128]{2,1,0:T(8,128)(2,1)S(1)}, u32[]{:S(2)}, u32[]{:S(2)}) collective-permute-start(bf16[2,400,128]{2,1,0:T(8,128)(2,1)S(1)} %slice.133), channel_id=1, source_target_pairs={{0,24},{8,0},{16,8},{24,16},{1,25},{9,1},{17,9},{25,17},{2,26},{10... | collective-permute-start | bytes 614408 | tf_op jit(solution)/shard_map/ppermute | solution.py:178
  29.5 1.6 %collective-permute-start.11 = (bf16[2,400,128]{2,1,0:T(8,128)(2,1)S(1)}, bf16[2,400,128]{2,1,0:T(8,128)(2,1)S(1)}, u32[]{:S(2)}, u32[]{:S(2)}) collective-permute-start(bf16[2,400,128]{2,1,0:T(8,128)(2,1)S(1)} %slice.133), channel_id=1, source_target_pairs={{0,16},{8,24},{16,0},{24,8},{1,17},{9,25},{17,1},{25,9},{2,18},{10... | collective-permute-start | bytes 614408 | tf_op jit(solution)/shard_map/ppermute | solution.py:178
  31.0 0.1 broadcast_in_dim.133
  31.2 0.1 broadcast_in_dim.155
  31.4 2.2 %collective-permute-done.9 = bf16[2,400,128]{2,1,0:T(8,128)(2,1)S(1)} collective-permute-done((bf16[2,400,128]{2,1,0:T(8,128)(2,1)S(1)}, bf16[2,400,128]{2,1,0:T(8,128)(2,1)S(1)}, u32[]{:S(2)}, u32[]{:S(2)}) %collective-permute-start.9) | collective-permute-done | bytes 204832 | tf_op jit(solution)/shard_map/ppermute | solution.py:178
  33.7 5.4 %collective-permute-done.11 = bf16[2,400,128]{2,1,0:T(8,128)(2,1)S(1)} collective-permute-done((bf16[2,400,128]{2,1,0:T(8,128)(2,1)S(1)}, bf16[2,400,128]{2,1,0:T(8,128)(2,1)S(1)}, u32[]{:S(2)}, u32[]{:S(2)}) %collective-permute-start.11) | collective-permute-done | bytes 204832 | tf_op jit(solution)/shard_map/ppermute | solution.py:178
  39.1 0.1 slice.134
  39.2 0.1 collective-permute-start.12
  39.3 2.7 %collective-permute-start.13 = (bf16[4,2,368,128]{3,2,1,0:T(8,128)(2,1)S(1)}, bf16[4,2,368,128]{3,2,1,0:T(8,128)(2,1)S(1)}, u32[]{:S(2)}, u32[]{:S(2)}) collective-permute-start(bf16[4,2,368,128]{3,2,1,0:T(8,128)(2,1)S(1)} %slice.134), channel_id=1, source_target_pairs={{0,7},{1,0},{2,1},{3,2},{4,3},{5,4},{6,5},{7,6},{8,15},{9,8},{10,9... | collective-permute-start | bytes 2261000 | tf_op jit(solution)/shard_map/ppermute | solution.py:178
  41.9 4.0 %all-gather = bf16[8,2,32,128]{3,2,1,0:T(8,128)(2,1)S(1)} all-gather(bf16[4,2,32,128]{3,2,1,0:T(8,128)(2,1)S(1)} %slice.136), channel_id=2, replica_groups=mesh['x'=4,'core'=2,'y'=4,'z'=8] {'core'}, dimensions={0}, use_global_device_ids=true | all-gather | bytes 196608 | tf_op jit(solution)/shard_map/all_gather | solution.py:210
  45.9 1.2 %collective-permute-start.14 = (bf16[2,4,2,32,128]{4,3,2,1,0:T(8,128)(2,1)S(1)}, bf16[2,4,2,32,128]{4,3,2,1,0:T(8,128)(2,1)S(1)}, u32[]{:S(2)}, u32[]{:S(2)}) collective-permute-start(bf16[2,4,2,32,128]{4,3,2,1,0:T(8,128)(2,1)S(1)} %bitcast.152), channel_id=1, source_target_pairs={{0,64},{64,128},{128,192},{192,0},{1,65},{65,129},{129,193},{193,1... | collective-permute-start | bytes 393224 | tf_op jit(solution)/shard_map/ppermute | solution.py:178
  47.1 0.1 broadcast_in_dim.163
  47.3 0.4 broadcast_in_dim.154
  47.7 0.1 bitcast_dynamic-update-slice_fusion.5
  47.8 1.5 %collective-permute-start.15 = (bf16[2,4,2,32,128]{4,3,2,1,0:T(8,128)(2,1)S(1)}, bf16[2,4,2,32,128]{4,3,2,1,0:T(8,128)(2,1)S(1)}, u32[]{:S(2)}, u32[]{:S(2)}) collective-permute-start(bf16[2,4,2,32,128]{4,3,2,1,0:T(8,128)(2,1)S(1)} %bitcast.154), channel_id=1, source_target_pairs={{0,192},{64,0},{128,64},{192,128},{1,193},{65,1},{129,65},{193,129... | collective-permute-start | bytes 393224 | tf_op jit(solution)/shard_map/ppermute | solution.py:178
  49.4 1.6 %collective-permute-start.16 = (bf16[2,4,2,32,128]{4,3,2,1,0:T(8,128)(2,1)S(1)}, bf16[2,4,2,32,128]{4,3,2,1,0:T(8,128)(2,1)S(1)}, u32[]{:S(2)}, u32[]{:S(2)}) collective-permute-start(bf16[2,4,2,32,128]{4,3,2,1,0:T(8,128)(2,1)S(1)} %bitcast.155), channel_id=1, source_target_pairs={{0,128},{64,192},{128,0},{192,64},{1,129},{65,193},{129,1},{193,65... | collective-permute-start | bytes 393224 | tf_op jit(solution)/shard_map/ppermute | solution.py:178
  51.1 0.8 collective-permute-done.14
  51.9 0.4 collective-permute-done.15
  52.3 2.4 %collective-permute-start.4 = (bf16[1,480,128]{2,1,0:T(8,128)(2,1)S(1)}, bf16[1,480,128]{2,1,0:T(8,128)(2,1)S(1)}, u32[]{:S(2)}, u32[]{:S(2)}) collective-permute-start(bf16[1,480,128]{2,1,0:T(8,128)(2,1)S(1)} %slice.130), channel_id=1, source_target_pairs={{0,7},{1,0},{2,1},{3,2},{4,3},{5,4},{6,5},{7,6},{8,15},{9,8},{10,9... | collective-permute-start | bytes 368648 | tf_op jit(solution)/shard_map/ppermute | solution.py:178
  54.7 0.1 collective-permute-done.16
  54.9 0.2 broadcast_in_dim.168
  55.2 4.3 %collective-permute-done.3 = bf16[1,480,128]{2,1,0:T(8,128)(2,1)S(1)} collective-permute-done((bf16[1,480,128]{2,1,0:T(8,128)(2,1)S(1)}, bf16[1,480,128]{2,1,0:T(8,128)(2,1)S(1)}, u32[]{:S(2)}, u32[]{:S(2)}) %collective-permute-start.3) | collective-permute-done | bytes 122912 | tf_op jit(solution)/shard_map/ppermute | solution.py:178
  59.6 0.5 collective-permute-start.5
  60.1 2.4 %collective-permute-start.6 = (bf16[2,4,480,128]{3,2,1,0:T(8,128)(2,1)S(1)}, bf16[2,4,480,128]{3,2,1,0:T(8,128)(2,1)S(1)}, u32[]{:S(2)}, u32[]{:S(2)}) collective-permute-start(bf16[2,4,480,128]{3,2,1,0:T(8,128)(2,1)S(1)} %bitcast_dynamic-update-slice_fusion.23), channel_id=1, source_target_pairs={{0,24},{8,0},{16,8},{24,16},{1,25},{9,1},{17,9},{25,17},{2,26},{10... | collective-permute-start | bytes 2949128 | tf_op jit(solution)/shard_map/ppermute | solution.py:178
  62.5 0.6 broadcast_in_dim.132
  63.2 0.1 bitcast_dynamic-update-slice_fusion.2
  63.4 0.1 pad_maximum_fusion
  63.5 0.1 collective-permute-start.17
  63.6 2.7 %collective-permute-start.18 = (bf16[2752,128]{1,0:T(8,128)(2,1)S(1)}, bf16[2752,128]{1,0:T(8,128)(2,1)S(1)}, u32[]{:S(2)}, u32[]{:S(2)}) collective-permute-start(bf16[2752,128]{1,0:T(8,128)(2,1)S(1)} %get-tuple-element.10), channel_id=1, source_target_pairs={{0,7},{1,0},{2,1},{3,2},{4,3},{5,4},{6,5},{7,6},{8,15},{9,8},{10,9... | collective-permute-start | bytes 2113544 | tf_op jit(solution)/shard_map/ppermute | solution.py:178
  66.2 0.1 bitcast_dynamic-update-slice_fusion.4
  66.3 0.1 bitcast_dynamic-update-slice_fusion.3
  66.5 15.0 %collective-permute-done.5 = bf16[2,4,480,128]{3,2,1,0:T(8,128)(2,1)S(1)} collective-permute-done((bf16[2,4,480,128]{3,2,1,0:T(8,128)(2,1)S(1)}, bf16[2,4,480,128]{3,2,1,0:T(8,128)(2,1)S(1)}, u32[]{:S(2)}, u32[]{:S(2)}) %collective-permute-start.5) | collective-permute-done | bytes 983072 | tf_op jit(solution)/shard_map/ppermute | solution.py:178
  81.5 0.1 collective-permute-start.7
  81.7 2.7 %collective-permute-start.8 = (bf16[1,4,480,128]{3,2,1,0:T(8,128)(2,1)S(1)}, bf16[1,4,480,128]{3,2,1,0:T(8,128)(2,1)S(1)}, u32[]{:S(2)}, u32[]{:S(2)}) collective-permute-start(bf16[1,4,480,128]{3,2,1,0:T(8,128)(2,1)S(1)} %slice.132), channel_id=1, source_target_pairs={{0,24},{8,0},{16,8},{24,16},{1,25},{9,1},{17,9},{25,17},{2,26},{10... | collective-permute-start | bytes 1474568 | tf_op jit(solution)/shard_map/ppermute | solution.py:178
  84.4 0.1 bitcast_dynamic-update-slice_fusion.1
  84.5 0.1 bitcast_dynamic-update-slice_fusion
  84.7 0.1 collective-permute-start.19
  84.9 2.9 %collective-permute-start.20 = (bf16[4,1,160,128]{3,2,1,0:T(8,128)(2,1)S(1)}, bf16[4,1,160,128]{3,2,1,0:T(8,128)(2,1)S(1)}, u32[]{:S(2)}, u32[]{:S(2)}) collective-permute-start(bf16[4,1,160,128]{3,2,1,0:T(8,128)(2,1)S(1)} %slice.151), channel_id=1, source_target_pairs={{0,7},{1,0},{2,1},{3,2},{4,3},{5,4},{6,5},{7,6},{8,15},{9,8},{10,9... | collective-permute-start | bytes 491528 | tf_op jit(solution)/shard_map/ppermute | solution.py:178
  87.9 0.1 constant_dynamic-update-slice_fusion.11
  88.0 0.1 constant_dynamic-update-slice_fusion.10
  88.1 2.3 %collective-permute-done.19 = bf16[4,1,160,128]{3,2,1,0:T(8,128)(2,1)S(1)} collective-permute-done((bf16[4,1,160,128]{3,2,1,0:T(8,128)(2,1)S(1)}, bf16[4,1,160,128]{3,2,1,0:T(8,128)(2,1)S(1)}, u32[]{:S(2)}, u32[]{:S(2)}) %collective-permute-start.19) | collective-permute-done | bytes 163872 | tf_op jit(solution)/shard_map/ppermute | solution.py:178
  90.6 1.2 %collective-permute-done.7 = bf16[1,4,480,128]{3,2,1,0:T(8,128)(2,1)S(1)} collective-permute-done((bf16[1,4,480,128]{3,2,1,0:T(8,128)(2,1)S(1)}, bf16[1,4,480,128]{3,2,1,0:T(8,128)(2,1)S(1)}, u32[]{:S(2)}, u32[]{:S(2)}) %collective-permute-start.7) | collective-permute-done | bytes 491552 | tf_op jit(solution)/shard_map/ppermute | solution.py:178
  91.8 0.1 bitcast_dynamic-update-slice_fusion.7
  91.9 0.1 bitcast_dynamic-update-slice_fusion.6
  92.0 4.8 %shard_map.86 = (bf16[24,128,128]{2,1,0:T(8,128)(2,1)S(1)}, f32[26,128,128]{2,1,0:T(8,128)S(1)}) custom-call(s32[168]{0:T(256)S(1)} %reshape.51.codes, bf16[42,128,128]{2,1,0:T(8,128)(2,1)S(1)} %copy-done, bf16[32,480,128]{2,1,0:T(8,128)(2,1)S(1)} %bitcast.131), custom_call_target="tpu_custom_call" | custom-call | flops 503316480 | bytes 8388608 | tf_op jit(solution)/shard_map/pallas_call | solution.py:135
  96.8 7.5 %shard_map.87 = (bf16[42,128,128]{2,1,0:T(8,128)(2,1)}, bf16[8,128,128]{2,1,0:T(8,128)(2,1)S(1)}) custom-call(s32[168]{0:T(256)S(1)} %reshape.51.codes, s32[1]{0:T(128)} %bitcast.where, bf16[42,128,128]{2,1,0:T(8,128)(2,1)S(1)} %copy-done, bf16[128,128]{1,0:T(8,128)(2,1)S(1)} %bitcast.134, f32[26,128,128]{2,1,0:T(8,128)S(1)} %get-tuple-element.6.acc_in, ...), custom_call_target="tpu_custom_call" | custom-call | flops 528482304 | bytes 8388608 | tf_op jit(solution)/shard_map/pallas_call | solution.py:154
  104.3 15.3 %all_to_all.5 = bf16[8,128,128]{2,1,0:T(8,128)(2,1)S(1)} all-to-all(bf16[8,128,128]{2,1,0:T(8,128)(2,1)S(1)} %get-tuple-element.9), channel_id=1, replica_groups=mesh['x'=4,'core'=2,'y'=4,'z'=8] {'x','core'}, dimensions={0} | all-to-all | bytes 524288 | tf_op jit(solution)/shard_map/all_to_all | solution.py:271
  119.6 0.7 reduce_sum.12
  (65 shorter events, 1.1 us)
Async XLA Ops:
  5.7 12.5 %collective-permute-start = (bf16[880,128]{1,0:T(8,128)(2,1)S(1)}, bf16[880,128]{1,0:T(8,128)(2,1)S(1)}, u32[]{:S(2)}, u32[]{:S(2)}) collective-permute-start(bf16[880,128]{1,0:T(8,128)(2,1)S(1)} %constant_dynamic-update-slice_fusion), channel_id=1, source_target_pairs={{0,4},{1,5},{2,6},{3,7},{4,0},{5,1},{6,2},{7,3},{8,12},{9,13},{10,... | collective-permute-start | bytes 675848 | tf_op jit(solution)/shard_map/ppermute | solution.py:178
  18.2 29.6 %collective-permute-start.1 = (bf16[2,480,128]{2,1,0:T(8,128)(2,1)S(1)}, bf16[2,480,128]{2,1,0:T(8,128)(2,1)S(1)}, u32[]{:S(2)}, u32[]{:S(2)}) collective-permute-start(bf16[2,480,128]{2,1,0:T(8,128)(2,1)S(1)} %slice.128), channel_id=1, source_target_pairs={{0,1},{1,2},{2,3},{3,4},{4,5},{5,6},{6,7},{7,0},{8,9},{9,10},{10,1... | collective-permute-start | bytes 737288 | tf_op jit(solution)/shard_map/ppermute | solution.py:178
  22.7 26.7 %collective-permute-start.2 = (bf16[2,480,128]{2,1,0:T(8,128)(2,1)S(1)}, bf16[2,480,128]{2,1,0:T(8,128)(2,1)S(1)}, u32[]{:S(2)}, u32[]{:S(2)}) collective-permute-start(bf16[2,480,128]{2,1,0:T(8,128)(2,1)S(1)} %slice.128), channel_id=1, source_target_pairs={{0,7},{1,0},{2,1},{3,2},{4,3},{5,4},{6,5},{7,6},{8,15},{9,8},{10,9... | collective-permute-start | bytes 737288 | tf_op jit(solution)/shard_map/ppermute | solution.py:178
  26.6 7.0 %collective-permute-start.9 = (bf16[2,400,128]{2,1,0:T(8,128)(2,1)S(1)}, bf16[2,400,128]{2,1,0:T(8,128)(2,1)S(1)}, u32[]{:S(2)}, u32[]{:S(2)}) collective-permute-start(bf16[2,400,128]{2,1,0:T(8,128)(2,1)S(1)} %slice.133), channel_id=1, source_target_pairs={{0,8},{8,16},{16,24},{24,0},{1,9},{9,17},{17,25},{25,1},{2,10},{10... | collective-permute-start | bytes 614408 | tf_op jit(solution)/shard_map/ppermute | solution.py:178
  27.9 5.7 %collective-permute-start.10 = (bf16[2,400,128]{2,1,0:T(8,128)(2,1)S(1)}, bf16[2,400,128]{2,1,0:T(8,128)(2,1)S(1)}, u32[]{:S(2)}, u32[]{:S(2)}) collective-permute-start(bf16[2,400,128]{2,1,0:T(8,128)(2,1)S(1)} %slice.133), channel_id=1, source_target_pairs={{0,24},{8,0},{16,8},{24,16},{1,25},{9,1},{17,9},{25,17},{2,26},{10... | collective-permute-start | bytes 614408 | tf_op jit(solution)/shard_map/ppermute | solution.py:178
  29.5 9.6 %collective-permute-start.11 = (bf16[2,400,128]{2,1,0:T(8,128)(2,1)S(1)}, bf16[2,400,128]{2,1,0:T(8,128)(2,1)S(1)}, u32[]{:S(2)}, u32[]{:S(2)}) collective-permute-start(bf16[2,400,128]{2,1,0:T(8,128)(2,1)S(1)} %slice.133), channel_id=1, source_target_pairs={{0,16},{8,24},{16,0},{24,8},{1,17},{9,25},{17,1},{25,9},{2,18},{10... | collective-permute-start | bytes 614408 | tf_op jit(solution)/shard_map/ppermute | solution.py:178
  39.2 24.2 %collective-permute-start.12 = (bf16[4,2,368,128]{3,2,1,0:T(8,128)(2,1)S(1)}, bf16[4,2,368,128]{3,2,1,0:T(8,128)(2,1)S(1)}, u32[]{:S(2)}, u32[]{:S(2)}) collective-permute-start(bf16[4,2,368,128]{3,2,1,0:T(8,128)(2,1)S(1)} %slice.134), channel_id=1, source_target_pairs={{0,1},{1,2},{2,3},{3,4},{4,5},{5,6},{6,7},{7,0},{8,9},{9,10},{10,1... | collective-permute-start | bytes 2261000 | tf_op jit(solution)/shard_map/ppermute | solution.py:178
  39.3 24.0 %collective-permute-start.13 = (bf16[4,2,368,128]{3,2,1,0:T(8,128)(2,1)S(1)}, bf16[4,2,368,128]{3,2,1,0:T(8,128)(2,1)S(1)}, u32[]{:S(2)}, u32[]{:S(2)}) collective-permute-start(bf16[4,2,368,128]{3,2,1,0:T(8,128)(2,1)S(1)} %slice.134), channel_id=1, source_target_pairs={{0,7},{1,0},{2,1},{3,2},{4,3},{5,4},{6,5},{7,6},{8,15},{9,8},{10,9... | collective-permute-start | bytes 2261000 | tf_op jit(solution)/shard_map/ppermute | solution.py:178
  45.9 5.9 %collective-permute-start.14 = (bf16[2,4,2,32,128]{4,3,2,1,0:T(8,128)(2,1)S(1)}, bf16[2,4,2,32,128]{4,3,2,1,0:T(8,128)(2,1)S(1)}, u32[]{:S(2)}, u32[]{:S(2)}) collective-permute-start(bf16[2,4,2,32,128]{4,3,2,1,0:T(8,128)(2,1)S(1)} %bitcast.152), channel_id=1, source_target_pairs={{0,64},{64,128},{128,192},{192,0},{1,65},{65,129},{129,193},{193,1... | collective-permute-start | bytes 393224 | tf_op jit(solution)/shard_map/ppermute | solution.py:178
  47.8 4.5 %collective-permute-start.15 = (bf16[2,4,2,32,128]{4,3,2,1,0:T(8,128)(2,1)S(1)}, bf16[2,4,2,32,128]{4,3,2,1,0:T(8,128)(2,1)S(1)}, u32[]{:S(2)}, u32[]{:S(2)}) collective-permute-start(bf16[2,4,2,32,128]{4,3,2,1,0:T(8,128)(2,1)S(1)} %bitcast.154), channel_id=1, source_target_pairs={{0,192},{64,0},{128,64},{192,128},{1,193},{65,1},{129,65},{193,129... | collective-permute-start | bytes 393224 | tf_op jit(solution)/shard_map/ppermute | solution.py:178
  49.4 5.4 %collective-permute-start.16 = (bf16[2,4,2,32,128]{4,3,2,1,0:T(8,128)(2,1)S(1)}, bf16[2,4,2,32,128]{4,3,2,1,0:T(8,128)(2,1)S(1)}, u32[]{:S(2)}, u32[]{:S(2)}) collective-permute-start(bf16[2,4,2,32,128]{4,3,2,1,0:T(8,128)(2,1)S(1)} %bitcast.155), channel_id=1, source_target_pairs={{0,128},{64,192},{128,0},{192,64},{1,129},{65,193},{129,1},{193,65... | collective-permute-start | bytes 393224 | tf_op jit(solution)/shard_map/ppermute | solution.py:178
  51.9 7.7 %collective-permute-start.3 = (bf16[1,480,128]{2,1,0:T(8,128)(2,1)S(1)}, bf16[1,480,128]{2,1,0:T(8,128)(2,1)S(1)}, u32[]{:S(2)}, u32[]{:S(2)}) collective-permute-start(bf16[1,480,128]{2,1,0:T(8,128)(2,1)S(1)} %slice.129), channel_id=1, source_target_pairs={{0,1},{1,2},{2,3},{3,4},{4,5},{5,6},{6,7},{7,0},{8,9},{9,10},{10,1... | collective-permute-start | bytes 368648 | tf_op jit(solution)/shard_map/ppermute | solution.py:178
  52.3 7.3 %collective-permute-start.4 = (bf16[1,480,128]{2,1,0:T(8,128)(2,1)S(1)}, bf16[1,480,128]{2,1,0:T(8,128)(2,1)S(1)}, u32[]{:S(2)}, u32[]{:S(2)}) collective-permute-start(bf16[1,480,128]{2,1,0:T(8,128)(2,1)S(1)} %slice.130), channel_id=1, source_target_pairs={{0,7},{1,0},{2,1},{3,2},{4,3},{5,4},{6,5},{7,6},{8,15},{9,8},{10,9... | collective-permute-start | bytes 368648 | tf_op jit(solution)/shard_map/ppermute | solution.py:178
  59.6 21.9 %collective-permute-start.5 = (bf16[2,4,480,128]{3,2,1,0:T(8,128)(2,1)S(1)}, bf16[2,4,480,128]{3,2,1,0:T(8,128)(2,1)S(1)}, u32[]{:S(2)}, u32[]{:S(2)}) collective-permute-start(bf16[2,4,480,128]{3,2,1,0:T(8,128)(2,1)S(1)} %bitcast_dynamic-update-slice_fusion.23), channel_id=1, source_target_pairs={{0,8},{8,16},{16,24},{24,0},{1,9},{9,17},{17,25},{25,1},{2,10},{10... | collective-permute-start | bytes 2949128 | tf_op jit(solution)/shard_map/ppermute | solution.py:178
  60.1 21.5 %collective-permute-start.6 = (bf16[2,4,480,128]{3,2,1,0:T(8,128)(2,1)S(1)}, bf16[2,4,480,128]{3,2,1,0:T(8,128)(2,1)S(1)}, u32[]{:S(2)}, u32[]{:S(2)}) collective-permute-start(bf16[2,4,480,128]{3,2,1,0:T(8,128)(2,1)S(1)} %bitcast_dynamic-update-slice_fusion.23), channel_id=1, source_target_pairs={{0,24},{8,0},{16,8},{24,16},{1,25},{9,1},{17,9},{25,17},{2,26},{10... | collective-permute-start | bytes 2949128 | tf_op jit(solution)/shard_map/ppermute | solution.py:178
  63.5 21.2 %collective-permute-start.17 = (bf16[2752,128]{1,0:T(8,128)(2,1)S(1)}, bf16[2752,128]{1,0:T(8,128)(2,1)S(1)}, u32[]{:S(2)}, u32[]{:S(2)}) collective-permute-start(bf16[2752,128]{1,0:T(8,128)(2,1)S(1)} %get-tuple-element.11), channel_id=1, source_target_pairs={{0,1},{1,2},{2,3},{3,4},{4,5},{5,6},{6,7},{7,0},{8,9},{9,10},{10,1... | collective-permute-start | bytes 2113544 | tf_op jit(solution)/shard_map/ppermute | solution.py:178
  63.6 21.2 %collective-permute-start.18 = (bf16[2752,128]{1,0:T(8,128)(2,1)S(1)}, bf16[2752,128]{1,0:T(8,128)(2,1)S(1)}, u32[]{:S(2)}, u32[]{:S(2)}) collective-permute-start(bf16[2752,128]{1,0:T(8,128)(2,1)S(1)} %get-tuple-element.10), channel_id=1, source_target_pairs={{0,7},{1,0},{2,1},{3,2},{4,3},{5,4},{6,5},{7,6},{8,15},{9,8},{10,9... | collective-permute-start | bytes 2113544 | tf_op jit(solution)/shard_map/ppermute | solution.py:178
  81.5 10.3 %collective-permute-start.7 = (bf16[1,4,480,128]{3,2,1,0:T(8,128)(2,1)S(1)}, bf16[1,4,480,128]{3,2,1,0:T(8,128)(2,1)S(1)}, u32[]{:S(2)}, u32[]{:S(2)}) collective-permute-start(bf16[1,4,480,128]{3,2,1,0:T(8,128)(2,1)S(1)} %slice.131), channel_id=1, source_target_pairs={{0,8},{8,16},{16,24},{24,0},{1,9},{9,17},{17,25},{25,1},{2,10},{10... | collective-permute-start | bytes 1474568 | tf_op jit(solution)/shard_map/ppermute | solution.py:178
  81.7 10.2 %collective-permute-start.8 = (bf16[1,4,480,128]{3,2,1,0:T(8,128)(2,1)S(1)}, bf16[1,4,480,128]{3,2,1,0:T(8,128)(2,1)S(1)}, u32[]{:S(2)}, u32[]{:S(2)}) collective-permute-start(bf16[1,4,480,128]{3,2,1,0:T(8,128)(2,1)S(1)} %slice.132), channel_id=1, source_target_pairs={{0,24},{8,0},{16,8},{24,16},{1,25},{9,1},{17,9},{25,17},{2,26},{10... | collective-permute-start | bytes 1474568 | tf_op jit(solution)/shard_map/ppermute | solution.py:178
  84.7 5.8 %collective-permute-start.19 = (bf16[4,1,160,128]{3,2,1,0:T(8,128)(2,1)S(1)}, bf16[4,1,160,128]{3,2,1,0:T(8,128)(2,1)S(1)}, u32[]{:S(2)}, u32[]{:S(2)}) collective-permute-start(bf16[4,1,160,128]{3,2,1,0:T(8,128)(2,1)S(1)} %slice.150), channel_id=1, source_target_pairs={{0,1},{1,2},{2,3},{3,4},{4,5},{5,6},{6,7},{7,0},{8,9},{9,10},{10,1... | collective-permute-start | bytes 491528 | tf_op jit(solution)/shard_map/ppermute | solution.py:178
  84.9 5.6 %collective-permute-start.20 = (bf16[4,1,160,128]{3,2,1,0:T(8,128)(2,1)S(1)}, bf16[4,1,160,128]{3,2,1,0:T(8,128)(2,1)S(1)}, u32[]{:S(2)}, u32[]{:S(2)}) collective-permute-start(bf16[4,1,160,128]{3,2,1,0:T(8,128)(2,1)S(1)} %slice.151), channel_id=1, source_target_pairs={{0,7},{1,0},{2,1},{3,2},{4,3},{5,4},{6,5},{7,6},{8,15},{9,8},{10,9... | collective-permute-start | bytes 491528 | tf_op jit(solution)/shard_map/ppermute | solution.py:178
  87.9 4.1 %copy-start = (bf16[42,128,128]{2,1,0:T(8,128)(2,1)S(1)}, bf16[42,128,128]{2,1,0:T(8,128)(2,1)}, u32[]{:S(2)}) copy-start(bf16[42,128,128]{2,1,0:T(8,128)(2,1)} %rhs.3) | copy-start | bytes 4128772
  91.9 5.0 %copy-start.1 = (bf16[1,128,128]{2,1,0:T(8,128)(2,1)S(1)}, bf16[1,128,128]{2,1,0:T(8,128)(2,1)}, u32[]{:S(2)}) copy-start(bf16[1,128,128]{2,1,0:T(8,128)(2,1)} %param.8) | copy-start | bytes 98308

commit v5 on v4

--- a/solution.py
+++ b/solution.py
@@ -117,6 +117,34 @@
         store.wait()
 
 
+def pack_rows(row, diag, off, factor, inverse, packed, factor_rows, inverse_rows, spread, sems):
+    lead_diag, lead_off = FIRST * ROWS, FIRST * GROUP
+    rest_diag, rest_off = LATER * ROWS, LATER * GROUP
+    rest_at = LEAD_ROWS + LATER_PAD * ROWS
+    copies = (
+        pltpu.make_async_copy(factor, factor_rows, sems.at[0]),
+        pltpu.make_async_copy(inverse, inverse_rows, sems.at[1]),
+        pltpu.make_async_copy(diag.at[pl.ds(0, lead_diag)], packed.at[pl.ds(0, lead_diag)], sems.at[2]),
+        pltpu.make_async_copy(off.at[pl.ds(0, lead_off)], packed.at[pl.ds(lead_diag, lead_off)], sems.at[3]),
+        pltpu.make_async_copy(diag.at[pl.ds(lead_diag, rest_diag)], packed.at[pl.ds(LEAD_ROWS, rest_diag)], sems.at[4]),
+        pltpu.make_async_copy(off.at[pl.ds(lead_off, rest_off)], packed.at[pl.ds(rest_at, rest_off)], sems.at[5]),
+    )
+    for copy in copies:
+        copy.start()
+    gap = (LATER_PAD - LATER) * ROWS
+    packed[pl.ds(rest_at - gap, gap), :] = jnp.zeros((gap, B), BF16)
+    copies[0].wait()
+    copies[1].wait()
+    for i in range(ROWS):
+        line = inverse_rows[...].astype(F32)[i : i + 1]
+        spread[pl.ds(i, TOP, stride=ROWS), :] = jnp.broadcast_to(line, (TOP, B))
+    block = lax.broadcasted_iota(jnp.int32, (TOP_ROWS, B), 0) // ROWS
+    top = jnp.where(block == row[0], spread[...], factor_rows[...].astype(F32))
+    packed[pl.ds(LEAD_ROWS + REST_ROWS, TOP_ROWS), :] = top.astype(BF16)
+    for copy in copies[2:]:
+        copy.wait()
+
+
 VMEM = pl.BlockSpec(memory_space=pltpu.VMEM)
 SMEM = pl.BlockSpec(memory_space=pltpu.SMEM)
 HBM = pl.BlockSpec(memory_space=pl.ANY)
@@ -129,6 +157,23 @@
 
 def cost(blocks, nbytes):
     return pl.CostEstimate(flops=2 * B**3 * blocks, bytes_accessed=nbytes, transcendentals=0)
+
+
+def run_pack(row, diag, off, factor, inverse):
+    return pl.pallas_call(
+        pack_rows,
+        out_shape=jax.ShapeDtypeStruct((LEAD_ROWS + REST_ROWS + TOP_ROWS, B), BF16),
+        in_specs=[SMEM] + [HBM] * 4,
+        out_specs=VMEM,
+        scratch_shapes=[
+            pltpu.VMEM((TOP_ROWS, B), BF16),
+            pltpu.VMEM((ROWS, B), BF16),
+            pltpu.VMEM((TOP_ROWS, B), F32),
+            pltpu.SemaphoreType.DMA((6,)),
+        ],
+        compiler_params=pltpu.CompilerParams(vmem_limit_bytes=2 << 20),
+        cost_estimate=cost(0, 1 << 19),
+    )(row, diag, off, factor, inverse)
 
 
 def run_leaves(codes, rhs, lead):
@@ -182,10 +227,9 @@
     return lax.dynamic_update_slice(buffer, x, start + (0,) * (buffer.ndim - len(start)))
 
 
-def gather(rows, top):
+def gather(packed):
     chip, y, z = lax.axis_index("x"), lax.axis_index("y"), lax.axis_index("z")
     hi, lo = z // LO, z % LO
-    packed = jnp.concatenate([rows, top], axis=0)
     other = shift(packed, "z", LO)
     pair = put(put(jnp.zeros((HI, *packed.shape), BF16), packed[None], hi), other[None], 1 - hi)
     lead, late = pair[:, :LEAD_ROWS], pair[:, LEAD_ROWS:]
@@ -202,6 +246,7 @@
     late_all = put(jnp.zeros((NY, *late.shape), BF16), late[None], y)
     for k in (1, -1, 2):
         late_all = put(late_all, shift(late, "y", k)[None], (y - k) % NY)
+    late_all, own = lax.optimization_barrier((late_all, own))
     rest, top = late_all[:, :, :REST_ROWS], late_all[:, :, REST_ROWS:]
     rest_right, rest_left = shift(rest, "z", 1), shift(rest, "z", -1)
 
@@ -248,21 +293,14 @@
 
 def local(local_rhs, top_rhs, diag_inv, top_inv, off_blocks, top_factor, targets):
     position = lax.axis_index(ROW)
-    diag, off = diag_inv.reshape(-1, B), off_blocks.reshape(-1, B)
-    own = (jnp.arange(TOP) == position)[:, None, None]
-    top_rows = jnp.where(own, top_inv, top_factor[0]).reshape(-1, B)
-    pad = jnp.zeros(((LATER_PAD - LATER) * ROWS, B), BF16)
-    rows = jnp.concatenate(
-        [
-            diag[: FIRST * ROWS],
-            off[: FIRST * GROUP],
-            diag[FIRST * ROWS :],
-            pad,
-            off[FIRST * GROUP :],
-        ],
-        axis=0,
-    )
-    lead_all, rest_all, top_all = gather(rows, top_rows)
+    packed = run_pack(
+        position[None],
+        diag_inv.reshape(-1, B),
+        off_blocks.reshape(-1, B),
+        top_factor.reshape(-1, B),
+        top_inv.reshape(-1, B),
+    )
+    lead_all, rest_all, top_all = gather(packed)
     codes = targets.reshape(-1)
     leaf_sol, acc = run_leaves(codes, local_rhs, lead_all)
     sol, addends = run_later(

time: 121 us -> 115 us (0.950)
  waiting for transfers between devices: 35.5 us -> 30.2 us
    ppermute x21, waiting for transfers between devices: 35.5 us -> 30.2 us  [shift(): return lax.ppermute(x, axis, [(n, (n + k) % size) for n in range(size)])]
    slice x4 -> x0, local copies, waits for them, and re-layouts: 3.33 us -> none  [the longest x1 0.93 us: local(): off[:FIRST * GROUP]]
    unnamed x17 -> x20, local copies, waits for them, and re-layouts: 0.92 us -> 3.94 us
  transfers between devices with their start and end apart: 21 -> 21, of which waited for: 10 -> 8; matrix products, arithmetic and copies ran while one was open for 4% -> 4% of each run, Pallas kernels for 0% -> 4%
where the time goes in v5:
time: 115 us
  starting transfers between devices  42.3 us (37%)
  waiting for transfers between devices  30.2 us (26%)
  blocking collectives  20.1 us (17%)
  Pallas kernels  12.4 us (11%)
  local copies, waits for them, and re-layouts  7.62 us (7%)
  between operations  1.31 us (1%)
    ppermute x21, starting transfers between devices, shift(): return lax.ppermute(x, axis, [(n, (n + k) % size) for n in range(size)])  42.3 us
    ppermute x21, waiting for transfers between devices, shift(): return lax.ppermute(x, axis, [(n, (n + k) % size) for n in range(size)])  30.2 us
    all_to_all x1, blocking collectives, local(): parts = lax.all_to_all(addends, ROW, 0, 0, tiled=True)  15 us
    pallas_call x1, Pallas kernels, run_later(): pl.pallas_call(later_levels, out_shape=(jax.ShapeDtypeStruct((SUB, B, B),...  7.5 us
    all_gather x1, blocking collectives, gather(): cores = lax.all_gather(top, 'core', axis=0)  5.12 us
    pallas_call x1, Pallas kernels, run_leaves(): pl.pallas_call(leaf_level, out_shape=(jax.ShapeDtypeStruct((FIRST, B, B),...  4.57 us
    unnamed x20, local copies, waits for them, and re-layouts  3.94 us
  transfers between devices with their start and end apart: 21, of which 8 were waited for; matrix products, arithmetic and copies ran while one was open for 4% of the time, Pallas kernels for 4%

profile of v5, /device:TPU:1, one launch (start us, length us, event | category | flops | bytes accessed | tf_op | source)
XLA Modules:
  0.0 114.6 jit_solution(648430763422179722)
XLA Ops:
  0.6 0.9 copy-done.1
  1.6 0.8 copy-done.2
  2.3 0.7 copy-done.4
  3.0 0.7 copy-done.5
  3.7 0.3 shard_map.86
  4.1 7.8 %collective-permute-start = (bf16[880,128]{1,0:T(8,128)(2,1)S(1)}, bf16[880,128]{1,0:T(8,128)(2,1)S(1)}, u32[]{:S(2)}, u32[]{:S(2)}) collective-permute-start(bf16[880,128]{1,0:T(8,128)(2,1)S(1)} %shard_map.86), channel_id=1, source_target_pairs={{0,4},{1,5},{2,6},{3,7},{4,0},{5,1},{6,2},{7,3},{8,12},{9,13},{10,... | collective-permute-start | bytes 675848 | tf_op jit(solution)/shard_map/ppermute | solution.py:223
  11.9 0.8 copy.26
  12.7 0.1 reshape.49.codes
  12.8 0.1 broadcast_in_dim.107
  13.0 3.6 %collective-permute-done = bf16[880,128]{1,0:T(8,128)(2,1)S(1)} collective-permute-done((bf16[880,128]{1,0:T(8,128)(2,1)S(1)}, bf16[880,128]{1,0:T(8,128)(2,1)S(1)}, u32[]{:S(2)}, u32[]{:S(2)}) %collective-permute-start) | collective-permute-done | bytes 225312 | tf_op jit(solution)/shard_map/ppermute | solution.py:223
  16.6 1.9 %collective-permute-start.1 = (bf16[2,400,128]{2,1,0:T(8,128)(2,1)S(1)}, bf16[2,400,128]{2,1,0:T(8,128)(2,1)S(1)}, u32[]{:S(2)}, u32[]{:S(2)}) collective-permute-start(bf16[2,400,128]{2,1,0:T(8,128)(2,1)S(1)} %slice.96), channel_id=1, source_target_pairs={{0,8},{8,16},{16,24},{24,0},{1,9},{9,17},{17,25},{25,1},{2,10},{10... | collective-permute-start | bytes 614408 | tf_op jit(solution)/shard_map/ppermute | solution.py:223
  18.6 1.5 %collective-permute-start.2 = (bf16[2,400,128]{2,1,0:T(8,128)(2,1)S(1)}, bf16[2,400,128]{2,1,0:T(8,128)(2,1)S(1)}, u32[]{:S(2)}, u32[]{:S(2)}) collective-permute-start(bf16[2,400,128]{2,1,0:T(8,128)(2,1)S(1)} %slice.96), channel_id=1, source_target_pairs={{0,24},{8,0},{16,8},{24,16},{1,25},{9,1},{17,9},{25,17},{2,26},{10... | collective-permute-start | bytes 614408 | tf_op jit(solution)/shard_map/ppermute | solution.py:223
  20.1 1.6 %collective-permute-start.3 = (bf16[2,400,128]{2,1,0:T(8,128)(2,1)S(1)}, bf16[2,400,128]{2,1,0:T(8,128)(2,1)S(1)}, u32[]{:S(2)}, u32[]{:S(2)}) collective-permute-start(bf16[2,400,128]{2,1,0:T(8,128)(2,1)S(1)} %slice.96), channel_id=1, source_target_pairs={{0,16},{8,24},{16,0},{24,8},{1,17},{9,25},{17,1},{25,9},{2,18},{10... | collective-permute-start | bytes 614408 | tf_op jit(solution)/shard_map/ppermute | solution.py:223
  21.7 3.9 %collective-permute-start.4 = (bf16[2,480,128]{2,1,0:T(8,128)(2,1)S(1)}, bf16[2,480,128]{2,1,0:T(8,128)(2,1)S(1)}, u32[]{:S(2)}, u32[]{:S(2)}) collective-permute-start(bf16[2,480,128]{2,1,0:T(8,128)(2,1)S(1)} %slice.97), channel_id=1, source_target_pairs={{0,1},{1,2},{2,3},{3,4},{4,5},{5,6},{6,7},{7,0},{8,9},{9,10},{10,1... | collective-permute-start | bytes 737288 | tf_op jit(solution)/shard_map/ppermute | solution.py:223
  25.6 3.9 %collective-permute-start.5 = (bf16[2,480,128]{2,1,0:T(8,128)(2,1)S(1)}, bf16[2,480,128]{2,1,0:T(8,128)(2,1)S(1)}, u32[]{:S(2)}, u32[]{:S(2)}) collective-permute-start(bf16[2,480,128]{2,1,0:T(8,128)(2,1)S(1)} %slice.97), channel_id=1, source_target_pairs={{0,7},{1,0},{2,1},{3,2},{4,3},{5,4},{6,5},{7,6},{8,15},{9,8},{10,9... | collective-permute-start | bytes 737288 | tf_op jit(solution)/shard_map/ppermute | solution.py:223
  29.5 0.1 broadcast_in_dim.114
  29.6 0.1 broadcast_in_dim.106
  29.9 4.1 %collective-permute-done.4 = bf16[2,480,128]{2,1,0:T(8,128)(2,1)S(1)} collective-permute-done((bf16[2,480,128]{2,1,0:T(8,128)(2,1)S(1)}, bf16[2,480,128]{2,1,0:T(8,128)(2,1)S(1)}, u32[]{:S(2)}, u32[]{:S(2)}) %collective-permute-start.4) | collective-permute-done | bytes 245792 | tf_op jit(solution)/shard_map/ppermute | solution.py:223
  34.1 0.1 collective-permute-start.6
  34.2 0.0 collective-permute-done.5
  34.2 3.7 %collective-permute-start.7 = (bf16[1,480,128]{2,1,0:T(8,128)(2,1)S(1)}, bf16[1,480,128]{2,1,0:T(8,128)(2,1)S(1)}, u32[]{:S(2)}, u32[]{:S(2)}) collective-permute-start(bf16[1,480,128]{2,1,0:T(8,128)(2,1)S(1)} %slice.99), channel_id=1, source_target_pairs={{0,7},{1,0},{2,1},{3,2},{4,3},{5,4},{6,5},{7,6},{8,15},{9,8},{10,9... | collective-permute-start | bytes 368648 | tf_op jit(solution)/shard_map/ppermute | solution.py:223
  38.0 2.1 %collective-permute-done.6 = bf16[1,480,128]{2,1,0:T(8,128)(2,1)S(1)} collective-permute-done((bf16[1,480,128]{2,1,0:T(8,128)(2,1)S(1)}, bf16[1,480,128]{2,1,0:T(8,128)(2,1)S(1)}, u32[]{:S(2)}, u32[]{:S(2)}) %collective-permute-start.6) | collective-permute-done | bytes 122912 | tf_op jit(solution)/shard_map/ppermute | solution.py:223
  40.1 0.0 collective-permute-done.7
  40.1 0.6 collective-permute-start.8
  40.7 2.1 %collective-permute-start.9 = (bf16[2,4,480,128]{3,2,1,0:T(8,128)(2,1)S(1)}, bf16[2,4,480,128]{3,2,1,0:T(8,128)(2,1)S(1)}, u32[]{:S(2)}, u32[]{:S(2)}) collective-permute-start(bf16[2,4,480,128]{3,2,1,0:T(8,128)(2,1)S(1)} %bitcast_dynamic-update-slice_fusion.23), channel_id=1, source_target_pairs={{0,24},{8,0},{16,8},{24,16},{1,25},{9,1},{17,9},{25,17},{2,26},{10... | collective-permute-start | bytes 2949128 | tf_op jit(solution)/shard_map/ppermute | solution.py:223
  42.9 0.4 collective-permute-start.12
  43.3 2.5 %collective-permute-start.13 = (bf16[4,2,368,128]{3,2,1,0:T(8,128)(2,1)S(1)}, bf16[4,2,368,128]{3,2,1,0:T(8,128)(2,1)S(1)}, u32[]{:S(2)}, u32[]{:S(2)}) collective-permute-start(bf16[4,2,368,128]{3,2,1,0:T(8,128)(2,1)S(1)} %slice.78), channel_id=1, source_target_pairs={{0,7},{1,0},{2,1},{3,2},{4,3},{5,4},{6,5},{7,6},{8,15},{9,8},{10,9... | collective-permute-start | bytes 2261000 | tf_op jit(solution)/shard_map/ppermute | solution.py:223
  45.8 0.6 broadcast_in_dim.105
  46.5 0.1 bitcast_dynamic-update-slice_fusion.2
  46.6 5.1 %all-gather = bf16[8,2,32,128]{3,2,1,0:T(8,128)(2,1)S(1)} all-gather(bf16[4,2,32,128]{3,2,1,0:T(8,128)(2,1)S(1)} %slice.80), channel_id=2, replica_groups=mesh['x'=4,'core'=2,'y'=4,'z'=8] {'core'}, dimensions={0}, use_global_device_ids=true | all-gather | bytes 196608 | tf_op jit(solution)/shard_map/all_gather | solution.py:255
  51.7 1.2 %collective-permute-start.14 = (bf16[2,4,2,32,128]{4,3,2,1,0:T(8,128)(2,1)S(1)}, bf16[2,4,2,32,128]{4,3,2,1,0:T(8,128)(2,1)S(1)}, u32[]{:S(2)}, u32[]{:S(2)}) collective-permute-start(bf16[2,4,2,32,128]{4,3,2,1,0:T(8,128)(2,1)S(1)} %bitcast.153), channel_id=1, source_target_pairs={{0,64},{64,128},{128,192},{192,0},{1,65},{65,129},{129,193},{193,1... | collective-permute-start | bytes 393224 | tf_op jit(solution)/shard_map/ppermute | solution.py:223
  52.9 0.4 broadcast_in_dim.125
  53.3 0.1 bitcast_dynamic-update-slice_fusion.5
  53.5 0.1 broadcast_in_dim.129
  53.6 4.1 %collective-permute-done.14 = bf16[2,4,2,32,128]{4,3,2,1,0:T(8,128)(2,1)S(1)} collective-permute-done((bf16[2,4,2,32,128]{4,3,2,1,0:T(8,128)(2,1)S(1)}, bf16[2,4,2,32,128]{4,3,2,1,0:T(8,128)(2,1)S(1)}, u32[]{:S(2)}, u32[]{:S(2)}) %collective-permute-start.14) | collective-permute-done | bytes 131104 | tf_op jit(solution)/shard_map/ppermute | solution.py:223
  57.7 1.3 %collective-permute-start.15 = (bf16[2,4,2,32,128]{4,3,2,1,0:T(8,128)(2,1)S(1)}, bf16[2,4,2,32,128]{4,3,2,1,0:T(8,128)(2,1)S(1)}, u32[]{:S(2)}, u32[]{:S(2)}) collective-permute-start(bf16[2,4,2,32,128]{4,3,2,1,0:T(8,128)(2,1)S(1)} %bitcast.155), channel_id=1, source_target_pairs={{0,192},{64,0},{128,64},{192,128},{1,193},{65,1},{129,65},{193,129... | collective-permute-start | bytes 393224 | tf_op jit(solution)/shard_map/ppermute | solution.py:223
  59.0 2.8 %collective-permute-done.15 = bf16[2,4,2,32,128]{4,3,2,1,0:T(8,128)(2,1)S(1)} collective-permute-done((bf16[2,4,2,32,128]{4,3,2,1,0:T(8,128)(2,1)S(1)}, bf16[2,4,2,32,128]{4,3,2,1,0:T(8,128)(2,1)S(1)}, u32[]{:S(2)}, u32[]{:S(2)}) %collective-permute-start.15) | collective-permute-done | bytes 131104 | tf_op jit(solution)/shard_map/ppermute | solution.py:223
  61.8 1.5 %collective-permute-start.16 = (bf16[2,4,2,32,128]{4,3,2,1,0:T(8,128)(2,1)S(1)}, bf16[2,4,2,32,128]{4,3,2,1,0:T(8,128)(2,1)S(1)}, u32[]{:S(2)}, u32[]{:S(2)}) collective-permute-start(bf16[2,4,2,32,128]{4,3,2,1,0:T(8,128)(2,1)S(1)} %bitcast.156), channel_id=1, source_target_pairs={{0,128},{64,192},{128,0},{192,64},{1,129},{65,193},{129,1},{193,65... | collective-permute-start | bytes 393224 | tf_op jit(solution)/shard_map/ppermute | solution.py:223
  63.3 3.8 %collective-permute-done.16 = bf16[2,4,2,32,128]{4,3,2,1,0:T(8,128)(2,1)S(1)} collective-permute-done((bf16[2,4,2,32,128]{4,3,2,1,0:T(8,128)(2,1)S(1)}, bf16[2,4,2,32,128]{4,3,2,1,0:T(8,128)(2,1)S(1)}, u32[]{:S(2)}, u32[]{:S(2)}) %collective-permute-start.16) | collective-permute-done | bytes 131104 | tf_op jit(solution)/shard_map/ppermute | solution.py:223
  67.3 0.2 broadcast_in_dim.134
  67.6 0.0 collective-permute-done.12
  67.6 0.1 pad_maximum_fusion
  67.7 0.9 collective-permute-start.17
  68.7 1.8 %collective-permute-start.18 = (bf16[2752,128]{1,0:T(8,128)(2,1)S(1)}, bf16[2752,128]{1,0:T(8,128)(2,1)S(1)}, u32[]{:S(2)}, u32[]{:S(2)}) collective-permute-start(bf16[2752,128]{1,0:T(8,128)(2,1)S(1)} %get-tuple-element.14), channel_id=1, source_target_pairs={{0,7},{1,0},{2,1},{3,2},{4,3},{5,4},{6,5},{7,6},{8,15},{9,8},{10,9... | collective-permute-start | bytes 2113544 | tf_op jit(solution)/shard_map/ppermute | solution.py:223
  70.5 0.1 bitcast_dynamic-update-slice_fusion.4
  70.6 0.1 bitcast_dynamic-update-slice_fusion.3
  70.8 0.1 collective-permute-start.10
  70.9 2.7 %collective-permute-start.11 = (bf16[1,4,480,128]{3,2,1,0:T(8,128)(2,1)S(1)}, bf16[1,4,480,128]{3,2,1,0:T(8,128)(2,1)S(1)}, u32[]{:S(2)}, u32[]{:S(2)}) collective-permute-start(bf16[1,4,480,128]{3,2,1,0:T(8,128)(2,1)S(1)} %slice.101), channel_id=1, source_target_pairs={{0,24},{8,0},{16,8},{24,16},{1,25},{9,1},{17,9},{25,17},{2,26},{10... | collective-permute-start | bytes 1474568 | tf_op jit(solution)/shard_map/ppermute | solution.py:223
  73.6 0.1 bitcast_dynamic-update-slice_fusion.1
  73.8 0.1 bitcast_dynamic-update-slice_fusion
  73.9 9.2 %collective-permute-done.17 = bf16[2752,128]{1,0:T(8,128)(2,1)S(1)} collective-permute-done((bf16[2752,128]{1,0:T(8,128)(2,1)S(1)}, bf16[2752,128]{1,0:T(8,128)(2,1)S(1)}, u32[]{:S(2)}, u32[]{:S(2)}) %collective-permute-start.17) | collective-permute-done | bytes 704544 | tf_op jit(solution)/shard_map/ppermute | solution.py:223
  83.2 0.1 collective-permute-start.19
  83.2 0.4 collective-permute-done.18
  83.7 0.0 copy-start
  83.7 2.6 %collective-permute-start.20 = (bf16[4,1,160,128]{3,2,1,0:T(8,128)(2,1)S(1)}, bf16[4,1,160,128]{3,2,1,0:T(8,128)(2,1)S(1)}, u32[]{:S(2)}, u32[]{:S(2)}) collective-permute-start(bf16[4,1,160,128]{3,2,1,0:T(8,128)(2,1)S(1)} %slice.117), channel_id=1, source_target_pairs={{0,7},{1,0},{2,1},{3,2},{4,3},{5,4},{6,5},{7,6},{8,15},{9,8},{10,9... | collective-permute-start | bytes 491528 | tf_op jit(solution)/shard_map/ppermute | solution.py:223
  86.3 0.1 constant_dynamic-update-slice_fusion.5
  86.5 0.1 constant_dynamic-update-slice_fusion.4
  86.6 0.1 bitcast_dynamic-update-slice_fusion.7
  86.7 0.1 bitcast_dynamic-update-slice_fusion.6
  86.8 0.0 copy-start.3
  86.8 4.6 %shard_map.87 = (bf16[24,128,128]{2,1,0:T(8,128)(2,1)S(1)}, f32[26,128,128]{2,1,0:T(8,128)S(1)}) custom-call(s32[168]{0:T(256)S(1)} %reshape.49.codes, bf16[42,128,128]{2,1,0:T(8,128)(2,1)S(1)} %copy-done, bf16[32,480,128]{2,1,0:T(8,128)(2,1)S(1)} %bitcast.128), custom_call_target="tpu_custom_call" | custom-call | flops 503316480 | bytes 8388608 | tf_op jit(solution)/shard_map/pallas_call | solution.py:180
  91.5 7.5 %shard_map.88 = (bf16[42,128,128]{2,1,0:T(8,128)(2,1)}, bf16[8,128,128]{2,1,0:T(8,128)(2,1)S(1)}) custom-call(s32[168]{0:T(256)S(1)} %reshape.49.codes, s32[1]{0:T(128)} %bitcast.row.where, bf16[42,128,128]{2,1,0:T(8,128)(2,1)S(1)} %copy-done, bf16[128,128]{1,0:T(8,128)(2,1)S(1)} %bitcast.133, f32[26,128,128]{2,1,0:T(8,128)S(1)} %get-tuple-element.9.acc_in, ...), custom_call_target="tpu_custom_call" | custom-call | flops 528482304 | bytes 8388608 | tf_op jit(solution)/shard_map/pallas_call | solution.py:199
  99.0 15.0 %all_to_all.5 = bf16[8,128,128]{2,1,0:T(8,128)(2,1)S(1)} all-to-all(bf16[8,128,128]{2,1,0:T(8,128)(2,1)S(1)} %get-tuple-element.13), channel_id=1, replica_groups=mesh['x'=4,'core'=2,'y'=4,'z'=8] {'x','core'}, dimensions={0} | all-to-all | bytes 524288 | tf_op jit(solution)/shard_map/all_to_all | solution.py:309
  114.0 0.7 reduce_sum.12
  (60 shorter events, 1.1 us)
Async XLA Ops:
  0.6 0.9 copy-start.1
  1.6 0.8 copy-start.2
  2.3 0.7 copy-start.4
  3.0 0.7 copy-start.5
  4.1 12.5 %collective-permute-start = (bf16[880,128]{1,0:T(8,128)(2,1)S(1)}, bf16[880,128]{1,0:T(8,128)(2,1)S(1)}, u32[]{:S(2)}, u32[]{:S(2)}) collective-permute-start(bf16[880,128]{1,0:T(8,128)(2,1)S(1)} %shard_map.86), channel_id=1, source_target_pairs={{0,4},{1,5},{2,6},{3,7},{4,0},{5,1},{6,2},{7,3},{8,12},{9,13},{10,... | collective-permute-start | bytes 675848 | tf_op jit(solution)/shard_map/ppermute | solution.py:223
  16.6 13.2 %collective-permute-start.1 = (bf16[2,400,128]{2,1,0:T(8,128)(2,1)S(1)}, bf16[2,400,128]{2,1,0:T(8,128)(2,1)S(1)}, u32[]{:S(2)}, u32[]{:S(2)}) collective-permute-start(bf16[2,400,128]{2,1,0:T(8,128)(2,1)S(1)} %slice.96), channel_id=1, source_target_pairs={{0,8},{8,16},{16,24},{24,0},{1,9},{9,17},{17,25},{25,1},{2,10},{10... | collective-permute-start | bytes 614408 | tf_op jit(solution)/shard_map/ppermute | solution.py:223
  18.6 11.3 %collective-permute-start.2 = (bf16[2,400,128]{2,1,0:T(8,128)(2,1)S(1)}, bf16[2,400,128]{2,1,0:T(8,128)(2,1)S(1)}, u32[]{:S(2)}, u32[]{:S(2)}) collective-permute-start(bf16[2,400,128]{2,1,0:T(8,128)(2,1)S(1)} %slice.96), channel_id=1, source_target_pairs={{0,24},{8,0},{16,8},{24,16},{1,25},{9,1},{17,9},{25,17},{2,26},{10... | collective-permute-start | bytes 614408 | tf_op jit(solution)/shard_map/ppermute | solution.py:223
  20.1 9.8 %collective-permute-start.3 = (bf16[2,400,128]{2,1,0:T(8,128)(2,1)S(1)}, bf16[2,400,128]{2,1,0:T(8,128)(2,1)S(1)}, u32[]{:S(2)}, u32[]{:S(2)}) collective-permute-start(bf16[2,400,128]{2,1,0:T(8,128)(2,1)S(1)} %slice.96), channel_id=1, source_target_pairs={{0,16},{8,24},{16,0},{24,8},{1,17},{9,25},{17,1},{25,9},{2,18},{10... | collective-permute-start | bytes 614408 | tf_op jit(solution)/shard_map/ppermute | solution.py:223
  21.7 12.4 %collective-permute-start.4 = (bf16[2,480,128]{2,1,0:T(8,128)(2,1)S(1)}, bf16[2,480,128]{2,1,0:T(8,128)(2,1)S(1)}, u32[]{:S(2)}, u32[]{:S(2)}) collective-permute-start(bf16[2,480,128]{2,1,0:T(8,128)(2,1)S(1)} %slice.97), channel_id=1, source_target_pairs={{0,1},{1,2},{2,3},{3,4},{4,5},{5,6},{6,7},{7,0},{8,9},{9,10},{10,1... | collective-permute-start | bytes 737288 | tf_op jit(solution)/shard_map/ppermute | solution.py:223
  25.6 8.6 %collective-permute-start.5 = (bf16[2,480,128]{2,1,0:T(8,128)(2,1)S(1)}, bf16[2,480,128]{2,1,0:T(8,128)(2,1)S(1)}, u32[]{:S(2)}, u32[]{:S(2)}) collective-permute-start(bf16[2,480,128]{2,1,0:T(8,128)(2,1)S(1)} %slice.97), channel_id=1, source_target_pairs={{0,7},{1,0},{2,1},{3,2},{4,3},{5,4},{6,5},{7,6},{8,15},{9,8},{10,9... | collective-permute-start | bytes 737288 | tf_op jit(solution)/shard_map/ppermute | solution.py:223
  34.1 5.9 %collective-permute-start.6 = (bf16[1,480,128]{2,1,0:T(8,128)(2,1)S(1)}, bf16[1,480,128]{2,1,0:T(8,128)(2,1)S(1)}, u32[]{:S(2)}, u32[]{:S(2)}) collective-permute-start(bf16[1,480,128]{2,1,0:T(8,128)(2,1)S(1)} %slice.98), channel_id=1, source_target_pairs={{0,1},{1,2},{2,3},{3,4},{4,5},{5,6},{6,7},{7,0},{8,9},{9,10},{10,1... | collective-permute-start | bytes 368648 | tf_op jit(solution)/shard_map/ppermute | solution.py:223
  34.2 5.8 %collective-permute-start.7 = (bf16[1,480,128]{2,1,0:T(8,128)(2,1)S(1)}, bf16[1,480,128]{2,1,0:T(8,128)(2,1)S(1)}, u32[]{:S(2)}, u32[]{:S(2)}) collective-permute-start(bf16[1,480,128]{2,1,0:T(8,128)(2,1)S(1)} %slice.99), channel_id=1, source_target_pairs={{0,7},{1,0},{2,1},{3,2},{4,3},{5,4},{6,5},{7,6},{8,15},{9,8},{10,9... | collective-permute-start | bytes 368648 | tf_op jit(solution)/shard_map/ppermute | solution.py:223
  40.1 30.6 %collective-permute-start.8 = (bf16[2,4,480,128]{3,2,1,0:T(8,128)(2,1)S(1)}, bf16[2,4,480,128]{3,2,1,0:T(8,128)(2,1)S(1)}, u32[]{:S(2)}, u32[]{:S(2)}) collective-permute-start(bf16[2,4,480,128]{3,2,1,0:T(8,128)(2,1)S(1)} %bitcast_dynamic-update-slice_fusion.23), channel_id=1, source_target_pairs={{0,8},{8,16},{16,24},{24,0},{1,9},{9,17},{17,25},{25,1},{2,10},{10... | collective-permute-start | bytes 2949128 | tf_op jit(solution)/shard_map/ppermute | solution.py:223
  40.7 30.1 %collective-permute-start.9 = (bf16[2,4,480,128]{3,2,1,0:T(8,128)(2,1)S(1)}, bf16[2,4,480,128]{3,2,1,0:T(8,128)(2,1)S(1)}, u32[]{:S(2)}, u32[]{:S(2)}) collective-permute-start(bf16[2,4,480,128]{3,2,1,0:T(8,128)(2,1)S(1)} %bitcast_dynamic-update-slice_fusion.23), channel_id=1, source_target_pairs={{0,24},{8,0},{16,8},{24,16},{1,25},{9,1},{17,9},{25,17},{2,26},{10... | collective-permute-start | bytes 2949128 | tf_op jit(solution)/shard_map/ppermute | solution.py:223
  42.9 24.7 %collective-permute-start.12 = (bf16[4,2,368,128]{3,2,1,0:T(8,128)(2,1)S(1)}, bf16[4,2,368,128]{3,2,1,0:T(8,128)(2,1)S(1)}, u32[]{:S(2)}, u32[]{:S(2)}) collective-permute-start(bf16[4,2,368,128]{3,2,1,0:T(8,128)(2,1)S(1)} %slice.78), channel_id=1, source_target_pairs={{0,1},{1,2},{2,3},{3,4},{4,5},{5,6},{6,7},{7,0},{8,9},{9,10},{10,1... | collective-permute-start | bytes 2261000 | tf_op jit(solution)/shard_map/ppermute | solution.py:223
  43.3 24.3 %collective-permute-start.13 = (bf16[4,2,368,128]{3,2,1,0:T(8,128)(2,1)S(1)}, bf16[4,2,368,128]{3,2,1,0:T(8,128)(2,1)S(1)}, u32[]{:S(2)}, u32[]{:S(2)}) collective-permute-start(bf16[4,2,368,128]{3,2,1,0:T(8,128)(2,1)S(1)} %slice.78), channel_id=1, source_target_pairs={{0,7},{1,0},{2,1},{3,2},{4,3},{5,4},{6,5},{7,6},{8,15},{9,8},{10,9... | collective-permute-start | bytes 2261000 | tf_op jit(solution)/shard_map/ppermute | solution.py:223
  51.7 5.9 %collective-permute-start.14 = (bf16[2,4,2,32,128]{4,3,2,1,0:T(8,128)(2,1)S(1)}, bf16[2,4,2,32,128]{4,3,2,1,0:T(8,128)(2,1)S(1)}, u32[]{:S(2)}, u32[]{:S(2)}) collective-permute-start(bf16[2,4,2,32,128]{4,3,2,1,0:T(8,128)(2,1)S(1)} %bitcast.153), channel_id=1, source_target_pairs={{0,64},{64,128},{128,192},{192,0},{1,65},{65,129},{129,193},{193,1... | collective-permute-start | bytes 393224 | tf_op jit(solution)/shard_map/ppermute | solution.py:223
  57.7 4.1 %collective-permute-start.15 = (bf16[2,4,2,32,128]{4,3,2,1,0:T(8,128)(2,1)S(1)}, bf16[2,4,2,32,128]{4,3,2,1,0:T(8,128)(2,1)S(1)}, u32[]{:S(2)}, u32[]{:S(2)}) collective-permute-start(bf16[2,4,2,32,128]{4,3,2,1,0:T(8,128)(2,1)S(1)} %bitcast.155), channel_id=1, source_target_pairs={{0,192},{64,0},{128,64},{192,128},{1,193},{65,1},{129,65},{193,129... | collective-permute-start | bytes 393224 | tf_op jit(solution)/shard_map/ppermute | solution.py:223
  61.8 5.3 %collective-permute-start.16 = (bf16[2,4,2,32,128]{4,3,2,1,0:T(8,128)(2,1)S(1)}, bf16[2,4,2,32,128]{4,3,2,1,0:T(8,128)(2,1)S(1)}, u32[]{:S(2)}, u32[]{:S(2)}) collective-permute-start(bf16[2,4,2,32,128]{4,3,2,1,0:T(8,128)(2,1)S(1)} %bitcast.156), channel_id=1, source_target_pairs={{0,128},{64,192},{128,0},{192,64},{1,129},{65,193},{129,1},{193,65... | collective-permute-start | bytes 393224 | tf_op jit(solution)/shard_map/ppermute | solution.py:223
  67.7 15.4 %collective-permute-start.17 = (bf16[2752,128]{1,0:T(8,128)(2,1)S(1)}, bf16[2752,128]{1,0:T(8,128)(2,1)S(1)}, u32[]{:S(2)}, u32[]{:S(2)}) collective-permute-start(bf16[2752,128]{1,0:T(8,128)(2,1)S(1)} %get-tuple-element.15), channel_id=1, source_target_pairs={{0,1},{1,2},{2,3},{3,4},{4,5},{5,6},{6,7},{7,0},{8,9},{9,10},{10,1... | collective-permute-start | bytes 2113544 | tf_op jit(solution)/shard_map/ppermute | solution.py:223
  68.7 15.0 %collective-permute-start.18 = (bf16[2752,128]{1,0:T(8,128)(2,1)S(1)}, bf16[2752,128]{1,0:T(8,128)(2,1)S(1)}, u32[]{:S(2)}, u32[]{:S(2)}) collective-permute-start(bf16[2752,128]{1,0:T(8,128)(2,1)S(1)} %get-tuple-element.14), channel_id=1, source_target_pairs={{0,7},{1,0},{2,1},{3,2},{4,3},{5,4},{6,5},{7,6},{8,15},{9,8},{10,9... | collective-permute-start | bytes 2113544 | tf_op jit(solution)/shard_map/ppermute | solution.py:223
  70.8 15.8 %collective-permute-start.10 = (bf16[1,4,480,128]{3,2,1,0:T(8,128)(2,1)S(1)}, bf16[1,4,480,128]{3,2,1,0:T(8,128)(2,1)S(1)}, u32[]{:S(2)}, u32[]{:S(2)}) collective-permute-start(bf16[1,4,480,128]{3,2,1,0:T(8,128)(2,1)S(1)} %slice.100), channel_id=1, source_target_pairs={{0,8},{8,16},{16,24},{24,0},{1,9},{9,17},{17,25},{25,1},{2,10},{10... | collective-permute-start | bytes 1474568 | tf_op jit(solution)/shard_map/ppermute | solution.py:223
  70.9 15.8 %collective-permute-start.11 = (bf16[1,4,480,128]{3,2,1,0:T(8,128)(2,1)S(1)}, bf16[1,4,480,128]{3,2,1,0:T(8,128)(2,1)S(1)}, u32[]{:S(2)}, u32[]{:S(2)}) collective-permute-start(bf16[1,4,480,128]{3,2,1,0:T(8,128)(2,1)S(1)} %slice.101), channel_id=1, source_target_pairs={{0,24},{8,0},{16,8},{24,16},{1,25},{9,1},{17,9},{25,17},{2,26},{10... | collective-permute-start | bytes 1474568 | tf_op jit(solution)/shard_map/ppermute | solution.py:223
  83.2 8.2 %collective-permute-start.19 = (bf16[4,1,160,128]{3,2,1,0:T(8,128)(2,1)S(1)}, bf16[4,1,160,128]{3,2,1,0:T(8,128)(2,1)S(1)}, u32[]{:S(2)}, u32[]{:S(2)}) collective-permute-start(bf16[4,1,160,128]{3,2,1,0:T(8,128)(2,1)S(1)} %slice.116), channel_id=1, source_target_pairs={{0,1},{1,2},{2,3},{3,4},{4,5},{5,6},{6,7},{7,0},{8,9},{9,10},{10,1... | collective-permute-start | bytes 491528 | tf_op jit(solution)/shard_map/ppermute | solution.py:223
  83.7 3.1 %copy-start = (bf16[42,128,128]{2,1,0:T(8,128)(2,1)S(1)}, bf16[42,128,128]{2,1,0:T(8,128)(2,1)}, u32[]{:S(2)}) copy-start(bf16[42,128,128]{2,1,0:T(8,128)(2,1)} %rhs.3) | copy-start | bytes 4128772
  83.7 7.7 %collective-permute-start.20 = (bf16[4,1,160,128]{3,2,1,0:T(8,128)(2,1)S(1)}, bf16[4,1,160,128]{3,2,1,0:T(8,128)(2,1)S(1)}, u32[]{:S(2)}, u32[]{:S(2)}) collective-permute-start(bf16[4,1,160,128]{3,2,1,0:T(8,128)(2,1)S(1)} %slice.117), channel_id=1, source_target_pairs={{0,7},{1,0},{2,1},{3,2},{4,3},{5,4},{6,5},{7,6},{8,15},{9,8},{10,9... | collective-permute-start | bytes 491528 | tf_op jit(solution)/shard_map/ppermute | solution.py:223
  86.8 4.7 %copy-start.3 = (bf16[1,128,128]{2,1,0:T(8,128)(2,1)S(1)}, bf16[1,128,128]{2,1,0:T(8,128)(2,1)}, u32[]{:S(2)}) copy-start(bf16[1,128,128]{2,1,0:T(8,128)(2,1)} %param.8) | copy-start | bytes 98308

commit v6 on v3

--- a/solution.py
+++ b/solution.py
@@ -16,9 +16,9 @@
 FIRST = LEVELS[0][1]
 LATER = SUB - FIRST
 LATER_PAD = -(-LATER // 4) * 4
-LOW = tuple(k - k % 2 for k in range(TOP))
-START = tuple(sum(TOP - LOW[q] for q in range(k)) for k in range(TOP))
-TOP_BLOCKS = sum(TOP - low for low in LOW)
+WIDTH = tuple(t - t % 2 + 2 for t in range(TOP))
+START = tuple(sum(WIDTH[:t]) for t in range(TOP))
+TOP_BLOCKS = sum(WIDTH)
 LEAD_ROWS = FIRST * (1 + NB) * ROWS
 REST_ROWS = (LATER_PAD + LATER * NB + TOP_BLOCKS) * ROWS
 TOP_ROW = (LATER_PAD + LATER * NB) * ROWS
@@ -106,16 +106,42 @@
         own = jnp.where(where[0] == t, top_rhs[...].astype(F32), 0.0)
         base[t] = own - summed(acc, natural, SUB - FIRST + t)
     for k in range(TOP):
-        at = LATER_PAD + START[k] - LOW[k]
-        solved = jnp.dot(weights[at + k], base[k].astype(BF16), preferred_element_type=F32)
+        at = LATER_PAD + k
+        solved = jnp.dot(weights[at + START[k]], base[k].astype(BF16), preferred_element_type=F32)
         solved = solved.astype(BF16)
         part[k] = solved
-        if k + 1 < TOP:
-            below = weights[at + k + 1 : at + TOP].reshape((TOP - 1 - k) * B, B)
-            update = jnp.dot(below, solved, preferred_element_type=F32)
-            base[k + 1 :] = base[k + 1 :] - update.reshape(TOP - 1 - k, B, B)
+        for t in range(k + 1, TOP):
+            base[t] -= jnp.dot(weights[at + START[t]], solved, preferred_element_type=F32)
     for store in stores:
         store.wait()
+
+
+def pack_rows(row, diag, off, factor, inverse, lead, rest, own, factor_rows, inverse_rows, spread, sems):
+    lead_diag, lead_off = FIRST * ROWS, FIRST * GROUP
+    rest_diag, rest_off = LATER * ROWS, LATER * GROUP
+    rest_at = LATER_PAD * ROWS
+    copies = (
+        pltpu.make_async_copy(factor, factor_rows, sems.at[0]),
+        pltpu.make_async_copy(inverse, inverse_rows, sems.at[1]),
+        pltpu.make_async_copy(diag.at[pl.ds(0, lead_diag)], lead.at[pl.ds(0, lead_diag)], sems.at[2]),
+        pltpu.make_async_copy(off.at[pl.ds(0, lead_off)], lead.at[pl.ds(lead_diag, lead_off)], sems.at[3]),
+        pltpu.make_async_copy(diag.at[pl.ds(lead_diag, rest_diag)], rest.at[pl.ds(0, rest_diag)], sems.at[4]),
+        pltpu.make_async_copy(off.at[pl.ds(lead_off, rest_off)], rest.at[pl.ds(rest_at, rest_off)], sems.at[5]),
+    )
+    for copy in copies:
+        copy.start()
+    gap = (LATER_PAD - LATER) * ROWS
+    rest[pl.ds(rest_at - gap, gap), :] = jnp.zeros((gap, B), BF16)
+    copies[0].wait()
+    copies[1].wait()
+    for i in range(ROWS):
+        line = inverse_rows[...].astype(F32)[i : i + 1]
+        spread[pl.ds(i, TOP, stride=ROWS), :] = jnp.broadcast_to(line, (TOP, B))
+    block = lax.broadcasted_iota(jnp.int32, (TOP * ROWS, B), 0) // ROWS
+    top = jnp.where(block == row[0], spread[...], factor_rows[...].astype(F32))
+    own[...] = top.astype(BF16)
+    for copy in copies[2:]:
+        copy.wait()
 
 
 VMEM = pl.BlockSpec(memory_space=pltpu.VMEM)
@@ -130,6 +156,25 @@
 
 def cost(blocks, nbytes):
     return pl.CostEstimate(flops=2 * B**3 * blocks, bytes_accessed=nbytes, transcendentals=0)
+
+
+def run_pack(row, diag, off, factor, inverse):
+    return pl.pallas_call(
+        pack_rows,
+        out_shape=[
+            jax.ShapeDtypeStruct((rows, B), BF16) for rows in (LEAD_ROWS, TOP_ROW, TOP * ROWS)
+        ],
+        in_specs=[SMEM] + [HBM] * 4,
+        out_specs=[VMEM] * 3,
+        scratch_shapes=[
+            pltpu.VMEM((TOP * ROWS, B), BF16),
+            pltpu.VMEM((ROWS, B), BF16),
+            pltpu.VMEM((TOP * ROWS, B), F32),
+            pltpu.SemaphoreType.DMA((6,)),
+        ],
+        compiler_params=pltpu.CompilerParams(vmem_limit_bytes=56 << 20),
+        cost_estimate=cost(0, 1 << 19),
+    )(row, diag, off, factor, inverse)
 
 
 def run_leaves(codes, rhs, lead):
@@ -229,20 +274,15 @@
 
 def local(local_rhs, top_rhs, diag_inv, top_inv, off_blocks, top_factor, targets):
     position = lax.axis_index(ROW)
-    diag, off = diag_inv.reshape(-1, B), off_blocks.reshape(-1, B)
-    own = (jnp.arange(TOP) == position)[:, None, None]
-    top_all = gather_row(jnp.where(own, top_inv, top_factor[0]))
-    top_rows = jnp.concatenate([top_all[LOW[k] :, k] for k in range(TOP)], axis=0)
-    lead = jnp.concatenate([diag[: FIRST * ROWS], off[: FIRST * GROUP]], axis=0)
-    rest = jnp.concatenate(
-        [
-            diag[FIRST * ROWS :],
-            jnp.zeros(((LATER_PAD - LATER) * ROWS, B), BF16),
-            off[FIRST * GROUP :],
-            top_rows.reshape(-1, B),
-        ],
-        axis=0,
-    )
+    lead, rest, top_rows = run_pack(
+        position[None],
+        diag_inv.reshape(-1, B),
+        off_blocks.reshape(-1, B),
+        top_factor.reshape(-1, B),
+        top_inv.reshape(-1, B),
+    )
+    top_all = gather_row(top_rows)
+    rest = jnp.concatenate([rest, *(top_all[t, : WIDTH[t] * ROWS] for t in range(TOP))], axis=0)
     lead_all = gather_z_then_y(lead)
     rest_all = gather_y_then_z(rest)
     codes = targets.reshape(-1)

time: 109 us -> 108 us (level)
  local copies, waits for them, and re-layouts: 7.44 us -> 5.64 us
  Pallas kernels: 12.1 us -> 13.7 us
  other arithmetic: 1.77 us -> 0.65 us
    slice x8 -> x0, local copies, waits for them, and re-layouts: 3.41 us -> none  [the longest x2 1.68 us: local(): lead = jnp.concatenate([diag[:FIRST * ROWS], off[:FIRST * GROUP]], axis=0)]
    pallas_call x0 -> x1, Pallas kernels: none -> 1.73 us  [run_pack(): pl.pallas_call(pack_rows, out_shape=[jax.ShapeDtypeStruct((rows, B), BF16...]
    dynamic_update_slice x28 -> x30, local copies, waits for them, and re-layouts: 1.39 us -> 2.34 us  [put(): return lax.dynamic_update_slice(buffer, x.reshape(shape), start)]
  transfers between devices with their start and end apart: 25 -> 25, of which waited for: 7 -> 7; matrix products, arithmetic and copies ran while one was open for 6% -> 5% of each run, Pallas kernels for 4% -> 4%
where the time goes in v6:
time: 108 us
  starting transfers between devices  37.4 us (35%)
  waiting for transfers between devices  31.8 us (29%)
  blocking collectives  17.4 us (16%)
  Pallas kernels  13.7 us (13%)
  local copies, waits for them, and re-layouts  5.64 us (5%)
  between operations  1.44 us (1%)
    ppermute x25, starting transfers between devices, shift(): return lax.ppermute(x, axis, [(n, (n + k) % size) for n in range(size)])  37.4 us
    ppermute x25, waiting for transfers between devices, shift(): return lax.ppermute(x, axis, [(n, (n + k) % size) for n in range(size)])  31.8 us
    all_to_all x1, blocking collectives, local(): parts = lax.all_to_all(addends, ROW, 0, 0, tiled=True)  14.7 us
    pallas_call x1, Pallas kernels, run_later(): pl.pallas_call(later_levels, out_shape=(jax.ShapeDtypeStruct((SUB, B, B),...  7.46 us
    pallas_call x1, Pallas kernels, run_leaves(): pl.pallas_call(leaf_level, out_shape=(jax.ShapeDtypeStruct((FIRST, B, B),...  4.48 us
    all_gather x1, blocking collectives, gather_row(): pair = lax.all_gather(x, 'core', axis=0)  2.64 us
    dynamic_update_slice x30, local copies, waits for them, and re-layouts, put(): return lax.dynamic_update_slice(buffer, x.reshape(shape), start)  2.34 us
  transfers between devices with their start and end apart: 25, of which 7 were waited for; matrix products, arithmetic and copies ran while one was open for 5% of the time, Pallas kernels for 4%

profile of v6, /device:TPU:1, one launch (start us, length us, event | category | flops | bytes accessed | tf_op | source)
XLA Modules:
  0.0 108.0 jit_solution(5755711877950877556)
XLA Ops:
  0.6 1.7 %shard_map.86 = (bf16[480,128]{1,0:T(8,128)(2,1)}, bf16[368,128]{1,0:T(8,128)(2,1)}, bf16[32,128]{1,0:T(8,128)(2,1)}) custom-call(s32[1]{0:T(128)} %bitcast.row.where, bf16[168,128]{1,0:T(8,128)(2,1)} %bitcast.134, bf16[672,128]{1,0:T(8,128)(2,1)} %bitcast.129, bf16[32,128]{1,0:T(8,128)(2,1)} %bitcast.136, bf16[4,128]{1,0:T(4,128)(2,1)} %bitcast.137), custom_call_target="tpu_custom_call" | custom-call | bytes 524288 | tf_op jit(solution)/shard_map/pallas_call | solution.py:162
  2.4 2.5 %collective-permute-start = (bf16[480,128]{1,0:T(8,128)(2,1)}, bf16[480,128]{1,0:T(8,128)(2,1)S(1)}, u32[]{:S(2)}, u32[]{:S(2)}) collective-permute-start(bf16[480,128]{1,0:T(8,128)(2,1)} %get-tuple-element.9), channel_id=1, source_target_pairs={{0,1},{1,2},{2,3},{3,4},{4,5},{5,6},{6,7},{7,0},{8,9},{9,10},{10,1... | collective-permute-start | bytes 368648 | tf_op jit(solution)/shard_map/ppermute | solution.py:224
  4.9 4.0 %collective-permute-start.1 = (bf16[480,128]{1,0:T(8,128)(2,1)}, bf16[480,128]{1,0:T(8,128)(2,1)S(1)}, u32[]{:S(2)}, u32[]{:S(2)}) collective-permute-start(bf16[480,128]{1,0:T(8,128)(2,1)} %get-tuple-element.9), channel_id=1, source_target_pairs={{0,7},{1,0},{2,1},{3,2},{4,3},{5,4},{6,5},{7,6},{8,15},{9,8},{10,9... | collective-permute-start | bytes 368648 | tf_op jit(solution)/shard_map/ppermute | solution.py:224
  9.0 2.6 %all-gather = bf16[64,128]{1,0:T(8,128)(2,1)S(1)} all-gather(bf16[32,128]{1,0:T(8,128)(2,1)} %get-tuple-element.13), channel_id=2, replica_groups=mesh['x'=4,'core'=2,'y'=4,'z'=8] {'core'}, dimensions={0}, use_global_device_ids=true | all-gather | bytes 24576 | tf_op jit(solution)/shard_map/all_gather | solution.py:268
  11.6 1.2 %collective-permute-start.11 = (bf16[2,32,128]{2,1,0:T(8,128)(2,1)S(1)}, bf16[2,32,128]{2,1,0:T(8,128)(2,1)S(1)}, u32[]{:S(2)}, u32[]{:S(2)}) collective-permute-start(bf16[2,32,128]{2,1,0:T(8,128)(2,1)S(1)} %bitcast.130), channel_id=1, source_target_pairs={{0,64},{64,128},{128,192},{192,0},{1,65},{65,129},{129,193},{193,1... | collective-permute-start | bytes 49160 | tf_op jit(solution)/shard_map/ppermute | solution.py:224
  12.8 1.5 %collective-permute-start.12 = (bf16[2,32,128]{2,1,0:T(8,128)(2,1)S(1)}, bf16[2,32,128]{2,1,0:T(8,128)(2,1)S(1)}, u32[]{:S(2)}, u32[]{:S(2)}) collective-permute-start(bf16[2,32,128]{2,1,0:T(8,128)(2,1)S(1)} %bitcast.131), channel_id=1, source_target_pairs={{0,192},{64,0},{128,64},{192,128},{1,193},{65,1},{129,65},{193,129... | collective-permute-start | bytes 49160 | tf_op jit(solution)/shard_map/ppermute | solution.py:224
  14.3 1.5 %collective-permute-start.13 = (bf16[2,32,128]{2,1,0:T(8,128)(2,1)S(1)}, bf16[2,32,128]{2,1,0:T(8,128)(2,1)S(1)}, u32[]{:S(2)}, u32[]{:S(2)}) collective-permute-start(bf16[2,32,128]{2,1,0:T(8,128)(2,1)S(1)} %bitcast.132), channel_id=1, source_target_pairs={{0,128},{64,192},{128,0},{192,64},{1,129},{65,193},{129,1},{193,65... | collective-permute-start | bytes 49160 | tf_op jit(solution)/shard_map/ppermute | solution.py:224
  15.8 0.9 constant_dynamic-update-slice_fusion.8
  16.7 0.1 broadcast_in_dim.55
  16.8 0.9 bitcast_dynamic-update-slice_fusion.25
  18.0 0.8 copy.17
  18.8 0.1 reshape.94.codes
  19.0 0.0 collective-permute-done.11
  19.0 0.0 collective-permute-done.13
  19.2 1.4 %collective-permute-start.14 = (bf16[528,128]{1,0:T(8,128)(2,1)S(1)}, bf16[528,128]{1,0:T(8,128)(2,1)S(1)}, u32[]{:S(2)}, u32[]{:S(2)}) collective-permute-start(bf16[528,128]{1,0:T(8,128)(2,1)S(1)} %constant_dynamic-update-slice_fusion), channel_id=1, source_target_pairs={{0,8},{8,16},{16,24},{24,0},{1,9},{9,17},{17,25},{25,1},{2,10},{10... | collective-permute-start | bytes 405512 | tf_op jit(solution)/shard_map/ppermute | solution.py:224
  20.5 1.5 %collective-permute-start.15 = (bf16[528,128]{1,0:T(8,128)(2,1)S(1)}, bf16[528,128]{1,0:T(8,128)(2,1)S(1)}, u32[]{:S(2)}, u32[]{:S(2)}) collective-permute-start(bf16[528,128]{1,0:T(8,128)(2,1)S(1)} %constant_dynamic-update-slice_fusion), channel_id=1, source_target_pairs={{0,24},{8,0},{16,8},{24,16},{1,25},{9,1},{17,9},{25,17},{2,26},{10... | collective-permute-start | bytes 405512 | tf_op jit(solution)/shard_map/ppermute | solution.py:224
  22.1 1.6 %collective-permute-start.16 = (bf16[528,128]{1,0:T(8,128)(2,1)S(1)}, bf16[528,128]{1,0:T(8,128)(2,1)S(1)}, u32[]{:S(2)}, u32[]{:S(2)}) collective-permute-start(bf16[528,128]{1,0:T(8,128)(2,1)S(1)} %constant_dynamic-update-slice_fusion), channel_id=1, source_target_pairs={{0,16},{8,24},{16,0},{24,8},{1,17},{9,25},{17,1},{25,9},{2,18},{10... | collective-permute-start | bytes 405512 | tf_op jit(solution)/shard_map/ppermute | solution.py:224
  23.6 0.1 broadcast_in_dim.59
  23.7 0.0 collective-permute-done
  23.7 0.1 collective-permute-start.2
  23.8 0.0 collective-permute-done.1
  23.8 2.7 %collective-permute-start.3 = (bf16[480,128]{1,0:T(8,128)(2,1)S(1)}, bf16[480,128]{1,0:T(8,128)(2,1)S(1)}, u32[]{:S(2)}, u32[]{:S(2)}) collective-permute-start(bf16[480,128]{1,0:T(8,128)(2,1)S(1)} %collective-permute-done.1), channel_id=1, source_target_pairs={{0,7},{1,0},{2,1},{3,2},{4,3},{5,4},{6,5},{7,6},{8,15},{9,8},{10,9... | collective-permute-start | bytes 368648 | tf_op jit(solution)/shard_map/ppermute | solution.py:224
  26.6 0.0 collective-permute-done.14
  26.6 2.5 %collective-permute-done.16 = bf16[528,128]{1,0:T(8,128)(2,1)S(1)} collective-permute-done((bf16[528,128]{1,0:T(8,128)(2,1)S(1)}, bf16[528,128]{1,0:T(8,128)(2,1)S(1)}, u32[]{:S(2)}, u32[]{:S(2)}) %collective-permute-start.16) | collective-permute-done | bytes 135200 | tf_op jit(solution)/shard_map/ppermute | solution.py:224
  29.2 0.1 collective-permute-start.17
  29.3 2.7 %collective-permute-start.18 = (bf16[4,528,128]{2,1,0:T(8,128)(2,1)S(1)}, bf16[4,528,128]{2,1,0:T(8,128)(2,1)S(1)}, u32[]{:S(2)}, u32[]{:S(2)}) collective-permute-start(bf16[4,528,128]{2,1,0:T(8,128)(2,1)S(1)} %bitcast_dynamic-update-slice_fusion.14), channel_id=1, source_target_pairs={{0,7},{1,0},{2,1},{3,2},{4,3},{5,4},{6,5},{7,6},{8,15},{9,8},{10,9... | collective-permute-start | bytes 1622024 | tf_op jit(solution)/shard_map/ppermute | solution.py:224
  32.0 0.6 broadcast_in_dim.58
  32.5 0.1 bitcast_dynamic-update-slice_fusion.9
  32.6 0.1 collective-permute-start.4
  32.7 0.0 collective-permute-done.3
  32.7 2.7 %collective-permute-start.5 = (bf16[480,128]{1,0:T(8,128)(2,1)S(1)}, bf16[480,128]{1,0:T(8,128)(2,1)S(1)}, u32[]{:S(2)}, u32[]{:S(2)}) collective-permute-start(bf16[480,128]{1,0:T(8,128)(2,1)S(1)} %collective-permute-done.3), channel_id=1, source_target_pairs={{0,7},{1,0},{2,1},{3,2},{4,3},{5,4},{6,5},{7,6},{8,15},{9,8},{10,9... | collective-permute-start | bytes 368648 | tf_op jit(solution)/shard_map/ppermute | solution.py:224
  35.4 9.7 %collective-permute-done.4 = bf16[480,128]{1,0:T(8,128)(2,1)S(1)} collective-permute-done((bf16[480,128]{1,0:T(8,128)(2,1)S(1)}, bf16[480,128]{1,0:T(8,128)(2,1)S(1)}, u32[]{:S(2)}, u32[]{:S(2)}) %collective-permute-start.4) | collective-permute-done | bytes 122912 | tf_op jit(solution)/shard_map/ppermute | solution.py:224
  45.1 0.0 collective-permute-start.6
  45.2 4.9 %collective-permute-done.6 = bf16[480,128]{1,0:T(8,128)(2,1)S(1)} collective-permute-done((bf16[480,128]{1,0:T(8,128)(2,1)S(1)}, bf16[480,128]{1,0:T(8,128)(2,1)S(1)}, u32[]{:S(2)}, u32[]{:S(2)}) %collective-permute-start.6) | collective-permute-done | bytes 122912 | tf_op jit(solution)/shard_map/ppermute | solution.py:224
  50.1 0.1 collective-permute-start.7
  50.1 2.7 %collective-permute-start.8 = (bf16[8,480,128]{2,1,0:T(8,128)(2,1)S(1)}, bf16[8,480,128]{2,1,0:T(8,128)(2,1)S(1)}, u32[]{:S(2)}, u32[]{:S(2)}) collective-permute-start(bf16[8,480,128]{2,1,0:T(8,128)(2,1)S(1)} %bitcast_dynamic-update-slice_fusion.18), channel_id=1, source_target_pairs={{0,24},{8,0},{16,8},{24,16},{1,25},{9,1},{17,9},{25,17},{2,26},{10... | collective-permute-start | bytes 2949128 | tf_op jit(solution)/shard_map/ppermute | solution.py:224
  52.8 2.7 %collective-permute-start.20 = (bf16[4,528,128]{2,1,0:T(8,128)(2,1)S(1)}, bf16[4,528,128]{2,1,0:T(8,128)(2,1)S(1)}, u32[]{:S(2)}, u32[]{:S(2)}) collective-permute-start(bf16[4,528,128]{2,1,0:T(8,128)(2,1)S(1)} %collective-permute-done.18), channel_id=1, source_target_pairs={{0,7},{1,0},{2,1},{3,2},{4,3},{5,4},{6,5},{7,6},{8,15},{9,8},{10,9... | collective-permute-start | bytes 1622024 | tf_op jit(solution)/shard_map/ppermute | solution.py:224
  55.5 0.6 broadcast_in_dim.54
  56.1 0.1 bitcast_dynamic-update-slice_fusion.2
  56.2 0.1 bitcast_dynamic-update-slice_fusion.8
  56.3 0.1 bitcast_dynamic-update-slice_fusion.7
  56.4 7.0 %collective-permute-done.19 = bf16[4,528,128]{2,1,0:T(8,128)(2,1)S(1)} collective-permute-done((bf16[4,528,128]{2,1,0:T(8,128)(2,1)S(1)}, bf16[4,528,128]{2,1,0:T(8,128)(2,1)S(1)}, u32[]{:S(2)}, u32[]{:S(2)}) %collective-permute-start.19) | collective-permute-done | bytes 540704 | tf_op jit(solution)/shard_map/ppermute | solution.py:224
  63.4 2.7 %collective-permute-start.22 = (bf16[4,528,128]{2,1,0:T(8,128)(2,1)S(1)}, bf16[4,528,128]{2,1,0:T(8,128)(2,1)S(1)}, u32[]{:S(2)}, u32[]{:S(2)}) collective-permute-start(bf16[4,528,128]{2,1,0:T(8,128)(2,1)S(1)} %collective-permute-done.20), channel_id=1, source_target_pairs={{0,7},{1,0},{2,1},{3,2},{4,3},{5,4},{6,5},{7,6},{8,15},{9,8},{10,9... | collective-permute-start | bytes 1622024 | tf_op jit(solution)/shard_map/ppermute | solution.py:224
  66.0 0.1 bitcast_dynamic-update-slice_fusion.6
  66.1 0.1 bitcast_dynamic-update-slice_fusion.5
  66.2 4.5 %collective-permute-done.7 = bf16[8,480,128]{2,1,0:T(8,128)(2,1)S(1)} collective-permute-done((bf16[8,480,128]{2,1,0:T(8,128)(2,1)S(1)}, bf16[8,480,128]{2,1,0:T(8,128)(2,1)S(1)}, u32[]{:S(2)}, u32[]{:S(2)}) %collective-permute-start.7) | collective-permute-done | bytes 983072 | tf_op jit(solution)/shard_map/ppermute | solution.py:224
  70.7 0.1 collective-permute-start.9
  70.9 0.0 copy-start
  70.9 2.7 %collective-permute-start.10 = (bf16[4,480,128]{2,1,0:T(8,128)(2,1)S(1)}, bf16[4,480,128]{2,1,0:T(8,128)(2,1)S(1)}, u32[]{:S(2)}, u32[]{:S(2)}) collective-permute-start(bf16[4,480,128]{2,1,0:T(8,128)(2,1)S(1)} %slice.49), channel_id=1, source_target_pairs={{0,24},{8,0},{16,8},{24,16},{1,25},{9,1},{17,9},{25,17},{2,26},{10... | collective-permute-start | bytes 1474568 | tf_op jit(solution)/shard_map/ppermute | solution.py:224
  73.6 0.1 bitcast_dynamic-update-slice_fusion.1
  73.8 0.1 bitcast_dynamic-update-slice_fusion
  73.9 0.2 collective-permute-done.21
  74.1 0.1 collective-permute-start.23
  74.3 2.9 %collective-permute-start.24 = (bf16[2,528,128]{2,1,0:T(8,128)(2,1)S(1)}, bf16[2,528,128]{2,1,0:T(8,128)(2,1)S(1)}, u32[]{:S(2)}, u32[]{:S(2)}) collective-permute-start(bf16[2,528,128]{2,1,0:T(8,128)(2,1)S(1)} %slice.59), channel_id=1, source_target_pairs={{0,7},{1,0},{2,1},{3,2},{4,3},{5,4},{6,5},{7,6},{8,15},{9,8},{10,9... | collective-permute-start | bytes 811016 | tf_op jit(solution)/shard_map/ppermute | solution.py:224
  77.2 0.1 bitcast_dynamic-update-slice_fusion.4
  77.3 0.1 bitcast_dynamic-update-slice_fusion.3
  77.4 0.0 copy-start.1
  77.4 3.0 %collective-permute-done.9 = bf16[4,480,128]{2,1,0:T(8,128)(2,1)S(1)} collective-permute-done((bf16[4,480,128]{2,1,0:T(8,128)(2,1)S(1)}, bf16[4,480,128]{2,1,0:T(8,128)(2,1)S(1)}, u32[]{:S(2)}, u32[]{:S(2)}) %collective-permute-start.9) | collective-permute-done | bytes 491552 | tf_op jit(solution)/shard_map/ppermute | solution.py:224
  80.4 0.1 bitcast_dynamic-update-slice_fusion.11
  80.5 0.1 bitcast_dynamic-update-slice_fusion.10
  80.6 4.5 %shard_map.87 = (bf16[24,128,128]{2,1,0:T(8,128)(2,1)S(1)}, f32[26,128,128]{2,1,0:T(8,128)S(1)}) custom-call(s32[168]{0:T(256)S(1)} %reshape.94.codes, bf16[42,128,128]{2,1,0:T(8,128)(2,1)S(1)} %copy-done, bf16[32,480,128]{2,1,0:T(8,128)(2,1)S(1)} %bitcast.119), custom_call_target="tpu_custom_call" | custom-call | flops 503316480 | bytes 8388608 | tf_op jit(solution)/shard_map/pallas_call | solution.py:181
  85.2 7.5 %shard_map.88 = (bf16[42,128,128]{2,1,0:T(8,128)(2,1)}, bf16[8,128,128]{2,1,0:T(8,128)(2,1)S(1)}) custom-call(s32[168]{0:T(256)S(1)} %reshape.94.codes, s32[1]{0:T(128)} %bitcast.row.where, bf16[42,128,128]{2,1,0:T(8,128)(2,1)S(1)} %copy-done, bf16[128,128]{1,0:T(8,128)(2,1)S(1)} %bitcast.120, f32[26,128,128]{2,1,0:T(8,128)S(1)} %get-tuple-element.10.acc_in, ...), custom_call_target="tpu_custom_call" | custom-call | flops 528482304 | bytes 8388608 | tf_op jit(solution)/shard_map/pallas_call | solution.py:200
  92.6 14.7 %all_to_all.5 = bf16[8,128,128]{2,1,0:T(8,128)(2,1)S(1)} all-to-all(bf16[8,128,128]{2,1,0:T(8,128)(2,1)S(1)} %get-tuple-element.15), channel_id=1, replica_groups=mesh['x'=4,'core'=2,'y'=4,'z'=8] {'x','core'}, dimensions={0} | all-to-all | bytes 524288 | tf_op jit(solution)/shard_map/all_to_all | solution.py:291
  107.3 0.7 reduce_sum.12
  (46 shorter events, 0.6 us)
Async XLA Ops:
  2.4 21.4 %collective-permute-start = (bf16[480,128]{1,0:T(8,128)(2,1)}, bf16[480,128]{1,0:T(8,128)(2,1)S(1)}, u32[]{:S(2)}, u32[]{:S(2)}) collective-permute-start(bf16[480,128]{1,0:T(8,128)(2,1)} %get-tuple-element.9), channel_id=1, source_target_pairs={{0,1},{1,2},{2,3},{3,4},{4,5},{5,6},{6,7},{7,0},{8,9},{9,10},{10,1... | collective-permute-start | bytes 368648 | tf_op jit(solution)/shard_map/ppermute | solution.py:224
  4.9 18.9 %collective-permute-start.1 = (bf16[480,128]{1,0:T(8,128)(2,1)}, bf16[480,128]{1,0:T(8,128)(2,1)S(1)}, u32[]{:S(2)}, u32[]{:S(2)}) collective-permute-start(bf16[480,128]{1,0:T(8,128)(2,1)} %get-tuple-element.9), channel_id=1, source_target_pairs={{0,7},{1,0},{2,1},{3,2},{4,3},{5,4},{6,5},{7,6},{8,15},{9,8},{10,9... | collective-permute-start | bytes 368648 | tf_op jit(solution)/shard_map/ppermute | solution.py:224
  11.6 7.4 %collective-permute-start.11 = (bf16[2,32,128]{2,1,0:T(8,128)(2,1)S(1)}, bf16[2,32,128]{2,1,0:T(8,128)(2,1)S(1)}, u32[]{:S(2)}, u32[]{:S(2)}) collective-permute-start(bf16[2,32,128]{2,1,0:T(8,128)(2,1)S(1)} %bitcast.130), channel_id=1, source_target_pairs={{0,64},{64,128},{128,192},{192,0},{1,65},{65,129},{129,193},{193,1... | collective-permute-start | bytes 49160 | tf_op jit(solution)/shard_map/ppermute | solution.py:224
  12.8 6.2 %collective-permute-start.12 = (bf16[2,32,128]{2,1,0:T(8,128)(2,1)S(1)}, bf16[2,32,128]{2,1,0:T(8,128)(2,1)S(1)}, u32[]{:S(2)}, u32[]{:S(2)}) collective-permute-start(bf16[2,32,128]{2,1,0:T(8,128)(2,1)S(1)} %bitcast.131), channel_id=1, source_target_pairs={{0,192},{64,0},{128,64},{192,128},{1,193},{65,1},{129,65},{193,129... | collective-permute-start | bytes 49160 | tf_op jit(solution)/shard_map/ppermute | solution.py:224
  14.3 4.8 %collective-permute-start.13 = (bf16[2,32,128]{2,1,0:T(8,128)(2,1)S(1)}, bf16[2,32,128]{2,1,0:T(8,128)(2,1)S(1)}, u32[]{:S(2)}, u32[]{:S(2)}) collective-permute-start(bf16[2,32,128]{2,1,0:T(8,128)(2,1)S(1)} %bitcast.132), channel_id=1, source_target_pairs={{0,128},{64,192},{128,0},{192,64},{1,129},{65,193},{129,1},{193,65... | collective-permute-start | bytes 49160 | tf_op jit(solution)/shard_map/ppermute | solution.py:224
  19.2 7.4 %collective-permute-start.14 = (bf16[528,128]{1,0:T(8,128)(2,1)S(1)}, bf16[528,128]{1,0:T(8,128)(2,1)S(1)}, u32[]{:S(2)}, u32[]{:S(2)}) collective-permute-start(bf16[528,128]{1,0:T(8,128)(2,1)S(1)} %constant_dynamic-update-slice_fusion), channel_id=1, source_target_pairs={{0,8},{8,16},{16,24},{24,0},{1,9},{9,17},{17,25},{25,1},{2,10},{10... | collective-permute-start | bytes 405512 | tf_op jit(solution)/shard_map/ppermute | solution.py:224
  20.5 6.1 %collective-permute-start.15 = (bf16[528,128]{1,0:T(8,128)(2,1)S(1)}, bf16[528,128]{1,0:T(8,128)(2,1)S(1)}, u32[]{:S(2)}, u32[]{:S(2)}) collective-permute-start(bf16[528,128]{1,0:T(8,128)(2,1)S(1)} %constant_dynamic-update-slice_fusion), channel_id=1, source_target_pairs={{0,24},{8,0},{16,8},{24,16},{1,25},{9,1},{17,9},{25,17},{2,26},{10... | collective-permute-start | bytes 405512 | tf_op jit(solution)/shard_map/ppermute | solution.py:224
  22.1 7.1 %collective-permute-start.16 = (bf16[528,128]{1,0:T(8,128)(2,1)S(1)}, bf16[528,128]{1,0:T(8,128)(2,1)S(1)}, u32[]{:S(2)}, u32[]{:S(2)}) collective-permute-start(bf16[528,128]{1,0:T(8,128)(2,1)S(1)} %constant_dynamic-update-slice_fusion), channel_id=1, source_target_pairs={{0,16},{8,24},{16,0},{24,8},{1,17},{9,25},{17,1},{25,9},{2,18},{10... | collective-permute-start | bytes 405512 | tf_op jit(solution)/shard_map/ppermute | solution.py:224
  23.7 8.9 %collective-permute-start.2 = (bf16[480,128]{1,0:T(8,128)(2,1)S(1)}, bf16[480,128]{1,0:T(8,128)(2,1)S(1)}, u32[]{:S(2)}, u32[]{:S(2)}) collective-permute-start(bf16[480,128]{1,0:T(8,128)(2,1)S(1)} %collective-permute-done), channel_id=1, source_target_pairs={{0,1},{1,2},{2,3},{3,4},{4,5},{5,6},{6,7},{7,0},{8,9},{9,10},{10,1... | collective-permute-start | bytes 368648 | tf_op jit(solution)/shard_map/ppermute | solution.py:224
  23.8 8.9 %collective-permute-start.3 = (bf16[480,128]{1,0:T(8,128)(2,1)S(1)}, bf16[480,128]{1,0:T(8,128)(2,1)S(1)}, u32[]{:S(2)}, u32[]{:S(2)}) collective-permute-start(bf16[480,128]{1,0:T(8,128)(2,1)S(1)} %collective-permute-done.1), channel_id=1, source_target_pairs={{0,7},{1,0},{2,1},{3,2},{4,3},{5,4},{6,5},{7,6},{8,15},{9,8},{10,9... | collective-permute-start | bytes 368648 | tf_op jit(solution)/shard_map/ppermute | solution.py:224
  29.2 23.6 %collective-permute-start.17 = (bf16[4,528,128]{2,1,0:T(8,128)(2,1)S(1)}, bf16[4,528,128]{2,1,0:T(8,128)(2,1)S(1)}, u32[]{:S(2)}, u32[]{:S(2)}) collective-permute-start(bf16[4,528,128]{2,1,0:T(8,128)(2,1)S(1)} %bitcast_dynamic-update-slice_fusion.14), channel_id=1, source_target_pairs={{0,1},{1,2},{2,3},{3,4},{4,5},{5,6},{6,7},{7,0},{8,9},{9,10},{10,1... | collective-permute-start | bytes 1622024 | tf_op jit(solution)/shard_map/ppermute | solution.py:224
  29.3 23.5 %collective-permute-start.18 = (bf16[4,528,128]{2,1,0:T(8,128)(2,1)S(1)}, bf16[4,528,128]{2,1,0:T(8,128)(2,1)S(1)}, u32[]{:S(2)}, u32[]{:S(2)}) collective-permute-start(bf16[4,528,128]{2,1,0:T(8,128)(2,1)S(1)} %bitcast_dynamic-update-slice_fusion.14), channel_id=1, source_target_pairs={{0,7},{1,0},{2,1},{3,2},{4,3},{5,4},{6,5},{7,6},{8,15},{9,8},{10,9... | collective-permute-start | bytes 1622024 | tf_op jit(solution)/shard_map/ppermute | solution.py:224
  32.6 12.5 %collective-permute-start.4 = (bf16[480,128]{1,0:T(8,128)(2,1)S(1)}, bf16[480,128]{1,0:T(8,128)(2,1)S(1)}, u32[]{:S(2)}, u32[]{:S(2)}) collective-permute-start(bf16[480,128]{1,0:T(8,128)(2,1)S(1)} %collective-permute-done.2), channel_id=1, source_target_pairs={{0,1},{1,2},{2,3},{3,4},{4,5},{5,6},{6,7},{7,0},{8,9},{9,10},{10,1... | collective-permute-start | bytes 368648 | tf_op jit(solution)/shard_map/ppermute | solution.py:224
  32.7 12.4 %collective-permute-start.5 = (bf16[480,128]{1,0:T(8,128)(2,1)S(1)}, bf16[480,128]{1,0:T(8,128)(2,1)S(1)}, u32[]{:S(2)}, u32[]{:S(2)}) collective-permute-start(bf16[480,128]{1,0:T(8,128)(2,1)S(1)} %collective-permute-done.3), channel_id=1, source_target_pairs={{0,7},{1,0},{2,1},{3,2},{4,3},{5,4},{6,5},{7,6},{8,15},{9,8},{10,9... | collective-permute-start | bytes 368648 | tf_op jit(solution)/shard_map/ppermute | solution.py:224
  45.1 4.9 %collective-permute-start.6 = (bf16[480,128]{1,0:T(8,128)(2,1)S(1)}, bf16[480,128]{1,0:T(8,128)(2,1)S(1)}, u32[]{:S(2)}, u32[]{:S(2)}) collective-permute-start(bf16[480,128]{1,0:T(8,128)(2,1)S(1)} %collective-permute-done.4), channel_id=1, source_target_pairs={{0,1},{1,2},{2,3},{3,4},{4,5},{5,6},{6,7},{7,0},{8,9},{9,10},{10,1... | collective-permute-start | bytes 368648 | tf_op jit(solution)/shard_map/ppermute | solution.py:224
  50.1 20.7 %collective-permute-start.7 = (bf16[8,480,128]{2,1,0:T(8,128)(2,1)S(1)}, bf16[8,480,128]{2,1,0:T(8,128)(2,1)S(1)}, u32[]{:S(2)}, u32[]{:S(2)}) collective-permute-start(bf16[8,480,128]{2,1,0:T(8,128)(2,1)S(1)} %bitcast_dynamic-update-slice_fusion.18), channel_id=1, source_target_pairs={{0,8},{8,16},{16,24},{24,0},{1,9},{9,17},{17,25},{25,1},{2,10},{10... | collective-permute-start | bytes 2949128 | tf_op jit(solution)/shard_map/ppermute | solution.py:224
  50.1 20.7 %collective-permute-start.8 = (bf16[8,480,128]{2,1,0:T(8,128)(2,1)S(1)}, bf16[8,480,128]{2,1,0:T(8,128)(2,1)S(1)}, u32[]{:S(2)}, u32[]{:S(2)}) collective-permute-start(bf16[8,480,128]{2,1,0:T(8,128)(2,1)S(1)} %bitcast_dynamic-update-slice_fusion.18), channel_id=1, source_target_pairs={{0,24},{8,0},{16,8},{24,16},{1,25},{9,1},{17,9},{25,17},{2,26},{10... | collective-permute-start | bytes 2949128 | tf_op jit(solution)/shard_map/ppermute | solution.py:224
  52.8 10.5 %collective-permute-start.19 = (bf16[4,528,128]{2,1,0:T(8,128)(2,1)S(1)}, bf16[4,528,128]{2,1,0:T(8,128)(2,1)S(1)}, u32[]{:S(2)}, u32[]{:S(2)}) collective-permute-start(bf16[4,528,128]{2,1,0:T(8,128)(2,1)S(1)} %collective-permute-done.17), channel_id=1, source_target_pairs={{0,1},{1,2},{2,3},{3,4},{4,5},{5,6},{6,7},{7,0},{8,9},{9,10},{10,1... | collective-permute-start | bytes 1622024 | tf_op jit(solution)/shard_map/ppermute | solution.py:224
  52.8 10.5 %collective-permute-start.20 = (bf16[4,528,128]{2,1,0:T(8,128)(2,1)S(1)}, bf16[4,528,128]{2,1,0:T(8,128)(2,1)S(1)}, u32[]{:S(2)}, u32[]{:S(2)}) collective-permute-start(bf16[4,528,128]{2,1,0:T(8,128)(2,1)S(1)} %collective-permute-done.18), channel_id=1, source_target_pairs={{0,7},{1,0},{2,1},{3,2},{4,3},{5,4},{6,5},{7,6},{8,15},{9,8},{10,9... | collective-permute-start | bytes 1622024 | tf_op jit(solution)/shard_map/ppermute | solution.py:224
  63.4 10.8 %collective-permute-start.21 = (bf16[4,528,128]{2,1,0:T(8,128)(2,1)S(1)}, bf16[4,528,128]{2,1,0:T(8,128)(2,1)S(1)}, u32[]{:S(2)}, u32[]{:S(2)}) collective-permute-start(bf16[4,528,128]{2,1,0:T(8,128)(2,1)S(1)} %collective-permute-done.19), channel_id=1, source_target_pairs={{0,1},{1,2},{2,3},{3,4},{4,5},{5,6},{6,7},{7,0},{8,9},{9,10},{10,1... | collective-permute-start | bytes 1622024 | tf_op jit(solution)/shard_map/ppermute | solution.py:224
  63.4 10.9 %collective-permute-start.22 = (bf16[4,528,128]{2,1,0:T(8,128)(2,1)S(1)}, bf16[4,528,128]{2,1,0:T(8,128)(2,1)S(1)}, u32[]{:S(2)}, u32[]{:S(2)}) collective-permute-start(bf16[4,528,128]{2,1,0:T(8,128)(2,1)S(1)} %collective-permute-done.20), channel_id=1, source_target_pairs={{0,7},{1,0},{2,1},{3,2},{4,3},{5,4},{6,5},{7,6},{8,15},{9,8},{10,9... | collective-permute-start | bytes 1622024 | tf_op jit(solution)/shard_map/ppermute | solution.py:224
  70.7 9.6 %collective-permute-start.9 = (bf16[4,480,128]{2,1,0:T(8,128)(2,1)S(1)}, bf16[4,480,128]{2,1,0:T(8,128)(2,1)S(1)}, u32[]{:S(2)}, u32[]{:S(2)}) collective-permute-start(bf16[4,480,128]{2,1,0:T(8,128)(2,1)S(1)} %slice.48), channel_id=1, source_target_pairs={{0,8},{8,16},{16,24},{24,0},{1,9},{9,17},{17,25},{25,1},{2,10},{10... | collective-permute-start | bytes 1474568 | tf_op jit(solution)/shard_map/ppermute | solution.py:224
  70.9 9.7 %copy-start = (bf16[42,128,128]{2,1,0:T(8,128)(2,1)S(1)}, bf16[42,128,128]{2,1,0:T(8,128)(2,1)}, u32[]{:S(2)}) copy-start(bf16[42,128,128]{2,1,0:T(8,128)(2,1)} %rhs.3) | copy-start | bytes 4128772
  70.9 9.6 %collective-permute-start.10 = (bf16[4,480,128]{2,1,0:T(8,128)(2,1)S(1)}, bf16[4,480,128]{2,1,0:T(8,128)(2,1)S(1)}, u32[]{:S(2)}, u32[]{:S(2)}) collective-permute-start(bf16[4,480,128]{2,1,0:T(8,128)(2,1)S(1)} %slice.49), channel_id=1, source_target_pairs={{0,24},{8,0},{16,8},{24,16},{1,25},{9,1},{17,9},{25,17},{2,26},{10... | collective-permute-start | bytes 1474568 | tf_op jit(solution)/shard_map/ppermute | solution.py:224
  74.1 10.9 %collective-permute-start.23 = (bf16[2,528,128]{2,1,0:T(8,128)(2,1)S(1)}, bf16[2,528,128]{2,1,0:T(8,128)(2,1)S(1)}, u32[]{:S(2)}, u32[]{:S(2)}) collective-permute-start(bf16[2,528,128]{2,1,0:T(8,128)(2,1)S(1)} %slice.58), channel_id=1, source_target_pairs={{0,1},{1,2},{2,3},{3,4},{4,5},{5,6},{6,7},{7,0},{8,9},{9,10},{10,1... | collective-permute-start | bytes 811016 | tf_op jit(solution)/shard_map/ppermute | solution.py:224
  74.3 10.8 %collective-permute-start.24 = (bf16[2,528,128]{2,1,0:T(8,128)(2,1)S(1)}, bf16[2,528,128]{2,1,0:T(8,128)(2,1)S(1)}, u32[]{:S(2)}, u32[]{:S(2)}) collective-permute-start(bf16[2,528,128]{2,1,0:T(8,128)(2,1)S(1)} %slice.59), channel_id=1, source_target_pairs={{0,7},{1,0},{2,1},{3,2},{4,3},{5,4},{6,5},{7,6},{8,15},{9,8},{10,9... | collective-permute-start | bytes 811016 | tf_op jit(solution)/shard_map/ppermute | solution.py:224
  77.4 7.8 %copy-start.1 = (bf16[1,128,128]{2,1,0:T(8,128)(2,1)S(1)}, bf16[1,128,128]{2,1,0:T(8,128)(2,1)}, u32[]{:S(2)}) copy-start(bf16[1,128,128]{2,1,0:T(8,128)(2,1)} %param.8) | copy-start | bytes 98308

commit v7 on v6

--- a/solution.py
+++ b/solution.py
@@ -230,12 +230,14 @@
     return lax.dynamic_update_slice(buffer, x.reshape(shape), start)
 
 
-def gather_z_then_y(x):
+def gather_z_then_y(x, other, after):
     y, z = lax.axis_index("y"), lax.axis_index("z")
     own = put(jnp.zeros((NZ, *x.shape), x.dtype), x, z)
     right, left = x, x
     for k in range(1, 4):
         right, left = shift(right, "z", 1), shift(left, "z", -1)
+        if k == after:
+            right, left, other = lax.optimization_barrier((right, left, other))
         own = put(put(own, right, (z - k) % NZ), left, (z + k) % NZ)
     own = put(own, shift(right, "z", 1), (z + 4) % NZ)
     half = NZ // 2
@@ -244,14 +246,19 @@
     every = put(put(every, right, (y - 1) % NY), left, (y + 1) % NY)
     every = put(every, shift(right[:half], "y", 1)[None], (y + 2) % NY)
     every = put(every, shift(left[half:], "y", -1)[None], (y + 2) % NY, half)
-    return every.reshape(PARTS, *x.shape)
-
-
-def gather_y_then_z(x):
-    y, z = lax.axis_index("y"), lax.axis_index("z")
+    return every.reshape(PARTS, *x.shape), other
+
+
+def gather_y(x):
+    y = lax.axis_index("y")
     own = put(jnp.zeros((NY, *x.shape), x.dtype), x, y)
     for k in (1, -1, 2):
         own = put(own, shift(x, "y", k), (y - k) % NY)
+    return own
+
+
+def gather_z(own):
+    x, z = own[0], lax.axis_index("z")
     half = NY // 2
     every = put(jnp.zeros((NY, NZ, *x.shape), x.dtype), own[:, None], 0, z)
     right, left = own, own
@@ -283,8 +290,8 @@
     )
     top_all = gather_row(top_rows)
     rest = jnp.concatenate([rest, *(top_all[t, : WIDTH[t] * ROWS] for t in range(TOP))], axis=0)
-    lead_all = gather_z_then_y(lead)
-    rest_all = gather_y_then_z(rest)
+    lead_all, rest = gather_z_then_y(lead, rest, 1)
+    rest_all = gather_z(gather_y(rest))
     codes = targets.reshape(-1)
     leaf_sol, acc = run_leaves(codes, local_rhs, lead_all)
     sol, addends = run_later(codes, position[None], local_rhs, top_rhs[0], acc, leaf_sol, rest_all)

time: 108 us -> 107 us (level)
  waiting for transfers between devices: 31.8 us -> 30.6 us
    ppermute x25, waiting for transfers between devices: 31.8 us -> 30.6 us  [shift(): return lax.ppermute(x, axis, [(n, (n + k) % size) for n in range(size)])]
  transfers between devices with their start and end apart: 25 -> 25, of which waited for: 7 -> 6; matrix products, arithmetic and copies ran while one was open for 5% -> 5% of each run, Pallas kernels for 4% -> 4%
where the time goes in v7:
time: 107 us
  starting transfers between devices  37.8 us (35%)
  waiting for transfers between devices  30.6 us (29%)
  blocking collectives  16.8 us (16%)
  Pallas kernels  13.7 us (13%)
  local copies, waits for them, and re-layouts  5.65 us (5%)
  between operations  1.43 us (1%)
    ppermute x25, starting transfers between devices, shift(): return lax.ppermute(x, axis, [(n, (n + k) % size) for n in range(size)])  37.8 us
    ppermute x25, waiting for transfers between devices, shift(): return lax.ppermute(x, axis, [(n, (n + k) % size) for n in range(size)])  30.6 us
    all_to_all x1, blocking collectives, local(): parts = lax.all_to_all(addends, ROW, 0, 0, tiled=True)  14.2 us
    pallas_call x1, Pallas kernels, run_later(): pl.pallas_call(later_levels, out_shape=(jax.ShapeDtypeStruct((SUB, B, B),...  7.47 us
    pallas_call x1, Pallas kernels, run_leaves(): pl.pallas_call(leaf_level, out_shape=(jax.ShapeDtypeStruct((FIRST, B, B),...  4.47 us
    all_gather x1, blocking collectives, gather_row(): pair = lax.all_gather(x, 'core', axis=0)  2.64 us
    dynamic_update_slice x30, local copies, waits for them, and re-layouts, put(): return lax.dynamic_update_slice(buffer, x.reshape(shape), start)  2.35 us
  transfers between devices with their start and end apart: 25, of which 6 were waited for; matrix products, arithmetic and copies ran while one was open for 5% of the time, Pallas kernels for 4%

profile of v7, /device:TPU:1, one launch (start us, length us, event | category | flops | bytes accessed | tf_op | source)
XLA Modules:
  0.0 106.7 jit_solution(2627230311137812914)
XLA Ops:
  0.6 1.7 %shard_map.86 = (bf16[480,128]{1,0:T(8,128)(2,1)}, bf16[368,128]{1,0:T(8,128)(2,1)}, bf16[32,128]{1,0:T(8,128)(2,1)}) custom-call(s32[1]{0:T(128)} %bitcast.row.where, bf16[168,128]{1,0:T(8,128)(2,1)} %bitcast.134, bf16[672,128]{1,0:T(8,128)(2,1)} %bitcast.129, bf16[32,128]{1,0:T(8,128)(2,1)} %bitcast.136, bf16[4,128]{1,0:T(4,128)(2,1)} %bitcast.137), custom_call_target="tpu_custom_call" | custom-call | bytes 524288 | tf_op jit(solution)/shard_map/pallas_call | solution.py:162
  2.4 2.5 %collective-permute-start = (bf16[480,128]{1,0:T(8,128)(2,1)}, bf16[480,128]{1,0:T(8,128)(2,1)S(1)}, u32[]{:S(2)}, u32[]{:S(2)}) collective-permute-start(bf16[480,128]{1,0:T(8,128)(2,1)} %get-tuple-element.12), channel_id=1, source_target_pairs={{0,1},{1,2},{2,3},{3,4},{4,5},{5,6},{6,7},{7,0},{8,9},{9,10},{10,1... | collective-permute-start | bytes 368648 | tf_op jit(solution)/shard_map/ppermute | solution.py:224
  4.9 4.0 %collective-permute-start.1 = (bf16[480,128]{1,0:T(8,128)(2,1)}, bf16[480,128]{1,0:T(8,128)(2,1)S(1)}, u32[]{:S(2)}, u32[]{:S(2)}) collective-permute-start(bf16[480,128]{1,0:T(8,128)(2,1)} %get-tuple-element.12), channel_id=1, source_target_pairs={{0,7},{1,0},{2,1},{3,2},{4,3},{5,4},{6,5},{7,6},{8,15},{9,8},{10,9... | collective-permute-start | bytes 368648 | tf_op jit(solution)/shard_map/ppermute | solution.py:224
  9.0 2.6 %all-gather = bf16[64,128]{1,0:T(8,128)(2,1)S(1)} all-gather(bf16[32,128]{1,0:T(8,128)(2,1)} %get-tuple-element.14), channel_id=2, replica_groups=mesh['x'=4,'core'=2,'y'=4,'z'=8] {'core'}, dimensions={0}, use_global_device_ids=true | all-gather | bytes 24576 | tf_op jit(solution)/shard_map/all_gather | solution.py:275
  11.6 1.2 %collective-permute-start.2 = (bf16[2,32,128]{2,1,0:T(8,128)(2,1)S(1)}, bf16[2,32,128]{2,1,0:T(8,128)(2,1)S(1)}, u32[]{:S(2)}, u32[]{:S(2)}) collective-permute-start(bf16[2,32,128]{2,1,0:T(8,128)(2,1)S(1)} %bitcast.130), channel_id=1, source_target_pairs={{0,64},{64,128},{128,192},{192,0},{1,65},{65,129},{129,193},{193,1... | collective-permute-start | bytes 49160 | tf_op jit(solution)/shard_map/ppermute | solution.py:224
  12.8 1.5 %collective-permute-start.3 = (bf16[2,32,128]{2,1,0:T(8,128)(2,1)S(1)}, bf16[2,32,128]{2,1,0:T(8,128)(2,1)S(1)}, u32[]{:S(2)}, u32[]{:S(2)}) collective-permute-start(bf16[2,32,128]{2,1,0:T(8,128)(2,1)S(1)} %bitcast.131), channel_id=1, source_target_pairs={{0,192},{64,0},{128,64},{192,128},{1,193},{65,1},{129,65},{193,129... | collective-permute-start | bytes 49160 | tf_op jit(solution)/shard_map/ppermute | solution.py:224
  14.3 1.5 %collective-permute-start.4 = (bf16[2,32,128]{2,1,0:T(8,128)(2,1)S(1)}, bf16[2,32,128]{2,1,0:T(8,128)(2,1)S(1)}, u32[]{:S(2)}, u32[]{:S(2)}) collective-permute-start(bf16[2,32,128]{2,1,0:T(8,128)(2,1)S(1)} %bitcast.132), channel_id=1, source_target_pairs={{0,128},{64,192},{128,0},{192,64},{1,129},{65,193},{129,1},{193,65... | collective-permute-start | bytes 49160 | tf_op jit(solution)/shard_map/ppermute | solution.py:224
  15.8 0.9 constant_dynamic-update-slice_fusion.8
  16.7 0.1 broadcast_in_dim.55
  16.8 0.9 bitcast_dynamic-update-slice_fusion.25
  18.0 0.8 copy.17
  18.8 0.1 reshape.94.codes
  19.0 0.0 collective-permute-done.2
  19.0 0.0 collective-permute-done.4
  19.2 0.0 collective-permute-done
  19.2 1.4 %collective-permute-start.14 = (bf16[528,128]{1,0:T(8,128)(2,1)S(1)}, bf16[528,128]{1,0:T(8,128)(2,1)S(1)}, u32[]{:S(2)}, u32[]{:S(2)}) collective-permute-start(bf16[528,128]{1,0:T(8,128)(2,1)S(1)} %constant_dynamic-update-slice_fusion), channel_id=1, source_target_pairs={{0,8},{8,16},{16,24},{24,0},{1,9},{9,17},{17,25},{25,1},{2,10},{10... | collective-permute-start | bytes 405512 | tf_op jit(solution)/shard_map/ppermute | solution.py:224
  20.6 1.5 %collective-permute-start.15 = (bf16[528,128]{1,0:T(8,128)(2,1)S(1)}, bf16[528,128]{1,0:T(8,128)(2,1)S(1)}, u32[]{:S(2)}, u32[]{:S(2)}) collective-permute-start(bf16[528,128]{1,0:T(8,128)(2,1)S(1)} %constant_dynamic-update-slice_fusion), channel_id=1, source_target_pairs={{0,24},{8,0},{16,8},{24,16},{1,25},{9,1},{17,9},{25,17},{2,26},{10... | collective-permute-start | bytes 405512 | tf_op jit(solution)/shard_map/ppermute | solution.py:224
  22.1 1.6 %collective-permute-start.16 = (bf16[528,128]{1,0:T(8,128)(2,1)S(1)}, bf16[528,128]{1,0:T(8,128)(2,1)S(1)}, u32[]{:S(2)}, u32[]{:S(2)}) collective-permute-start(bf16[528,128]{1,0:T(8,128)(2,1)S(1)} %constant_dynamic-update-slice_fusion), channel_id=1, source_target_pairs={{0,16},{8,24},{16,0},{24,8},{1,17},{9,25},{17,1},{25,9},{2,18},{10... | collective-permute-start | bytes 405512 | tf_op jit(solution)/shard_map/ppermute | solution.py:224
  23.6 0.0 collective-permute-start.5
  23.7 2.7 %collective-permute-start.6 = (bf16[480,128]{1,0:T(8,128)(2,1)S(1)}, bf16[480,128]{1,0:T(8,128)(2,1)S(1)}, u32[]{:S(2)}, u32[]{:S(2)}) collective-permute-start(bf16[480,128]{1,0:T(8,128)(2,1)S(1)} %collective-permute-done.1), channel_id=1, source_target_pairs={{0,7},{1,0},{2,1},{3,2},{4,3},{5,4},{6,5},{7,6},{8,15},{9,8},{10,9... | collective-permute-start | bytes 368648 | tf_op jit(solution)/shard_map/ppermute | solution.py:224
  26.3 0.1 broadcast_in_dim.60
  26.5 2.1 %collective-permute-done.5 = bf16[480,128]{1,0:T(8,128)(2,1)S(1)} collective-permute-done((bf16[480,128]{1,0:T(8,128)(2,1)S(1)}, bf16[480,128]{1,0:T(8,128)(2,1)S(1)}, u32[]{:S(2)}, u32[]{:S(2)}) %collective-permute-start.5) | collective-permute-done | bytes 122912 | tf_op jit(solution)/shard_map/ppermute | solution.py:224
  28.6 0.0 collective-permute-start.7
  28.6 0.0 collective-permute-done.6
  28.6 3.0 %collective-permute-start.8 = (bf16[480,128]{1,0:T(8,128)(2,1)S(1)}, bf16[480,128]{1,0:T(8,128)(2,1)S(1)}, u32[]{:S(2)}, u32[]{:S(2)}) collective-permute-start(bf16[480,128]{1,0:T(8,128)(2,1)S(1)} %collective-permute-done.6), channel_id=1, source_target_pairs={{0,7},{1,0},{2,1},{3,2},{4,3},{5,4},{6,5},{7,6},{8,15},{9,8},{10,9... | collective-permute-start | bytes 368648 | tf_op jit(solution)/shard_map/ppermute | solution.py:224
  31.7 0.0 collective-permute-done.15
  31.7 0.1 collective-permute-start.17
  31.8 2.7 %collective-permute-start.18 = (bf16[4,528,128]{2,1,0:T(8,128)(2,1)S(1)}, bf16[4,528,128]{2,1,0:T(8,128)(2,1)S(1)}, u32[]{:S(2)}, u32[]{:S(2)}) collective-permute-start(bf16[4,528,128]{2,1,0:T(8,128)(2,1)S(1)} %bitcast_dynamic-update-slice_fusion.14), channel_id=1, source_target_pairs={{0,7},{1,0},{2,1},{3,2},{4,3},{5,4},{6,5},{7,6},{8,15},{9,8},{10,9... | collective-permute-start | bytes 1622024 | tf_op jit(solution)/shard_map/ppermute | solution.py:224
  34.5 0.6 broadcast_in_dim.59
  35.1 0.1 bitcast_dynamic-update-slice_fusion.9
  35.1 0.0 collective-permute-done.7
  35.2 0.3 collective-permute-start.9
  35.5 0.0 collective-permute-done.8
  35.5 12.9 %collective-permute-done.9 = bf16[480,128]{1,0:T(8,128)(2,1)S(1)} collective-permute-done((bf16[480,128]{1,0:T(8,128)(2,1)S(1)}, bf16[480,128]{1,0:T(8,128)(2,1)S(1)}, u32[]{:S(2)}, u32[]{:S(2)}) %collective-permute-start.9) | collective-permute-done | bytes 122912 | tf_op jit(solution)/shard_map/ppermute | solution.py:224
  48.4 0.2 collective-permute-start.10
  48.6 2.6 %collective-permute-start.11 = (bf16[8,480,128]{2,1,0:T(8,128)(2,1)S(1)}, bf16[8,480,128]{2,1,0:T(8,128)(2,1)S(1)}, u32[]{:S(2)}, u32[]{:S(2)}) collective-permute-start(bf16[8,480,128]{2,1,0:T(8,128)(2,1)S(1)} %bitcast_dynamic-update-slice_fusion.18), channel_id=1, source_target_pairs={{0,24},{8,0},{16,8},{24,16},{1,25},{9,1},{17,9},{25,17},{2,26},{10... | collective-permute-start | bytes 2949128 | tf_op jit(solution)/shard_map/ppermute | solution.py:224
  51.2 2.7 %collective-permute-start.20 = (bf16[4,528,128]{2,1,0:T(8,128)(2,1)S(1)}, bf16[4,528,128]{2,1,0:T(8,128)(2,1)S(1)}, u32[]{:S(2)}, u32[]{:S(2)}) collective-permute-start(bf16[4,528,128]{2,1,0:T(8,128)(2,1)S(1)} %collective-permute-done.18), channel_id=1, source_target_pairs={{0,7},{1,0},{2,1},{3,2},{4,3},{5,4},{6,5},{7,6},{8,15},{9,8},{10,9... | collective-permute-start | bytes 1622024 | tf_op jit(solution)/shard_map/ppermute | solution.py:224
  53.9 0.6 broadcast_in_dim.54
  54.4 0.1 bitcast_dynamic-update-slice_fusion.2
  54.6 0.1 bitcast_dynamic-update-slice_fusion.8
  54.7 0.1 bitcast_dynamic-update-slice_fusion.7
  54.8 7.6 %collective-permute-done.19 = bf16[4,528,128]{2,1,0:T(8,128)(2,1)S(1)} collective-permute-done((bf16[4,528,128]{2,1,0:T(8,128)(2,1)S(1)}, bf16[4,528,128]{2,1,0:T(8,128)(2,1)S(1)}, u32[]{:S(2)}, u32[]{:S(2)}) %collective-permute-start.19) | collective-permute-done | bytes 540704 | tf_op jit(solution)/shard_map/ppermute | solution.py:224
  62.4 2.7 %collective-permute-start.22 = (bf16[4,528,128]{2,1,0:T(8,128)(2,1)S(1)}, bf16[4,528,128]{2,1,0:T(8,128)(2,1)S(1)}, u32[]{:S(2)}, u32[]{:S(2)}) collective-permute-start(bf16[4,528,128]{2,1,0:T(8,128)(2,1)S(1)} %collective-permute-done.20), channel_id=1, source_target_pairs={{0,7},{1,0},{2,1},{3,2},{4,3},{5,4},{6,5},{7,6},{8,15},{9,8},{10,9... | collective-permute-start | bytes 1622024 | tf_op jit(solution)/shard_map/ppermute | solution.py:224
  65.0 0.1 bitcast_dynamic-update-slice_fusion.6
  65.1 0.1 bitcast_dynamic-update-slice_fusion.5
  65.2 4.5 %collective-permute-done.10 = bf16[8,480,128]{2,1,0:T(8,128)(2,1)S(1)} collective-permute-done((bf16[8,480,128]{2,1,0:T(8,128)(2,1)S(1)}, bf16[8,480,128]{2,1,0:T(8,128)(2,1)S(1)}, u32[]{:S(2)}, u32[]{:S(2)}) %collective-permute-start.10) | collective-permute-done | bytes 983072 | tf_op jit(solution)/shard_map/ppermute | solution.py:224
  69.7 0.1 collective-permute-start.12
  69.9 0.0 copy-start
  69.9 2.7 %collective-permute-start.13 = (bf16[4,480,128]{2,1,0:T(8,128)(2,1)S(1)}, bf16[4,480,128]{2,1,0:T(8,128)(2,1)S(1)}, u32[]{:S(2)}, u32[]{:S(2)}) collective-permute-start(bf16[4,480,128]{2,1,0:T(8,128)(2,1)S(1)} %slice.57), channel_id=1, source_target_pairs={{0,24},{8,0},{16,8},{24,16},{1,25},{9,1},{17,9},{25,17},{2,26},{10... | collective-permute-start | bytes 1474568 | tf_op jit(solution)/shard_map/ppermute | solution.py:224
  72.6 0.1 bitcast_dynamic-update-slice_fusion.1
  72.8 0.1 bitcast_dynamic-update-slice_fusion
  72.9 0.2 collective-permute-done.21
  73.1 0.1 collective-permute-start.23
  73.2 2.9 %collective-permute-start.24 = (bf16[2,528,128]{2,1,0:T(8,128)(2,1)S(1)}, bf16[2,528,128]{2,1,0:T(8,128)(2,1)S(1)}, u32[]{:S(2)}, u32[]{:S(2)}) collective-permute-start(bf16[2,528,128]{2,1,0:T(8,128)(2,1)S(1)} %slice.59), channel_id=1, source_target_pairs={{0,7},{1,0},{2,1},{3,2},{4,3},{5,4},{6,5},{7,6},{8,15},{9,8},{10,9... | collective-permute-start | bytes 811016 | tf_op jit(solution)/shard_map/ppermute | solution.py:224
  76.2 0.1 bitcast_dynamic-update-slice_fusion.4
  76.3 0.1 bitcast_dynamic-update-slice_fusion.3
  76.3 0.0 copy-start.1
  76.4 3.2 %collective-permute-done.12 = bf16[4,480,128]{2,1,0:T(8,128)(2,1)S(1)} collective-permute-done((bf16[4,480,128]{2,1,0:T(8,128)(2,1)S(1)}, bf16[4,480,128]{2,1,0:T(8,128)(2,1)S(1)}, u32[]{:S(2)}, u32[]{:S(2)}) %collective-permute-start.12) | collective-permute-done | bytes 491552 | tf_op jit(solution)/shard_map/ppermute | solution.py:224
  79.6 0.1 bitcast_dynamic-update-slice_fusion.11
  79.6 0.1 bitcast_dynamic-update-slice_fusion.10
  79.7 4.5 %shard_map.87 = (bf16[24,128,128]{2,1,0:T(8,128)(2,1)S(1)}, f32[26,128,128]{2,1,0:T(8,128)S(1)}) custom-call(s32[168]{0:T(256)S(1)} %reshape.94.codes, bf16[42,128,128]{2,1,0:T(8,128)(2,1)S(1)} %copy-done, bf16[32,480,128]{2,1,0:T(8,128)(2,1)S(1)} %bitcast.119), custom_call_target="tpu_custom_call" | custom-call | flops 503316480 | bytes 8388608 | tf_op jit(solution)/shard_map/pallas_call | solution.py:181
  84.3 7.5 %shard_map.88 = (bf16[42,128,128]{2,1,0:T(8,128)(2,1)}, bf16[8,128,128]{2,1,0:T(8,128)(2,1)S(1)}) custom-call(s32[168]{0:T(256)S(1)} %reshape.94.codes, s32[1]{0:T(128)} %bitcast.row.where, bf16[42,128,128]{2,1,0:T(8,128)(2,1)S(1)} %copy-done, bf16[128,128]{1,0:T(8,128)(2,1)S(1)} %bitcast.120, f32[26,128,128]{2,1,0:T(8,128)S(1)} %get-tuple-element.17.acc_in, ...), custom_call_target="tpu_custom_call" | custom-call | flops 528482304 | bytes 8388608 | tf_op jit(solution)/shard_map/pallas_call | solution.py:200
  91.8 14.2 %all_to_all.5 = bf16[8,128,128]{2,1,0:T(8,128)(2,1)S(1)} all-to-all(bf16[8,128,128]{2,1,0:T(8,128)(2,1)S(1)} %get-tuple-element.21), channel_id=1, replica_groups=mesh['x'=4,'core'=2,'y'=4,'z'=8] {'x','core'}, dimensions={0} | all-to-all | bytes 524288 | tf_op jit(solution)/shard_map/all_to_all | solution.py:298
  106.0 0.7 reduce_sum.12
  (46 shorter events, 0.6 us)
Async XLA Ops:
  2.4 16.8 %collective-permute-start = (bf16[480,128]{1,0:T(8,128)(2,1)}, bf16[480,128]{1,0:T(8,128)(2,1)S(1)}, u32[]{:S(2)}, u32[]{:S(2)}) collective-permute-start(bf16[480,128]{1,0:T(8,128)(2,1)} %get-tuple-element.12), channel_id=1, source_target_pairs={{0,1},{1,2},{2,3},{3,4},{4,5},{5,6},{6,7},{7,0},{8,9},{9,10},{10,1... | collective-permute-start | bytes 368648 | tf_op jit(solution)/shard_map/ppermute | solution.py:224
  4.9 14.3 %collective-permute-start.1 = (bf16[480,128]{1,0:T(8,128)(2,1)}, bf16[480,128]{1,0:T(8,128)(2,1)S(1)}, u32[]{:S(2)}, u32[]{:S(2)}) collective-permute-start(bf16[480,128]{1,0:T(8,128)(2,1)} %get-tuple-element.12), channel_id=1, source_target_pairs={{0,7},{1,0},{2,1},{3,2},{4,3},{5,4},{6,5},{7,6},{8,15},{9,8},{10,9... | collective-permute-start | bytes 368648 | tf_op jit(solution)/shard_map/ppermute | solution.py:224
  11.6 7.4 %collective-permute-start.2 = (bf16[2,32,128]{2,1,0:T(8,128)(2,1)S(1)}, bf16[2,32,128]{2,1,0:T(8,128)(2,1)S(1)}, u32[]{:S(2)}, u32[]{:S(2)}) collective-permute-start(bf16[2,32,128]{2,1,0:T(8,128)(2,1)S(1)} %bitcast.130), channel_id=1, source_target_pairs={{0,64},{64,128},{128,192},{192,0},{1,65},{65,129},{129,193},{193,1... | collective-permute-start | bytes 49160 | tf_op jit(solution)/shard_map/ppermute | solution.py:224
  12.8 6.2 %collective-permute-start.3 = (bf16[2,32,128]{2,1,0:T(8,128)(2,1)S(1)}, bf16[2,32,128]{2,1,0:T(8,128)(2,1)S(1)}, u32[]{:S(2)}, u32[]{:S(2)}) collective-permute-start(bf16[2,32,128]{2,1,0:T(8,128)(2,1)S(1)} %bitcast.131), channel_id=1, source_target_pairs={{0,192},{64,0},{128,64},{192,128},{1,193},{65,1},{129,65},{193,129... | collective-permute-start | bytes 49160 | tf_op jit(solution)/shard_map/ppermute | solution.py:224
  14.3 4.8 %collective-permute-start.4 = (bf16[2,32,128]{2,1,0:T(8,128)(2,1)S(1)}, bf16[2,32,128]{2,1,0:T(8,128)(2,1)S(1)}, u32[]{:S(2)}, u32[]{:S(2)}) collective-permute-start(bf16[2,32,128]{2,1,0:T(8,128)(2,1)S(1)} %bitcast.132), channel_id=1, source_target_pairs={{0,128},{64,192},{128,0},{192,64},{1,129},{65,193},{129,1},{193,65... | collective-permute-start | bytes 49160 | tf_op jit(solution)/shard_map/ppermute | solution.py:224
  19.2 12.4 %collective-permute-start.14 = (bf16[528,128]{1,0:T(8,128)(2,1)S(1)}, bf16[528,128]{1,0:T(8,128)(2,1)S(1)}, u32[]{:S(2)}, u32[]{:S(2)}) collective-permute-start(bf16[528,128]{1,0:T(8,128)(2,1)S(1)} %constant_dynamic-update-slice_fusion), channel_id=1, source_target_pairs={{0,8},{8,16},{16,24},{24,0},{1,9},{9,17},{17,25},{25,1},{2,10},{10... | collective-permute-start | bytes 405512 | tf_op jit(solution)/shard_map/ppermute | solution.py:224
  20.6 11.1 %collective-permute-start.15 = (bf16[528,128]{1,0:T(8,128)(2,1)S(1)}, bf16[528,128]{1,0:T(8,128)(2,1)S(1)}, u32[]{:S(2)}, u32[]{:S(2)}) collective-permute-start(bf16[528,128]{1,0:T(8,128)(2,1)S(1)} %constant_dynamic-update-slice_fusion), channel_id=1, source_target_pairs={{0,24},{8,0},{16,8},{24,16},{1,25},{9,1},{17,9},{25,17},{2,26},{10... | collective-permute-start | bytes 405512 | tf_op jit(solution)/shard_map/ppermute | solution.py:224
  22.1 9.6 %collective-permute-start.16 = (bf16[528,128]{1,0:T(8,128)(2,1)S(1)}, bf16[528,128]{1,0:T(8,128)(2,1)S(1)}, u32[]{:S(2)}, u32[]{:S(2)}) collective-permute-start(bf16[528,128]{1,0:T(8,128)(2,1)S(1)} %constant_dynamic-update-slice_fusion), channel_id=1, source_target_pairs={{0,16},{8,24},{16,0},{24,8},{1,17},{9,25},{17,1},{25,9},{2,18},{10... | collective-permute-start | bytes 405512 | tf_op jit(solution)/shard_map/ppermute | solution.py:224
  23.6 4.9 %collective-permute-start.5 = (bf16[480,128]{1,0:T(8,128)(2,1)S(1)}, bf16[480,128]{1,0:T(8,128)(2,1)S(1)}, u32[]{:S(2)}, u32[]{:S(2)}) collective-permute-start(bf16[480,128]{1,0:T(8,128)(2,1)S(1)} %collective-permute-done), channel_id=1, source_target_pairs={{0,1},{1,2},{2,3},{3,4},{4,5},{5,6},{6,7},{7,0},{8,9},{9,10},{10,1... | collective-permute-start | bytes 368648 | tf_op jit(solution)/shard_map/ppermute | solution.py:224
  23.7 4.9 %collective-permute-start.6 = (bf16[480,128]{1,0:T(8,128)(2,1)S(1)}, bf16[480,128]{1,0:T(8,128)(2,1)S(1)}, u32[]{:S(2)}, u32[]{:S(2)}) collective-permute-start(bf16[480,128]{1,0:T(8,128)(2,1)S(1)} %collective-permute-done.1), channel_id=1, source_target_pairs={{0,7},{1,0},{2,1},{3,2},{4,3},{5,4},{6,5},{7,6},{8,15},{9,8},{10,9... | collective-permute-start | bytes 368648 | tf_op jit(solution)/shard_map/ppermute | solution.py:224
  28.6 6.6 %collective-permute-start.7 = (bf16[480,128]{1,0:T(8,128)(2,1)S(1)}, bf16[480,128]{1,0:T(8,128)(2,1)S(1)}, u32[]{:S(2)}, u32[]{:S(2)}) collective-permute-start(bf16[480,128]{1,0:T(8,128)(2,1)S(1)} %collective-permute-done.5), channel_id=1, source_target_pairs={{0,1},{1,2},{2,3},{3,4},{4,5},{5,6},{6,7},{7,0},{8,9},{9,10},{10,1... | collective-permute-start | bytes 368648 | tf_op jit(solution)/shard_map/ppermute | solution.py:224
  28.6 6.9 %collective-permute-start.8 = (bf16[480,128]{1,0:T(8,128)(2,1)S(1)}, bf16[480,128]{1,0:T(8,128)(2,1)S(1)}, u32[]{:S(2)}, u32[]{:S(2)}) collective-permute-start(bf16[480,128]{1,0:T(8,128)(2,1)S(1)} %collective-permute-done.6), channel_id=1, source_target_pairs={{0,7},{1,0},{2,1},{3,2},{4,3},{5,4},{6,5},{7,6},{8,15},{9,8},{10,9... | collective-permute-start | bytes 368648 | tf_op jit(solution)/shard_map/ppermute | solution.py:224
  31.7 19.4 %collective-permute-start.17 = (bf16[4,528,128]{2,1,0:T(8,128)(2,1)S(1)}, bf16[4,528,128]{2,1,0:T(8,128)(2,1)S(1)}, u32[]{:S(2)}, u32[]{:S(2)}) collective-permute-start(bf16[4,528,128]{2,1,0:T(8,128)(2,1)S(1)} %bitcast_dynamic-update-slice_fusion.14), channel_id=1, source_target_pairs={{0,1},{1,2},{2,3},{3,4},{4,5},{5,6},{6,7},{7,0},{8,9},{9,10},{10,1... | collective-permute-start | bytes 1622024 | tf_op jit(solution)/shard_map/ppermute | solution.py:224
  31.8 19.4 %collective-permute-start.18 = (bf16[4,528,128]{2,1,0:T(8,128)(2,1)S(1)}, bf16[4,528,128]{2,1,0:T(8,128)(2,1)S(1)}, u32[]{:S(2)}, u32[]{:S(2)}) collective-permute-start(bf16[4,528,128]{2,1,0:T(8,128)(2,1)S(1)} %bitcast_dynamic-update-slice_fusion.14), channel_id=1, source_target_pairs={{0,7},{1,0},{2,1},{3,2},{4,3},{5,4},{6,5},{7,6},{8,15},{9,8},{10,9... | collective-permute-start | bytes 1622024 | tf_op jit(solution)/shard_map/ppermute | solution.py:224
  35.2 13.3 %collective-permute-start.9 = (bf16[480,128]{1,0:T(8,128)(2,1)S(1)}, bf16[480,128]{1,0:T(8,128)(2,1)S(1)}, u32[]{:S(2)}, u32[]{:S(2)}) collective-permute-start(bf16[480,128]{1,0:T(8,128)(2,1)S(1)} %collective-permute-done.7), channel_id=1, source_target_pairs={{0,1},{1,2},{2,3},{3,4},{4,5},{5,6},{6,7},{7,0},{8,9},{9,10},{10,1... | collective-permute-start | bytes 368648 | tf_op jit(solution)/shard_map/ppermute | solution.py:224
  48.4 21.3 %collective-permute-start.10 = (bf16[8,480,128]{2,1,0:T(8,128)(2,1)S(1)}, bf16[8,480,128]{2,1,0:T(8,128)(2,1)S(1)}, u32[]{:S(2)}, u32[]{:S(2)}) collective-permute-start(bf16[8,480,128]{2,1,0:T(8,128)(2,1)S(1)} %bitcast_dynamic-update-slice_fusion.18), channel_id=1, source_target_pairs={{0,8},{8,16},{16,24},{24,0},{1,9},{9,17},{17,25},{25,1},{2,10},{10... | collective-permute-start | bytes 2949128 | tf_op jit(solution)/shard_map/ppermute | solution.py:224
  48.6 21.2 %collective-permute-start.11 = (bf16[8,480,128]{2,1,0:T(8,128)(2,1)S(1)}, bf16[8,480,128]{2,1,0:T(8,128)(2,1)S(1)}, u32[]{:S(2)}, u32[]{:S(2)}) collective-permute-start(bf16[8,480,128]{2,1,0:T(8,128)(2,1)S(1)} %bitcast_dynamic-update-slice_fusion.18), channel_id=1, source_target_pairs={{0,24},{8,0},{16,8},{24,16},{1,25},{9,1},{17,9},{25,17},{2,26},{10... | collective-permute-start | bytes 2949128 | tf_op jit(solution)/shard_map/ppermute | solution.py:224
  51.2 11.2 %collective-permute-start.19 = (bf16[4,528,128]{2,1,0:T(8,128)(2,1)S(1)}, bf16[4,528,128]{2,1,0:T(8,128)(2,1)S(1)}, u32[]{:S(2)}, u32[]{:S(2)}) collective-permute-start(bf16[4,528,128]{2,1,0:T(8,128)(2,1)S(1)} %collective-permute-done.17), channel_id=1, source_target_pairs={{0,1},{1,2},{2,3},{3,4},{4,5},{5,6},{6,7},{7,0},{8,9},{9,10},{10,1... | collective-permute-start | bytes 1622024 | tf_op jit(solution)/shard_map/ppermute | solution.py:224
  51.2 11.2 %collective-permute-start.20 = (bf16[4,528,128]{2,1,0:T(8,128)(2,1)S(1)}, bf16[4,528,128]{2,1,0:T(8,128)(2,1)S(1)}, u32[]{:S(2)}, u32[]{:S(2)}) collective-permute-start(bf16[4,528,128]{2,1,0:T(8,128)(2,1)S(1)} %collective-permute-done.18), channel_id=1, source_target_pairs={{0,7},{1,0},{2,1},{3,2},{4,3},{5,4},{6,5},{7,6},{8,15},{9,8},{10,9... | collective-permute-start | bytes 1622024 | tf_op jit(solution)/shard_map/ppermute | solution.py:224
  62.4 10.7 %collective-permute-start.21 = (bf16[4,528,128]{2,1,0:T(8,128)(2,1)S(1)}, bf16[4,528,128]{2,1,0:T(8,128)(2,1)S(1)}, u32[]{:S(2)}, u32[]{:S(2)}) collective-permute-start(bf16[4,528,128]{2,1,0:T(8,128)(2,1)S(1)} %collective-permute-done.19), channel_id=1, source_target_pairs={{0,1},{1,2},{2,3},{3,4},{4,5},{5,6},{6,7},{7,0},{8,9},{9,10},{10,1... | collective-permute-start | bytes 1622024 | tf_op jit(solution)/shard_map/ppermute | solution.py:224
  62.4 10.8 %collective-permute-start.22 = (bf16[4,528,128]{2,1,0:T(8,128)(2,1)S(1)}, bf16[4,528,128]{2,1,0:T(8,128)(2,1)S(1)}, u32[]{:S(2)}, u32[]{:S(2)}) collective-permute-start(bf16[4,528,128]{2,1,0:T(8,128)(2,1)S(1)} %collective-permute-done.20), channel_id=1, source_target_pairs={{0,7},{1,0},{2,1},{3,2},{4,3},{5,4},{6,5},{7,6},{8,15},{9,8},{10,9... | collective-permute-start | bytes 1622024 | tf_op jit(solution)/shard_map/ppermute | solution.py:224
  69.7 9.8 %collective-permute-start.12 = (bf16[4,480,128]{2,1,0:T(8,128)(2,1)S(1)}, bf16[4,480,128]{2,1,0:T(8,128)(2,1)S(1)}, u32[]{:S(2)}, u32[]{:S(2)}) collective-permute-start(bf16[4,480,128]{2,1,0:T(8,128)(2,1)S(1)} %slice.56), channel_id=1, source_target_pairs={{0,8},{8,16},{16,24},{24,0},{1,9},{9,17},{17,25},{25,1},{2,10},{10... | collective-permute-start | bytes 1474568 | tf_op jit(solution)/shard_map/ppermute | solution.py:224
  69.9 9.8 %copy-start = (bf16[42,128,128]{2,1,0:T(8,128)(2,1)S(1)}, bf16[42,128,128]{2,1,0:T(8,128)(2,1)}, u32[]{:S(2)}) copy-start(bf16[42,128,128]{2,1,0:T(8,128)(2,1)} %rhs.3) | copy-start | bytes 4128772
  69.9 9.7 %collective-permute-start.13 = (bf16[4,480,128]{2,1,0:T(8,128)(2,1)S(1)}, bf16[4,480,128]{2,1,0:T(8,128)(2,1)S(1)}, u32[]{:S(2)}, u32[]{:S(2)}) collective-permute-start(bf16[4,480,128]{2,1,0:T(8,128)(2,1)S(1)} %slice.57), channel_id=1, source_target_pairs={{0,24},{8,0},{16,8},{24,16},{1,25},{9,1},{17,9},{25,17},{2,26},{10... | collective-permute-start | bytes 1474568 | tf_op jit(solution)/shard_map/ppermute | solution.py:224
  73.1 11.1 %collective-permute-start.23 = (bf16[2,528,128]{2,1,0:T(8,128)(2,1)S(1)}, bf16[2,528,128]{2,1,0:T(8,128)(2,1)S(1)}, u32[]{:S(2)}, u32[]{:S(2)}) collective-permute-start(bf16[2,528,128]{2,1,0:T(8,128)(2,1)S(1)} %slice.58), channel_id=1, source_target_pairs={{0,1},{1,2},{2,3},{3,4},{4,5},{5,6},{6,7},{7,0},{8,9},{9,10},{10,1... | collective-permute-start | bytes 811016 | tf_op jit(solution)/shard_map/ppermute | solution.py:224
  73.2 11.0 %collective-permute-start.24 = (bf16[2,528,128]{2,1,0:T(8,128)(2,1)S(1)}, bf16[2,528,128]{2,1,0:T(8,128)(2,1)S(1)}, u32[]{:S(2)}, u32[]{:S(2)}) collective-permute-start(bf16[2,528,128]{2,1,0:T(8,128)(2,1)S(1)} %slice.59), channel_id=1, source_target_pairs={{0,7},{1,0},{2,1},{3,2},{4,3},{5,4},{6,5},{7,6},{8,15},{9,8},{10,9... | collective-permute-start | bytes 811016 | tf_op jit(solution)/shard_map/ppermute | solution.py:224
  76.3 8.0 %copy-start.1 = (bf16[1,128,128]{2,1,0:T(8,128)(2,1)S(1)}, bf16[1,128,128]{2,1,0:T(8,128)(2,1)}, u32[]{:S(2)}) copy-start(bf16[1,128,128]{2,1,0:T(8,128)(2,1)} %param.8) | copy-start | bytes 98308

commit v8 on v7

--- a/solution.py
+++ b/solution.py
@@ -29,25 +29,23 @@
 
 
 def collect(source, stage, natural, weights, first_row, first_block, groups):
-    def step(g, _):
-        at = pl.multiple_of(first_row + g * GROUP, GROUP)
-        rows = source[:, pl.ds(at, GROUP), :].astype(F32)
-        stage[...] = rows.reshape(PARTS * GROUP, B)
+    for g in range(groups):
+        slot = g % 2
+        rows = source[:, pl.ds(first_row + g * GROUP, GROUP), :].astype(F32)
+        stage[slot] = rows.reshape(PARTS * GROUP, B)
         for q in range(GROUP // ROWS):
             for i in range(ROWS):
-                natural[q, pl.ds(i, PARTS, stride=ROWS), :] = stage[
-                    pl.ds(q * ROWS + i, PARTS, stride=GROUP), :
+                natural[slot * 4 + q, pl.ds(i, PARTS, stride=ROWS), :] = stage[
+                    slot, pl.ds(q * ROWS + i, PARTS, stride=GROUP), :
                 ]
-            weights[first_block + g * 4 + q] = natural[q].astype(BF16)
-        return 0
-
-    lax.fori_loop(0, groups, step, 0)
+            weights[first_block + g * 4 + q] = natural[slot * 4 + q].astype(BF16)
 
 
 def summed(acc, natural, target):
+    slot = target % 8
     for i in range(ROWS):
-        natural[0, pl.ds(i, PARTS, stride=ROWS), :] = acc[target, pl.ds(i * PARTS, PARTS), :]
-    return natural[0]
+        natural[slot, pl.ds(i, PARTS, stride=ROWS), :] = acc[target, pl.ds(i * PARTS, PARTS), :]
+    return natural[slot]
 
 
 def solve_level(
@@ -148,8 +146,8 @@
 SMEM = pl.BlockSpec(memory_space=pltpu.SMEM)
 HBM = pl.BlockSpec(memory_space=pl.ANY)
 WORK = (
-    pltpu.VMEM((PARTS * GROUP, B), F32),
-    pltpu.VMEM((4, B, B), F32),
+    pltpu.VMEM((2, PARTS * GROUP, B), F32),
+    pltpu.VMEM((8, B, B), F32),
 )
 ACC_SHAPE = (SUB - FIRST + TOP, B, B)
 

time: 107 us -> 107 us (level)
  no operation moved by 1% of the time
where the time goes in v8:
time: 107 us; the launch traced here: 106 us
  starting transfers between devices  37.8 us (35%)
  waiting for transfers between devices  30.6 us (29%)
  blocking collectives  16.8 us (16%)
  Pallas kernels  13.5 us (13%)
  local copies, waits for them, and re-layouts  5.65 us (5%)
  between operations  1.43 us (1%)
    ppermute x25, starting transfers between devices, shift(): return lax.ppermute(x, axis, [(n, (n + k) % size) for n in range(size)])  37.8 us
    ppermute x25, waiting for transfers between devices, shift(): return lax.ppermute(x, axis, [(n, (n + k) % size) for n in range(size)])  30.6 us
    all_to_all x1, blocking collectives, local(): parts = lax.all_to_all(addends, ROW, 0, 0, tiled=True)  14.2 us
    pallas_call x1, Pallas kernels, run_later(): pl.pallas_call(later_levels, out_shape=(jax.ShapeDtypeStruct((SUB, B, B),...  7.37 us
    pallas_call x1, Pallas kernels, run_leaves(): pl.pallas_call(leaf_level, out_shape=(jax.ShapeDtypeStruct((FIRST, B, B),...  4.38 us
    all_gather x1, blocking collectives, gather_row(): pair = lax.all_gather(x, 'core', axis=0)  2.64 us
    dynamic_update_slice x30, local copies, waits for them, and re-layouts, put(): return lax.dynamic_update_slice(buffer, x.reshape(shape), start)  2.35 us
  transfers between devices with their start and end apart: 25, of which 6 were waited for; matrix products, arithmetic and copies ran while one was open for 5% of the time, Pallas kernels for 4%

profile of v8, /device:TPU:1, one launch (start us, length us, event | category | flops | bytes accessed | tf_op | source)
XLA Modules:
  0.0 106.5 jit_solution(867310118110670165)
XLA Ops:
  0.6 1.7 %shard_map.86 = (bf16[480,128]{1,0:T(8,128)(2,1)}, bf16[368,128]{1,0:T(8,128)(2,1)}, bf16[32,128]{1,0:T(8,128)(2,1)}) custom-call(s32[1]{0:T(128)} %bitcast.row.where, bf16[168,128]{1,0:T(8,128)(2,1)} %bitcast.134, bf16[672,128]{1,0:T(8,128)(2,1)} %bitcast.129, bf16[32,128]{1,0:T(8,128)(2,1)} %bitcast.136, bf16[4,128]{1,0:T(4,128)(2,1)} %bitcast.137), custom_call_target="tpu_custom_call" | custom-call | bytes 524288 | tf_op jit(solution)/shard_map/pallas_call | solution.py:160
  2.4 2.5 %collective-permute-start = (bf16[480,128]{1,0:T(8,128)(2,1)}, bf16[480,128]{1,0:T(8,128)(2,1)S(1)}, u32[]{:S(2)}, u32[]{:S(2)}) collective-permute-start(bf16[480,128]{1,0:T(8,128)(2,1)} %get-tuple-element.12), channel_id=1, source_target_pairs={{0,1},{1,2},{2,3},{3,4},{4,5},{5,6},{6,7},{7,0},{8,9},{9,10},{10,1... | collective-permute-start | bytes 368648 | tf_op jit(solution)/shard_map/ppermute | solution.py:222
  4.9 4.0 %collective-permute-start.1 = (bf16[480,128]{1,0:T(8,128)(2,1)}, bf16[480,128]{1,0:T(8,128)(2,1)S(1)}, u32[]{:S(2)}, u32[]{:S(2)}) collective-permute-start(bf16[480,128]{1,0:T(8,128)(2,1)} %get-tuple-element.12), channel_id=1, source_target_pairs={{0,7},{1,0},{2,1},{3,2},{4,3},{5,4},{6,5},{7,6},{8,15},{9,8},{10,9... | collective-permute-start | bytes 368648 | tf_op jit(solution)/shard_map/ppermute | solution.py:222
  9.0 2.6 %all-gather = bf16[64,128]{1,0:T(8,128)(2,1)S(1)} all-gather(bf16[32,128]{1,0:T(8,128)(2,1)} %get-tuple-element.14), channel_id=2, replica_groups=mesh['x'=4,'core'=2,'y'=4,'z'=8] {'core'}, dimensions={0}, use_global_device_ids=true | all-gather | bytes 24576 | tf_op jit(solution)/shard_map/all_gather | solution.py:273
  11.6 1.2 %collective-permute-start.2 = (bf16[2,32,128]{2,1,0:T(8,128)(2,1)S(1)}, bf16[2,32,128]{2,1,0:T(8,128)(2,1)S(1)}, u32[]{:S(2)}, u32[]{:S(2)}) collective-permute-start(bf16[2,32,128]{2,1,0:T(8,128)(2,1)S(1)} %bitcast.130), channel_id=1, source_target_pairs={{0,64},{64,128},{128,192},{192,0},{1,65},{65,129},{129,193},{193,1... | collective-permute-start | bytes 49160 | tf_op jit(solution)/shard_map/ppermute | solution.py:222
  12.8 1.5 %collective-permute-start.3 = (bf16[2,32,128]{2,1,0:T(8,128)(2,1)S(1)}, bf16[2,32,128]{2,1,0:T(8,128)(2,1)S(1)}, u32[]{:S(2)}, u32[]{:S(2)}) collective-permute-start(bf16[2,32,128]{2,1,0:T(8,128)(2,1)S(1)} %bitcast.131), channel_id=1, source_target_pairs={{0,192},{64,0},{128,64},{192,128},{1,193},{65,1},{129,65},{193,129... | collective-permute-start | bytes 49160 | tf_op jit(solution)/shard_map/ppermute | solution.py:222
  14.3 1.5 %collective-permute-start.4 = (bf16[2,32,128]{2,1,0:T(8,128)(2,1)S(1)}, bf16[2,32,128]{2,1,0:T(8,128)(2,1)S(1)}, u32[]{:S(2)}, u32[]{:S(2)}) collective-permute-start(bf16[2,32,128]{2,1,0:T(8,128)(2,1)S(1)} %bitcast.132), channel_id=1, source_target_pairs={{0,128},{64,192},{128,0},{192,64},{1,129},{65,193},{129,1},{193,65... | collective-permute-start | bytes 49160 | tf_op jit(solution)/shard_map/ppermute | solution.py:222
  15.8 0.9 constant_dynamic-update-slice_fusion.8
  16.7 0.1 broadcast_in_dim.55
  16.8 0.9 bitcast_dynamic-update-slice_fusion.25
  18.0 0.8 copy.17
  18.8 0.1 reshape.94.codes
  19.0 0.0 collective-permute-done.2
  19.0 0.0 collective-permute-done.4
  19.2 0.0 collective-permute-done
  19.2 1.4 %collective-permute-start.14 = (bf16[528,128]{1,0:T(8,128)(2,1)S(1)}, bf16[528,128]{1,0:T(8,128)(2,1)S(1)}, u32[]{:S(2)}, u32[]{:S(2)}) collective-permute-start(bf16[528,128]{1,0:T(8,128)(2,1)S(1)} %constant_dynamic-update-slice_fusion), channel_id=1, source_target_pairs={{0,8},{8,16},{16,24},{24,0},{1,9},{9,17},{17,25},{25,1},{2,10},{10... | collective-permute-start | bytes 405512 | tf_op jit(solution)/shard_map/ppermute | solution.py:222
  20.6 1.5 %collective-permute-start.15 = (bf16[528,128]{1,0:T(8,128)(2,1)S(1)}, bf16[528,128]{1,0:T(8,128)(2,1)S(1)}, u32[]{:S(2)}, u32[]{:S(2)}) collective-permute-start(bf16[528,128]{1,0:T(8,128)(2,1)S(1)} %constant_dynamic-update-slice_fusion), channel_id=1, source_target_pairs={{0,24},{8,0},{16,8},{24,16},{1,25},{9,1},{17,9},{25,17},{2,26},{10... | collective-permute-start | bytes 405512 | tf_op jit(solution)/shard_map/ppermute | solution.py:222
  22.1 1.6 %collective-permute-start.16 = (bf16[528,128]{1,0:T(8,128)(2,1)S(1)}, bf16[528,128]{1,0:T(8,128)(2,1)S(1)}, u32[]{:S(2)}, u32[]{:S(2)}) collective-permute-start(bf16[528,128]{1,0:T(8,128)(2,1)S(1)} %constant_dynamic-update-slice_fusion), channel_id=1, source_target_pairs={{0,16},{8,24},{16,0},{24,8},{1,17},{9,25},{17,1},{25,9},{2,18},{10... | collective-permute-start | bytes 405512 | tf_op jit(solution)/shard_map/ppermute | solution.py:222
  23.6 0.0 collective-permute-start.5
  23.7 2.7 %collective-permute-start.6 = (bf16[480,128]{1,0:T(8,128)(2,1)S(1)}, bf16[480,128]{1,0:T(8,128)(2,1)S(1)}, u32[]{:S(2)}, u32[]{:S(2)}) collective-permute-start(bf16[480,128]{1,0:T(8,128)(2,1)S(1)} %collective-permute-done.1), channel_id=1, source_target_pairs={{0,7},{1,0},{2,1},{3,2},{4,3},{5,4},{6,5},{7,6},{8,15},{9,8},{10,9... | collective-permute-start | bytes 368648 | tf_op jit(solution)/shard_map/ppermute | solution.py:222
  26.3 0.1 broadcast_in_dim.60
  26.5 2.1 %collective-permute-done.5 = bf16[480,128]{1,0:T(8,128)(2,1)S(1)} collective-permute-done((bf16[480,128]{1,0:T(8,128)(2,1)S(1)}, bf16[480,128]{1,0:T(8,128)(2,1)S(1)}, u32[]{:S(2)}, u32[]{:S(2)}) %collective-permute-start.5) | collective-permute-done | bytes 122912 | tf_op jit(solution)/shard_map/ppermute | solution.py:222
  28.6 0.0 collective-permute-start.7
  28.6 0.0 collective-permute-done.6
  28.6 3.0 %collective-permute-start.8 = (bf16[480,128]{1,0:T(8,128)(2,1)S(1)}, bf16[480,128]{1,0:T(8,128)(2,1)S(1)}, u32[]{:S(2)}, u32[]{:S(2)}) collective-permute-start(bf16[480,128]{1,0:T(8,128)(2,1)S(1)} %collective-permute-done.6), channel_id=1, source_target_pairs={{0,7},{1,0},{2,1},{3,2},{4,3},{5,4},{6,5},{7,6},{8,15},{9,8},{10,9... | collective-permute-start | bytes 368648 | tf_op jit(solution)/shard_map/ppermute | solution.py:222
  31.7 0.0 collective-permute-done.15
  31.7 0.1 collective-permute-start.17
  31.8 2.7 %collective-permute-start.18 = (bf16[4,528,128]{2,1,0:T(8,128)(2,1)S(1)}, bf16[4,528,128]{2,1,0:T(8,128)(2,1)S(1)}, u32[]{:S(2)}, u32[]{:S(2)}) collective-permute-start(bf16[4,528,128]{2,1,0:T(8,128)(2,1)S(1)} %bitcast_dynamic-update-slice_fusion.14), channel_id=1, source_target_pairs={{0,7},{1,0},{2,1},{3,2},{4,3},{5,4},{6,5},{7,6},{8,15},{9,8},{10,9... | collective-permute-start | bytes 1622024 | tf_op jit(solution)/shard_map/ppermute | solution.py:222
  34.5 0.6 broadcast_in_dim.59
  35.1 0.1 bitcast_dynamic-update-slice_fusion.9
  35.1 0.0 collective-permute-done.7
  35.2 0.3 collective-permute-start.9
  35.5 0.0 collective-permute-done.8
  35.5 12.9 %collective-permute-done.9 = bf16[480,128]{1,0:T(8,128)(2,1)S(1)} collective-permute-done((bf16[480,128]{1,0:T(8,128)(2,1)S(1)}, bf16[480,128]{1,0:T(8,128)(2,1)S(1)}, u32[]{:S(2)}, u32[]{:S(2)}) %collective-permute-start.9) | collective-permute-done | bytes 122912 | tf_op jit(solution)/shard_map/ppermute | solution.py:222
  48.4 0.2 collective-permute-start.10
  48.6 2.6 %collective-permute-start.11 = (bf16[8,480,128]{2,1,0:T(8,128)(2,1)S(1)}, bf16[8,480,128]{2,1,0:T(8,128)(2,1)S(1)}, u32[]{:S(2)}, u32[]{:S(2)}) collective-permute-start(bf16[8,480,128]{2,1,0:T(8,128)(2,1)S(1)} %bitcast_dynamic-update-slice_fusion.18), channel_id=1, source_target_pairs={{0,24},{8,0},{16,8},{24,16},{1,25},{9,1},{17,9},{25,17},{2,26},{10... | collective-permute-start | bytes 2949128 | tf_op jit(solution)/shard_map/ppermute | solution.py:222
  51.2 2.7 %collective-permute-start.20 = (bf16[4,528,128]{2,1,0:T(8,128)(2,1)S(1)}, bf16[4,528,128]{2,1,0:T(8,128)(2,1)S(1)}, u32[]{:S(2)}, u32[]{:S(2)}) collective-permute-start(bf16[4,528,128]{2,1,0:T(8,128)(2,1)S(1)} %collective-permute-done.18), channel_id=1, source_target_pairs={{0,7},{1,0},{2,1},{3,2},{4,3},{5,4},{6,5},{7,6},{8,15},{9,8},{10,9... | collective-permute-start | bytes 1622024 | tf_op jit(solution)/shard_map/ppermute | solution.py:222
  53.9 0.6 broadcast_in_dim.54
  54.4 0.1 bitcast_dynamic-update-slice_fusion.2
  54.6 0.1 bitcast_dynamic-update-slice_fusion.8
  54.7 0.1 bitcast_dynamic-update-slice_fusion.7
  54.8 7.6 %collective-permute-done.19 = bf16[4,528,128]{2,1,0:T(8,128)(2,1)S(1)} collective-permute-done((bf16[4,528,128]{2,1,0:T(8,128)(2,1)S(1)}, bf16[4,528,128]{2,1,0:T(8,128)(2,1)S(1)}, u32[]{:S(2)}, u32[]{:S(2)}) %collective-permute-start.19) | collective-permute-done | bytes 540704 | tf_op jit(solution)/shard_map/ppermute | solution.py:222
  62.4 2.7 %collective-permute-start.22 = (bf16[4,528,128]{2,1,0:T(8,128)(2,1)S(1)}, bf16[4,528,128]{2,1,0:T(8,128)(2,1)S(1)}, u32[]{:S(2)}, u32[]{:S(2)}) collective-permute-start(bf16[4,528,128]{2,1,0:T(8,128)(2,1)S(1)} %collective-permute-done.20), channel_id=1, source_target_pairs={{0,7},{1,0},{2,1},{3,2},{4,3},{5,4},{6,5},{7,6},{8,15},{9,8},{10,9... | collective-permute-start | bytes 1622024 | tf_op jit(solution)/shard_map/ppermute | solution.py:222
  65.0 0.1 bitcast_dynamic-update-slice_fusion.6
  65.1 0.1 bitcast_dynamic-update-slice_fusion.5
  65.2 4.5 %collective-permute-done.10 = bf16[8,480,128]{2,1,0:T(8,128)(2,1)S(1)} collective-permute-done((bf16[8,480,128]{2,1,0:T(8,128)(2,1)S(1)}, bf16[8,480,128]{2,1,0:T(8,128)(2,1)S(1)}, u32[]{:S(2)}, u32[]{:S(2)}) %collective-permute-start.10) | collective-permute-done | bytes 983072 | tf_op jit(solution)/shard_map/ppermute | solution.py:222
  69.7 0.1 collective-permute-start.12
  69.9 0.0 copy-start
  69.9 2.7 %collective-permute-start.13 = (bf16[4,480,128]{2,1,0:T(8,128)(2,1)S(1)}, bf16[4,480,128]{2,1,0:T(8,128)(2,1)S(1)}, u32[]{:S(2)}, u32[]{:S(2)}) collective-permute-start(bf16[4,480,128]{2,1,0:T(8,128)(2,1)S(1)} %slice.57), channel_id=1, source_target_pairs={{0,24},{8,0},{16,8},{24,16},{1,25},{9,1},{17,9},{25,17},{2,26},{10... | collective-permute-start | bytes 1474568 | tf_op jit(solution)/shard_map/ppermute | solution.py:222
  72.6 0.1 bitcast_dynamic-update-slice_fusion.1
  72.8 0.1 bitcast_dynamic-update-slice_fusion
  72.9 0.2 collective-permute-done.21
  73.1 0.1 collective-permute-start.23
  73.2 2.9 %collective-permute-start.24 = (bf16[2,528,128]{2,1,0:T(8,128)(2,1)S(1)}, bf16[2,528,128]{2,1,0:T(8,128)(2,1)S(1)}, u32[]{:S(2)}, u32[]{:S(2)}) collective-permute-start(bf16[2,528,128]{2,1,0:T(8,128)(2,1)S(1)} %slice.59), channel_id=1, source_target_pairs={{0,7},{1,0},{2,1},{3,2},{4,3},{5,4},{6,5},{7,6},{8,15},{9,8},{10,9... | collective-permute-start | bytes 811016 | tf_op jit(solution)/shard_map/ppermute | solution.py:222
  76.2 0.1 bitcast_dynamic-update-slice_fusion.4
  76.3 0.1 bitcast_dynamic-update-slice_fusion.3
  76.3 0.0 copy-start.1
  76.4 3.2 %collective-permute-done.12 = bf16[4,480,128]{2,1,0:T(8,128)(2,1)S(1)} collective-permute-done((bf16[4,480,128]{2,1,0:T(8,128)(2,1)S(1)}, bf16[4,480,128]{2,1,0:T(8,128)(2,1)S(1)}, u32[]{:S(2)}, u32[]{:S(2)}) %collective-permute-start.12) | collective-permute-done | bytes 491552 | tf_op jit(solution)/shard_map/ppermute | solution.py:222
  79.6 0.1 bitcast_dynamic-update-slice_fusion.11
  79.6 0.1 bitcast_dynamic-update-slice_fusion.10
  79.7 4.4 %shard_map.87 = (bf16[24,128,128]{2,1,0:T(8,128)(2,1)S(1)}, f32[26,128,128]{2,1,0:T(8,128)S(1)}) custom-call(s32[168]{0:T(256)S(1)} %reshape.94.codes, bf16[42,128,128]{2,1,0:T(8,128)(2,1)S(1)} %copy-done, bf16[32,480,128]{2,1,0:T(8,128)(2,1)S(1)} %bitcast.119), custom_call_target="tpu_custom_call" | custom-call | flops 503316480 | bytes 8388608 | tf_op jit(solution)/shard_map/pallas_call | solution.py:179
  84.3 7.4 %shard_map.88 = (bf16[42,128,128]{2,1,0:T(8,128)(2,1)}, bf16[8,128,128]{2,1,0:T(8,128)(2,1)S(1)}) custom-call(s32[168]{0:T(256)S(1)} %reshape.94.codes, s32[1]{0:T(128)} %bitcast.row.where, bf16[42,128,128]{2,1,0:T(8,128)(2,1)S(1)} %copy-done, bf16[128,128]{1,0:T(8,128)(2,1)S(1)} %bitcast.120, f32[26,128,128]{2,1,0:T(8,128)S(1)} %get-tuple-element.17.acc_in, ...), custom_call_target="tpu_custom_call" | custom-call | flops 528482304 | bytes 8388608 | tf_op jit(solution)/shard_map/pallas_call | solution.py:198
  91.6 14.2 %all_to_all.5 = bf16[8,128,128]{2,1,0:T(8,128)(2,1)S(1)} all-to-all(bf16[8,128,128]{2,1,0:T(8,128)(2,1)S(1)} %get-tuple-element.21), channel_id=1, replica_groups=mesh['x'=4,'core'=2,'y'=4,'z'=8] {'x','core'}, dimensions={0} | all-to-all | bytes 524288 | tf_op jit(solution)/shard_map/all_to_all | solution.py:296
  105.8 0.7 reduce_sum.12
  (46 shorter events, 0.6 us)
Async XLA Ops:
  2.4 16.8 %collective-permute-start = (bf16[480,128]{1,0:T(8,128)(2,1)}, bf16[480,128]{1,0:T(8,128)(2,1)S(1)}, u32[]{:S(2)}, u32[]{:S(2)}) collective-permute-start(bf16[480,128]{1,0:T(8,128)(2,1)} %get-tuple-element.12), channel_id=1, source_target_pairs={{0,1},{1,2},{2,3},{3,4},{4,5},{5,6},{6,7},{7,0},{8,9},{9,10},{10,1... | collective-permute-start | bytes 368648 | tf_op jit(solution)/shard_map/ppermute | solution.py:222
  4.9 14.3 %collective-permute-start.1 = (bf16[480,128]{1,0:T(8,128)(2,1)}, bf16[480,128]{1,0:T(8,128)(2,1)S(1)}, u32[]{:S(2)}, u32[]{:S(2)}) collective-permute-start(bf16[480,128]{1,0:T(8,128)(2,1)} %get-tuple-element.12), channel_id=1, source_target_pairs={{0,7},{1,0},{2,1},{3,2},{4,3},{5,4},{6,5},{7,6},{8,15},{9,8},{10,9... | collective-permute-start | bytes 368648 | tf_op jit(solution)/shard_map/ppermute | solution.py:222
  11.6 7.4 %collective-permute-start.2 = (bf16[2,32,128]{2,1,0:T(8,128)(2,1)S(1)}, bf16[2,32,128]{2,1,0:T(8,128)(2,1)S(1)}, u32[]{:S(2)}, u32[]{:S(2)}) collective-permute-start(bf16[2,32,128]{2,1,0:T(8,128)(2,1)S(1)} %bitcast.130), channel_id=1, source_target_pairs={{0,64},{64,128},{128,192},{192,0},{1,65},{65,129},{129,193},{193,1... | collective-permute-start | bytes 49160 | tf_op jit(solution)/shard_map/ppermute | solution.py:222
  12.8 6.2 %collective-permute-start.3 = (bf16[2,32,128]{2,1,0:T(8,128)(2,1)S(1)}, bf16[2,32,128]{2,1,0:T(8,128)(2,1)S(1)}, u32[]{:S(2)}, u32[]{:S(2)}) collective-permute-start(bf16[2,32,128]{2,1,0:T(8,128)(2,1)S(1)} %bitcast.131), channel_id=1, source_target_pairs={{0,192},{64,0},{128,64},{192,128},{1,193},{65,1},{129,65},{193,129... | collective-permute-start | bytes 49160 | tf_op jit(solution)/shard_map/ppermute | solution.py:222
  14.3 4.8 %collective-permute-start.4 = (bf16[2,32,128]{2,1,0:T(8,128)(2,1)S(1)}, bf16[2,32,128]{2,1,0:T(8,128)(2,1)S(1)}, u32[]{:S(2)}, u32[]{:S(2)}) collective-permute-start(bf16[2,32,128]{2,1,0:T(8,128)(2,1)S(1)} %bitcast.132), channel_id=1, source_target_pairs={{0,128},{64,192},{128,0},{192,64},{1,129},{65,193},{129,1},{193,65... | collective-permute-start | bytes 49160 | tf_op jit(solution)/shard_map/ppermute | solution.py:222
  19.2 12.4 %collective-permute-start.14 = (bf16[528,128]{1,0:T(8,128)(2,1)S(1)}, bf16[528,128]{1,0:T(8,128)(2,1)S(1)}, u32[]{:S(2)}, u32[]{:S(2)}) collective-permute-start(bf16[528,128]{1,0:T(8,128)(2,1)S(1)} %constant_dynamic-update-slice_fusion), channel_id=1, source_target_pairs={{0,8},{8,16},{16,24},{24,0},{1,9},{9,17},{17,25},{25,1},{2,10},{10... | collective-permute-start | bytes 405512 | tf_op jit(solution)/shard_map/ppermute | solution.py:222
  20.6 11.1 %collective-permute-start.15 = (bf16[528,128]{1,0:T(8,128)(2,1)S(1)}, bf16[528,128]{1,0:T(8,128)(2,1)S(1)}, u32[]{:S(2)}, u32[]{:S(2)}) collective-permute-start(bf16[528,128]{1,0:T(8,128)(2,1)S(1)} %constant_dynamic-update-slice_fusion), channel_id=1, source_target_pairs={{0,24},{8,0},{16,8},{24,16},{1,25},{9,1},{17,9},{25,17},{2,26},{10... | collective-permute-start | bytes 405512 | tf_op jit(solution)/shard_map/ppermute | solution.py:222
  22.1 9.6 %collective-permute-start.16 = (bf16[528,128]{1,0:T(8,128)(2,1)S(1)}, bf16[528,128]{1,0:T(8,128)(2,1)S(1)}, u32[]{:S(2)}, u32[]{:S(2)}) collective-permute-start(bf16[528,128]{1,0:T(8,128)(2,1)S(1)} %constant_dynamic-update-slice_fusion), channel_id=1, source_target_pairs={{0,16},{8,24},{16,0},{24,8},{1,17},{9,25},{17,1},{25,9},{2,18},{10... | collective-permute-start | bytes 405512 | tf_op jit(solution)/shard_map/ppermute | solution.py:222
  23.6 4.9 %collective-permute-start.5 = (bf16[480,128]{1,0:T(8,128)(2,1)S(1)}, bf16[480,128]{1,0:T(8,128)(2,1)S(1)}, u32[]{:S(2)}, u32[]{:S(2)}) collective-permute-start(bf16[480,128]{1,0:T(8,128)(2,1)S(1)} %collective-permute-done), channel_id=1, source_target_pairs={{0,1},{1,2},{2,3},{3,4},{4,5},{5,6},{6,7},{7,0},{8,9},{9,10},{10,1... | collective-permute-start | bytes 368648 | tf_op jit(solution)/shard_map/ppermute | solution.py:222
  23.7 4.9 %collective-permute-start.6 = (bf16[480,128]{1,0:T(8,128)(2,1)S(1)}, bf16[480,128]{1,0:T(8,128)(2,1)S(1)}, u32[]{:S(2)}, u32[]{:S(2)}) collective-permute-start(bf16[480,128]{1,0:T(8,128)(2,1)S(1)} %collective-permute-done.1), channel_id=1, source_target_pairs={{0,7},{1,0},{2,1},{3,2},{4,3},{5,4},{6,5},{7,6},{8,15},{9,8},{10,9... | collective-permute-start | bytes 368648 | tf_op jit(solution)/shard_map/ppermute | solution.py:222
  28.6 6.6 %collective-permute-start.7 = (bf16[480,128]{1,0:T(8,128)(2,1)S(1)}, bf16[480,128]{1,0:T(8,128)(2,1)S(1)}, u32[]{:S(2)}, u32[]{:S(2)}) collective-permute-start(bf16[480,128]{1,0:T(8,128)(2,1)S(1)} %collective-permute-done.5), channel_id=1, source_target_pairs={{0,1},{1,2},{2,3},{3,4},{4,5},{5,6},{6,7},{7,0},{8,9},{9,10},{10,1... | collective-permute-start | bytes 368648 | tf_op jit(solution)/shard_map/ppermute | solution.py:222
  28.6 6.9 %collective-permute-start.8 = (bf16[480,128]{1,0:T(8,128)(2,1)S(1)}, bf16[480,128]{1,0:T(8,128)(2,1)S(1)}, u32[]{:S(2)}, u32[]{:S(2)}) collective-permute-start(bf16[480,128]{1,0:T(8,128)(2,1)S(1)} %collective-permute-done.6), channel_id=1, source_target_pairs={{0,7},{1,0},{2,1},{3,2},{4,3},{5,4},{6,5},{7,6},{8,15},{9,8},{10,9... | collective-permute-start | bytes 368648 | tf_op jit(solution)/shard_map/ppermute | solution.py:222
  31.7 19.4 %collective-permute-start.17 = (bf16[4,528,128]{2,1,0:T(8,128)(2,1)S(1)}, bf16[4,528,128]{2,1,0:T(8,128)(2,1)S(1)}, u32[]{:S(2)}, u32[]{:S(2)}) collective-permute-start(bf16[4,528,128]{2,1,0:T(8,128)(2,1)S(1)} %bitcast_dynamic-update-slice_fusion.14), channel_id=1, source_target_pairs={{0,1},{1,2},{2,3},{3,4},{4,5},{5,6},{6,7},{7,0},{8,9},{9,10},{10,1... | collective-permute-start | bytes 1622024 | tf_op jit(solution)/shard_map/ppermute | solution.py:222
  31.8 19.4 %collective-permute-start.18 = (bf16[4,528,128]{2,1,0:T(8,128)(2,1)S(1)}, bf16[4,528,128]{2,1,0:T(8,128)(2,1)S(1)}, u32[]{:S(2)}, u32[]{:S(2)}) collective-permute-start(bf16[4,528,128]{2,1,0:T(8,128)(2,1)S(1)} %bitcast_dynamic-update-slice_fusion.14), channel_id=1, source_target_pairs={{0,7},{1,0},{2,1},{3,2},{4,3},{5,4},{6,5},{7,6},{8,15},{9,8},{10,9... | collective-permute-start | bytes 1622024 | tf_op jit(solution)/shard_map/ppermute | solution.py:222
  35.2 13.3 %collective-permute-start.9 = (bf16[480,128]{1,0:T(8,128)(2,1)S(1)}, bf16[480,128]{1,0:T(8,128)(2,1)S(1)}, u32[]{:S(2)}, u32[]{:S(2)}) collective-permute-start(bf16[480,128]{1,0:T(8,128)(2,1)S(1)} %collective-permute-done.7), channel_id=1, source_target_pairs={{0,1},{1,2},{2,3},{3,4},{4,5},{5,6},{6,7},{7,0},{8,9},{9,10},{10,1... | collective-permute-start | bytes 368648 | tf_op jit(solution)/shard_map/ppermute | solution.py:222
  48.4 21.3 %collective-permute-start.10 = (bf16[8,480,128]{2,1,0:T(8,128)(2,1)S(1)}, bf16[8,480,128]{2,1,0:T(8,128)(2,1)S(1)}, u32[]{:S(2)}, u32[]{:S(2)}) collective-permute-start(bf16[8,480,128]{2,1,0:T(8,128)(2,1)S(1)} %bitcast_dynamic-update-slice_fusion.18), channel_id=1, source_target_pairs={{0,8},{8,16},{16,24},{24,0},{1,9},{9,17},{17,25},{25,1},{2,10},{10... | collective-permute-start | bytes 2949128 | tf_op jit(solution)/shard_map/ppermute | solution.py:222
  48.6 21.2 %collective-permute-start.11 = (bf16[8,480,128]{2,1,0:T(8,128)(2,1)S(1)}, bf16[8,480,128]{2,1,0:T(8,128)(2,1)S(1)}, u32[]{:S(2)}, u32[]{:S(2)}) collective-permute-start(bf16[8,480,128]{2,1,0:T(8,128)(2,1)S(1)} %bitcast_dynamic-update-slice_fusion.18), channel_id=1, source_target_pairs={{0,24},{8,0},{16,8},{24,16},{1,25},{9,1},{17,9},{25,17},{2,26},{10... | collective-permute-start | bytes 2949128 | tf_op jit(solution)/shard_map/ppermute | solution.py:222
  51.2 11.2 %collective-permute-start.19 = (bf16[4,528,128]{2,1,0:T(8,128)(2,1)S(1)}, bf16[4,528,128]{2,1,0:T(8,128)(2,1)S(1)}, u32[]{:S(2)}, u32[]{:S(2)}) collective-permute-start(bf16[4,528,128]{2,1,0:T(8,128)(2,1)S(1)} %collective-permute-done.17), channel_id=1, source_target_pairs={{0,1},{1,2},{2,3},{3,4},{4,5},{5,6},{6,7},{7,0},{8,9},{9,10},{10,1... | collective-permute-start | bytes 1622024 | tf_op jit(solution)/shard_map/ppermute | solution.py:222
  51.2 11.2 %collective-permute-start.20 = (bf16[4,528,128]{2,1,0:T(8,128)(2,1)S(1)}, bf16[4,528,128]{2,1,0:T(8,128)(2,1)S(1)}, u32[]{:S(2)}, u32[]{:S(2)}) collective-permute-start(bf16[4,528,128]{2,1,0:T(8,128)(2,1)S(1)} %collective-permute-done.18), channel_id=1, source_target_pairs={{0,7},{1,0},{2,1},{3,2},{4,3},{5,4},{6,5},{7,6},{8,15},{9,8},{10,9... | collective-permute-start | bytes 1622024 | tf_op jit(solution)/shard_map/ppermute | solution.py:222
  62.4 10.7 %collective-permute-start.21 = (bf16[4,528,128]{2,1,0:T(8,128)(2,1)S(1)}, bf16[4,528,128]{2,1,0:T(8,128)(2,1)S(1)}, u32[]{:S(2)}, u32[]{:S(2)}) collective-permute-start(bf16[4,528,128]{2,1,0:T(8,128)(2,1)S(1)} %collective-permute-done.19), channel_id=1, source_target_pairs={{0,1},{1,2},{2,3},{3,4},{4,5},{5,6},{6,7},{7,0},{8,9},{9,10},{10,1... | collective-permute-start | bytes 1622024 | tf_op jit(solution)/shard_map/ppermute | solution.py:222
  62.4 10.8 %collective-permute-start.22 = (bf16[4,528,128]{2,1,0:T(8,128)(2,1)S(1)}, bf16[4,528,128]{2,1,0:T(8,128)(2,1)S(1)}, u32[]{:S(2)}, u32[]{:S(2)}) collective-permute-start(bf16[4,528,128]{2,1,0:T(8,128)(2,1)S(1)} %collective-permute-done.20), channel_id=1, source_target_pairs={{0,7},{1,0},{2,1},{3,2},{4,3},{5,4},{6,5},{7,6},{8,15},{9,8},{10,9... | collective-permute-start | bytes 1622024 | tf_op jit(solution)/shard_map/ppermute | solution.py:222
  69.7 9.8 %collective-permute-start.12 = (bf16[4,480,128]{2,1,0:T(8,128)(2,1)S(1)}, bf16[4,480,128]{2,1,0:T(8,128)(2,1)S(1)}, u32[]{:S(2)}, u32[]{:S(2)}) collective-permute-start(bf16[4,480,128]{2,1,0:T(8,128)(2,1)S(1)} %slice.56), channel_id=1, source_target_pairs={{0,8},{8,16},{16,24},{24,0},{1,9},{9,17},{17,25},{25,1},{2,10},{10... | collective-permute-start | bytes 1474568 | tf_op jit(solution)/shard_map/ppermute | solution.py:222
  69.9 9.8 %copy-start = (bf16[42,128,128]{2,1,0:T(8,128)(2,1)S(1)}, bf16[42,128,128]{2,1,0:T(8,128)(2,1)}, u32[]{:S(2)}) copy-start(bf16[42,128,128]{2,1,0:T(8,128)(2,1)} %rhs.3) | copy-start | bytes 4128772
  69.9 9.7 %collective-permute-start.13 = (bf16[4,480,128]{2,1,0:T(8,128)(2,1)S(1)}, bf16[4,480,128]{2,1,0:T(8,128)(2,1)S(1)}, u32[]{:S(2)}, u32[]{:S(2)}) collective-permute-start(bf16[4,480,128]{2,1,0:T(8,128)(2,1)S(1)} %slice.57), channel_id=1, source_target_pairs={{0,24},{8,0},{16,8},{24,16},{1,25},{9,1},{17,9},{25,17},{2,26},{10... | collective-permute-start | bytes 1474568 | tf_op jit(solution)/shard_map/ppermute | solution.py:222
  73.1 11.0 %collective-permute-start.23 = (bf16[2,528,128]{2,1,0:T(8,128)(2,1)S(1)}, bf16[2,528,128]{2,1,0:T(8,128)(2,1)S(1)}, u32[]{:S(2)}, u32[]{:S(2)}) collective-permute-start(bf16[2,528,128]{2,1,0:T(8,128)(2,1)S(1)} %slice.58), channel_id=1, source_target_pairs={{0,1},{1,2},{2,3},{3,4},{4,5},{5,6},{6,7},{7,0},{8,9},{9,10},{10,1... | collective-permute-start | bytes 811016 | tf_op jit(solution)/shard_map/ppermute | solution.py:222
  73.2 11.0 %collective-permute-start.24 = (bf16[2,528,128]{2,1,0:T(8,128)(2,1)S(1)}, bf16[2,528,128]{2,1,0:T(8,128)(2,1)S(1)}, u32[]{:S(2)}, u32[]{:S(2)}) collective-permute-start(bf16[2,528,128]{2,1,0:T(8,128)(2,1)S(1)} %slice.59), channel_id=1, source_target_pairs={{0,7},{1,0},{2,1},{3,2},{4,3},{5,4},{6,5},{7,6},{8,15},{9,8},{10,9... | collective-permute-start | bytes 811016 | tf_op jit(solution)/shard_map/ppermute | solution.py:222
  76.3 7.9 %copy-start.1 = (bf16[1,128,128]{2,1,0:T(8,128)(2,1)S(1)}, bf16[1,128,128]{2,1,0:T(8,128)(2,1)}, u32[]{:S(2)}) copy-start(bf16[1,128,128]{2,1,0:T(8,128)(2,1)} %param.8) | copy-start | bytes 98308
